TPU v7x, 128 devices: a whole 4x4x4 slice. The times are simulated.
128 devices in a mesh: ctx: 8 (over x, z_lo), exp: 16 (over y, z_hi, core).
Axes of the slice: x: 4, y: 4, z: 4 (z_hi: 2, z_lo: 2; z = z_hi * 2 + z_lo), core: 2. Of those that a mesh axis runs over, the one named last changes fastest.
Arguments:
- residual: bfloat16 [16384, 2048], P(('ctx', 'exp')), may hold values from -6 to 6
- queries: bfloat16 [16384, 4096], P('ctx', 'exp'), may hold values from -6.5 to 6.5
- key_rows: bfloat16 [16384, 512], P('ctx'), may hold values from -6.5 to 6.5
- value_rows: bfloat16 [16384, 512], P('ctx'), may hold values from -6 to 6
- segment_ids: int32 [16384], P('ctx'), may hold values from 0 to 31, never falling along the last dimension, each value on 1 to 8704 neighbouring positions
- out_weight: bfloat16 [4096, 2048], P('exp'), may hold values from -0.09375 to 0.09375
- norm_gain: float32 [2048], replicated, may hold values from 0.5 to 1.5
- expert_ids: int32 [16384, 8], P(('ctx', 'exp')), may hold values from 0 to 127, all different within a row; in each aligned block of 128 rows (0 to 127, 128 to 255, ...) at most 16 rows name the same one
- route_weight: float32 [16384, 8], P(('ctx', 'exp')), may hold values from 0.02 to 0.3
- gate_weight: bfloat16 [128, 2048, 768], P(('ctx', 'exp')), may hold values from -0.125 to 0.125
- up_weight: bfloat16 [128, 2048, 768], P(('ctx', 'exp')), may hold values from -0.125 to 0.125
- down_weight: bfloat16 [128, 768, 2048], P(('ctx', 'exp')), may hold values from -0.21875 to 0.21875
Outputs:
- layer_out: bfloat16 [16384, 2048], P(('ctx', 'exp'))
Inputs may be any that keep to these rules, and one draw needn't show every extreme that they name: `expert_ids`: within the rows of one device (128 aligned positions), no expert is named by more than 16 rows; some expert is named by exactly 16. `segment_ids`: never falling along positions; each segment covers at most 8704 positions, and some segment exactly 8704.
All inputs are finite; a program needn't handle non-finite values.
Results may differ from a plain program's by a relative error of at most 0.013.
Values may be sent and summed in bfloat16 or wider, within the bound.
No kernel may reach another device: no remote copies, remote signals or barrier semaphores. Data moves between devices by JAX's collectives and lax.ppermute only.
A program may use at most 128 MiB of HBM per device.

v0:
```python
import math

import jax
import jax.numpy as jnp
from jax import lax
from jax.sharding import PartitionSpec as P

HEADS = 32
KV_HEADS = 4
HEAD_DIM = 128
TOP = 8


def attend_keys(
    running, query_block, query_segs, query_anchor, key_piece, value_piece, key_segs, query_tile
):
    local_heads = query_block.shape[1] // HEAD_DIM
    query_count = query_block.shape[0] // query_tile
    key_count = key_piece.shape[0] // query_tile
    score_scale = 1.0 / math.sqrt(HEAD_DIM)
    tile_range = jnp.arange(query_tile, dtype=jnp.int32)

    def tile_step(tile_index, tile_state):
        query_begin = tile_index // key_count * query_tile
        key_begin = tile_index % key_count * query_tile
        query_part = lax.dynamic_slice_in_dim(query_block, query_begin, query_tile, 0).reshape(
            query_tile, local_heads, HEAD_DIM
        )
        part_segs = lax.dynamic_slice_in_dim(query_segs, query_begin, query_tile, 0)
        key_part = lax.dynamic_slice_in_dim(key_piece, key_begin, query_tile, 0)
        value_part = lax.dynamic_slice_in_dim(value_piece, key_begin, query_tile, 0)
        near_segs = lax.dynamic_slice_in_dim(key_segs, key_begin, query_tile, 0)
        query_pos = query_anchor + query_begin + tile_range
        key_pos = key_begin + tile_range
        reachable = (
            (key_pos[0] <= query_pos[-1])
            & (near_segs[-1] >= part_segs[0])
            & (near_segs[0] <= part_segs[-1])
        )

        def update(current):
            row_max, totals, accumulated = current
            old_max = lax.dynamic_slice_in_dim(row_max, query_begin, query_tile, 1)
            old_total = lax.dynamic_slice_in_dim(totals, query_begin, query_tile, 1)
            old_accum = lax.dynamic_slice_in_dim(accumulated, query_begin, query_tile, 0)
            scores = (
                jnp.einsum("qhd,kd->hqk", query_part, key_part, preferred_element_type=jnp.float32)
                * score_scale
            )
            visible = (part_segs[:, None] == near_segs[None, :]) & (
                key_pos[None, :] <= query_pos[:, None]
            )
            scores = jnp.where(visible[None], scores, -jnp.inf)
            new_max = jnp.maximum(old_max, jnp.max(scores, axis=-1))
            rescale = jnp.exp(old_max - new_max)
            unnormed = jnp.exp(scores - new_max[..., None])
            new_total = rescale * old_total + jnp.sum(unnormed, axis=-1)
            weights = unnormed.astype(jnp.bfloat16)
            gained = jnp.einsum(
                "hqk,kd->qhd", weights, value_part, preferred_element_type=jnp.float32
            )
            new_accum = old_accum * jnp.transpose(rescale)[:, :, None] + gained
            row_max = lax.dynamic_update_slice_in_dim(row_max, new_max, query_begin, 1)
            totals = lax.dynamic_update_slice_in_dim(totals, new_total, query_begin, 1)
            accumulated = lax.dynamic_update_slice_in_dim(accumulated, new_accum, query_begin, 0)
            return (row_max, totals, accumulated)

        def keep_state(current):
            return current

        return lax.cond(reachable, update, keep_state, tile_state)

    return lax.fori_loop(0, query_count * key_count, tile_step, running)


def expert_rows(arrived, gate_weight, up_weight, down_weight):
    in_shape = arrived.shape
    flat_rows = arrived.reshape(-1, in_shape[-1])
    gate_proj = jnp.dot(flat_rows, gate_weight[0], preferred_element_type=jnp.float32)
    up_proj = jnp.dot(flat_rows, up_weight[0], preferred_element_type=jnp.float32)
    hidden = (jax.nn.silu(gate_proj) * up_proj).astype(jnp.bfloat16)
    produced = jnp.dot(hidden, down_weight[0], preferred_element_type=jnp.float32).astype(
        jnp.bfloat16
    )
    return produced.reshape(in_shape)


def shards(
    residual,
    queries,
    key_rows,
    value_rows,
    segment_ids,
    out_weight,
    norm_gain,
    expert_ids,
    route_weight,
    gate_weight,
    up_weight,
    down_weight,
):
    ctx_rows = queries.shape[0]
    local_cols = queries.shape[1]
    local_heads = local_cols // HEAD_DIM
    group_size = HEADS // KV_HEADS
    exp_index = lax.axis_index("exp")
    ctx_index = lax.axis_index("ctx")
    ctx_count = lax.axis_size("ctx")
    exp_count = lax.axis_size("exp")
    kv_index = exp_index * local_heads // group_size
    my_keys = lax.dynamic_slice_in_dim(key_rows, kv_index * HEAD_DIM, HEAD_DIM, 1)
    my_values = lax.dynamic_slice_in_dim(value_rows, kv_index * HEAD_DIM, HEAD_DIM, 1)
    query_tile = min(512, ctx_rows)
    initial = (
        jnp.full((local_heads, ctx_rows), -1e30, jnp.float32),
        jnp.zeros((local_heads, ctx_rows), jnp.float32),
        jnp.zeros((ctx_rows, local_heads, HEAD_DIM), jnp.float32),
    )
    row_max, totals, accumulated = attend_keys(
        initial,
        queries,
        segment_ids,
        ctx_index * ctx_rows,
        lax.all_gather(my_keys, "ctx", axis=0, tiled=True),
        lax.all_gather(my_values, "ctx", axis=0, tiled=True),
        lax.all_gather(segment_ids, "ctx", axis=0, tiled=True),
        query_tile,
    )
    attended = (
        (accumulated / jnp.transpose(totals)[:, :, None])
        .reshape(ctx_rows, local_cols)
        .astype(jnp.bfloat16)
    )
    own_rows = residual.shape[0]
    attention_sum = lax.psum_scatter(
        jnp.dot(attended, out_weight, preferred_element_type=jnp.float32).astype(jnp.bfloat16),
        "exp",
        scatter_dimension=0,
        tiled=True,
    ).astype(jnp.float32)
    mixed_rows = residual.astype(jnp.float32) + attention_sum
    mean_square = jnp.mean(mixed_rows * mixed_rows, axis=-1, keepdims=True)
    normed = (mixed_rows * lax.rsqrt(mean_square + 1e-06) * norm_gain).astype(jnp.bfloat16)
    model_width = normed.shape[1]
    expert_count = ctx_count * exp_count
    capacity = 2 * own_rows * TOP // expert_count
    flat_ids = expert_ids.reshape(-1)
    onehot = (flat_ids[:, None] == jnp.arange(expert_count, dtype=jnp.int32)[None, :]).astype(
        jnp.int32
    )
    slot_index = jnp.sum(jnp.cumsum(onehot, axis=0) * onehot, axis=1) - 1
    repeated = jnp.repeat(normed, TOP, axis=0)
    outgoing = (
        jnp.zeros((expert_count, capacity, model_width), jnp.bfloat16)
        .at[flat_ids, slot_index]
        .set(repeated)
    )
    returned = lax.all_to_all(
        expert_rows(
            lax.all_to_all(outgoing, ("ctx", "exp"), split_axis=0, concat_axis=0, tiled=True),
            gate_weight,
            up_weight,
            down_weight,
        ),
        ("ctx", "exp"),
        split_axis=0,
        concat_axis=0,
        tiled=True,
    )
    fetched = returned[flat_ids, slot_index].astype(jnp.float32) * route_weight.reshape(-1)[:, None]
    routed = jnp.sum(fetched.reshape(own_rows, TOP, model_width), axis=1)
    return (mixed_rows + routed).astype(jnp.bfloat16)


def solution(mesh):
    return jax.shard_map(
        shards,
        mesh=mesh,
        in_specs=(
            P(("ctx", "exp"), None),
            P("ctx", "exp"),
            P("ctx", None),
            P("ctx", None),
            P("ctx"),
            P("exp", None),
            P(),
            P(("ctx", "exp"), None),
            P(("ctx", "exp"), None),
            P(("ctx", "exp"), None, None),
            P(("ctx", "exp"), None, None),
            P(("ctx", "exp"), None, None),
        ),
        out_specs=P(("ctx", "exp"), None),
        check_vma=False,
    )
```

profile of v0, /device:TPU:8, one launch (start us, length us, event | category | flops | bytes accessed | tf_op | source)
XLA Modules:
  0.0 2090.1 jit_solution(16325173353470231597)
XLA Ops:
  13.0 32.3 %all_gather.9 = s32[16384]{0:T(1024)S(1)} all-gather(s32[2048]{0:T(1024)S(1)} %copy-done.7), channel_id=1, replica_groups=mesh['ctx'=8,'exp'=16] {'ctx'}, dimensions={0}, use_global_device_ids=true | all-gather | bytes 73728 | tf_op jit(solution)/shard_map/all_gather | solution.py:126
  45.3 56.8 %all-gather.3.cloned.1.call-done = bf16[16384,128]{1,0:T(8,128)(2,1)} async-done(((bf16[2048,128]{1,0:T(8,128)(2,1)}), bf16[16384,128]{1,0:T(8,128)(2,1)}) %all-gather.3.cloned.1.call-update) | async-done | bytes 4194320 | tf_op jit(solution)/shard_map/all_gather | solution.py:124
  102.1 93.1 %all-gather.5.cloned.1.call-done = bf16[16384,128]{1,0:T(8,128)(2,1)} async-done(((bf16[2048,128]{1,0:T(8,128)(2,1)}), bf16[16384,128]{1,0:T(8,128)(2,1)}) %all-gather.5.cloned.1.call-update) | async-done | bytes 4194320 | tf_op jit(solution)/shard_map/all_gather | solution.py:125
  196.7 855.3 %while.21 = (s32[]{:T(128)}, f32[2,2048]{1,0:T(2,128)S(1)}, f32[2,2048]{1,0:T(2,128)S(1)}, f32[2048,2,128]{2,0,1:T(8,128)}, s32[]{:T(128)}, /*index=5*/s32[16384...) while((s32[]{:T(128)}, f32[2,2048]{1,0:T(2,128)S(1)}, ...), condition=%wide.region_5.6_spmd.clone.clone, body=%wide.region_0.5_spmd.clone.clone.sunk | while | flops 273158176 | bytes 18446056 | solution.py:73
  202.4 12.8 conditional.4
  397.8 12.8 conditional.4
  416.3 12.8 conditional.4
  605.9 12.8 conditional.4
  624.4 12.8 conditional.4
  642.9 12.8 conditional.4
  826.8 12.1 conditional.4
  844.6 12.1 conditional.4
  862.4 12.1 conditional.4
  880.2 12.1 conditional.4
  1056.8 6.9 convolution_convert_fusion.1
  1067.6 703.6 %reduce-scatter.2.cloned.1.call-done = bf16[128,2048]{1,0:T(8,128)(2,1)} async-done(((bf16[2048,2048]{1,0:T(8,128)(2,1)}), bf16[128,2048]{1,0:T(8,128)(2,1)}) %reduce-scatter.2.cloned.1.call-update) | async-done | bytes 524304 | tf_op jit(solution)/shard_map/reduce_scatter | solution.py:135
  1774.9 11.7 scatter_custom_fusion
  1786.6 112.2 %all_to_all.10 = bf16[128,16,2048]{2,1,0:T(8,128)(2,1)S(1)} all-to-all(bf16[128,16,2048]{2,1,0:T(8,128)(2,1)} %bitcast.58), channel_id=1, replica_groups=mesh['ctx'=8,'exp'=16] {'ctx','exp'}, dimensions={0} | all-to-all | bytes 16777216 | tf_op jit(solution)/shard_map/all_to_all | solution.py:160
  1902.1 8.5 fusion.21
  1910.6 21.3 %convolution_convert_fusion = bf16[2048,2048]{1,0:T(8,128)(2,1)} fusion(f32[2048,768]{1,0:T(8,128)} %fusion.21, bf16[2048,2048]{1,0:T(8,128)(2,1)} %bitcast.62, bf16[1,768,2048]{2,1,0:T(8,128)(2,1)S(1)} %copy-done, bf16[1,2048,768]{2,1,0:T(8,128)(2,1)} %param.26), kind=kOutput, calls=%fused_computation.26 | convolution fusion | flops 12898533376 | bytes 29360128 | tf_op jit(solution)/shard_map/dot_general | solution.py:82
  1931.8 5.5 all-to-all-start.1
  1937.5 113.0 %all-to-all-done.1 = bf16[128,16,2048]{2,1,0:T(8,128)(2,1)} async-done(((bf16[128,16,2048]{2,1,0:T(8,128)(2,1)}), bf16[128,16,2048]{2,1,0:T(8,128)(2,1)}, u32[]{:S(2)}, u32[]{:S(2)}) %all-to-all-start.1) | async-done | bytes 8388640 | tf_op jit(solution)/shard_map/all_to_all | solution.py:158
  2050.5 25.5 %gather_fusion = bf16[1024,2048]{1,0:T(8,128)(2,1)} fusion(bf16[128,16,2048]{2,1,0:T(8,128)(2,1)} %all-to-all-done.1, s32[1024]{0:T(1024)S(1)} %bitcast.57), kind=kCustom, calls=%fused_computation | custom fusion | bytes 8396800 | tf_op jit(solution)/shard_map/gather | solution.py:170
  2076.0 6.6 fusion.14
  (1068 shorter events, 391.1 us)
Async XLA Ops:
  6.5 1904.0 %copy-start = (bf16[1,768,2048]{2,1,0:T(8,128)(2,1)S(1)}, bf16[1,768,2048]{2,1,0:T(8,128)(2,1)}, u32[]{:S(2)}) copy-start(bf16[1,768,2048]{2,1,0:T(8,128)(2,1)} %param.27) | copy-start | bytes 9437188
  6.5 6.4 copy-start.7
  6.5 95.6 %all-gather.3.cloned.1.call-start = ((), (), s32[]{:S(2)}) async-start(), calls=%async_computation.3 | async-start | bytes 4718592 | tf_op jit(solution)/shard_map/all_gather | solution.py:124
  8.6 186.6 %all-gather.5.cloned.1.call-start = ((), (), s32[]{:S(2)}) async-start(), calls=%async_computation.4 | async-start | bytes 4718592 | tf_op jit(solution)/shard_map/all_gather | solution.py:125
  10.6 1760.7 %reduce-scatter.2.cloned.1.call-start = ((), (), s32[]{:S(2)}) async-start(), calls=%async_computation.5 | async-start | bytes 8912896 | tf_op jit(solution)/shard_map/reduce_scatter | solution.py:135
  205.3 1.3 copy-start.2
  400.7 1.3 copy-start.2
  608.8 1.3 copy-start.2
  627.3 1.3 copy-start.2
  645.8 1.3 copy-start.2
  829.7 1.3 copy-start.2
  847.5 1.3 copy-start.2
  865.3 1.3 copy-start.2
  883.1 1.3 copy-start.2
  1063.6 3.8 copy-start.12
  1063.6 3.9 copy-start.11
  1064.3 708.4 %copy-start.8 = (f32[2048]{0:T(1024)S(1)}, f32[2048]{0:T(1024)}, u32[]{:S(2)}) copy-start(f32[2048]{0:T(1024)} %param.22) | copy-start | bytes 24580
  1786.6 115.5 %copy-start.13 = (bf16[1,2048,768]{2,1,0:T(8,128)(2,1)S(1)}, bf16[1,2048,768]{2,1,0:T(8,128)(2,1)}, u32[]{:S(2)}) copy-start(bf16[1,2048,768]{2,1,0:T(8,128)(2,1)} %param.25) | copy-start | bytes 9437188
  1898.8 3.2 copy-start.3
  1931.8 5.6 copy-start.10
  1931.8 118.6 %all-to-all-start.1 = ((bf16[128,16,2048]{2,1,0:T(8,128)(2,1)}), bf16[128,16,2048]{2,1,0:T(8,128)(2,1)}, u32[]{:S(2)}, u32[]{:S(2)}) async-start(bf16[128,16,2048]{2,1,0:T(8,128)(2,1)} %bitcast.60), calls=%async_computation.2 | async-start | bytes 16777216 | tf_op jit(solution)/shard_map/all_to_all | solution.py:158
  2050.5 33.1 %copy-start.1 = (bf16[1,768,2048]{2,1,0:T(8,128)(2,1)S(1)}, bf16[1,768,2048]{2,1,0:T(8,128)(2,1)}, u32[]{:S(2)}) copy-start(bf16[1,768,2048]{2,1,0:T(8,128)(2,1)} %param.27) | copy-start | bytes 9437188
  2076.0 6.6 copy-start.4
  2076.0 6.6 copy-start.5
  (3 other events, 2.8 us)
Sparse Core Ops, SparseCore 0:
  9.0 93.0 all-gather.2
  103.7 91.4 all-gather.4
  1063.8 707.4 reduce-scatter.1
where the time goes:
time: 2110 us; the launch traced here: 2090 us
  waiting for transfers between devices  967 us (46%)
  loops' own time  490 us (23%)
  local copies, waits for them, and re-layouts  355 us (17%)
  blocking collectives  145 us (7%)
  matrix products  75.7 us (4%)
  other arithmetic  38.7 us (2%)
    reduce_scatter x1, waiting for transfers between devices, shards(): lax.psum_scatter(jnp.dot(attended, out_weight, preferred_element_type=jnp...  704 us
    another operation x1, loops' own time, attend_keys(): return lax.fori_loop(0, query_count * key_count, tile_step, running)  488 us
    all_to_all x1, waiting for transfers between devices, shards(): lax.all_to_all(expert_rows(lax.all_to_all(outgoing, ('ctx', 'exp'), split...  113 us
    all_to_all x1, blocking collectives, shards(): lax.all_to_all(outgoing, ('ctx', 'exp'), split_axis=0, concat_axis=0, til...  112 us
    all_gather x1, waiting for transfers between devices, shards(): lax.all_gather(my_values, 'ctx', axis=0, tiled=True)  93.1 us
    slice x128, local copies, waits for them, and re-layouts, tile_step(): part_segs[-1]  78 us
    slice x128, local copies, waits for them, and re-layouts, tile_step(): query_pos[-1]  77.2 us
    slice x128, local copies, waits for them, and re-layouts, tile_step(): key_pos[0] <= query_pos[-1]  65.7 us
  transfers between devices with their start and end apart: 4, of which 4 were waited for; matrix products, arithmetic and copies ran while one was open for 0% of the time, Pallas kernels for 0%

commit v1 on v0

v1 whole, which is shorter than its diff:
```python
import math

import jax
import jax.numpy as jnp
from jax import lax
from jax.experimental import pallas as pl
from jax.experimental.pallas import tpu as pltpu
from jax.sharding import Mesh
from jax.sharding import PartitionSpec as P

HEAD_DIM = 128
TOP = 8
SEGS = 32
TILE = 128
KEY_TILE = 512
HIDDEN_SCORE = -1e30
SCORE_SCALE = math.log2(math.e) / math.sqrt(HEAD_DIM)

CTX = ("x", "zl")
EXP = ("y", "zh", "c")
ALL = CTX + EXP
PARTS = (4, 2, 4, 2, 2)

CORE_SWAP = [(0, 1), (1, 0)]


def attend_kernel(block, scalars, q_ref, mine_ref, other_ref, o_ref, *scratch):
    kv, max_ref, total_ref, sum_ref, sems = scratch
    step = pl.program_id(0)
    ctx = scalars[SEGS]
    half = block // 2

    @pl.when(step == 0)
    def _():
        core = scalars[SEGS + 1]
        copies = []
        for i, (piece, side) in enumerate(((mine_ref, core), (other_ref, 1 - core))):
            for b in range(8):
                first = pl.multiple_of(b * block + side * half, half)
                copies.append(
                    pltpu.make_async_copy(
                        piece.at[b, pl.ds(2 * TILE, half), :],
                        kv.at[pl.ds(first, half), :],
                        sems.at[8 * i + b],
                    )
                )
        for copy in copies:
            copy.start()
        for copy in copies:
            copy.wait()

    begin = (step // 2) * block + (step % 2) * (block // 2) + ctx * TILE
    low_first = jnp.int32(0)
    low_last = jnp.int32(0)
    for s in range(SEGS):
        start = scalars[s]
        low_first = jnp.where(start <= begin, start, low_first)
        low_last = jnp.where(start <= begin + TILE - 1, start, low_last)
    chunk_begin = low_first // KEY_TILE
    chunk_end = (begin + TILE - 1) // KEY_TILE + 1
    clear_begin = jnp.minimum((low_last + KEY_TILE - 1) // KEY_TILE, chunk_end)
    clear_end = jnp.maximum(clear_begin, (begin + 1) // KEY_TILE)

    query = jnp.concatenate([q_ref[:, :HEAD_DIM], q_ref[:, HEAD_DIM:]], axis=0)
    position = begin + lax.broadcasted_iota(jnp.int32, (TILE, HEAD_DIM), 0)
    lowest = jnp.zeros((TILE, HEAD_DIM), jnp.int32)
    for s in range(SEGS):
        start = scalars[s]
        lowest = jnp.where(position >= start, start, lowest)
    wide = KEY_TILE // HEAD_DIM
    position = jnp.concatenate([position] * wide, axis=1)
    lowest = jnp.concatenate([lowest] * wide, axis=1)

    max_ref[...] = jnp.full_like(max_ref, HIDDEN_SCORE)
    total_ref[...] = jnp.zeros_like(total_ref)
    sum_ref[...] = jnp.zeros_like(sum_ref)

    def attend(chunk, masked):
        first = pl.multiple_of(chunk * KEY_TILE, KEY_TILE)
        key = kv[pl.ds(first, KEY_TILE), :HEAD_DIM]
        value = kv[pl.ds(first, KEY_TILE), HEAD_DIM:]
        scores = (
            lax.dot_general(
                query, key, (((1,), (1,)), ((), ())), preferred_element_type=jnp.float32
            )
            * SCORE_SCALE
        )
        if masked:
            at = first + lax.broadcasted_iota(jnp.int32, (TILE, KEY_TILE), 1)
            visible = (at >= lowest) & (at <= position)
            visible = jnp.concatenate([visible, visible], axis=0)
            scores = jnp.where(visible, scores, HIDDEN_SCORE)
        old_max = max_ref[...]
        new_max = jnp.maximum(old_max, jnp.max(scores, axis=1, keepdims=True))
        rescale = jnp.exp2(old_max - new_max)
        unnormed = jnp.exp2(scores - new_max)
        total_ref[...] = rescale * total_ref[...] + jnp.sum(unnormed, axis=1, keepdims=True)
        max_ref[...] = new_max
        sum_ref[...] = rescale * sum_ref[...] + jnp.dot(
            unnormed.astype(jnp.bfloat16), value, preferred_element_type=jnp.float32
        )

    @pl.loop(clear_begin, clear_end)
    def _(chunk):
        attend(chunk, False)

    before = clear_begin - chunk_begin

    @pl.loop(0, before + chunk_end - clear_end)
    def _(i):
        attend(jnp.where(i < before, chunk_begin + i, clear_end + i - before), True)

    attended = (sum_ref[...] / total_ref[...]).astype(o_ref.dtype)
    o_ref[:, :HEAD_DIM] = attended[:TILE]
    o_ref[:, HEAD_DIM:] = attended[TILE:]


def attend(queries, key_rows, value_rows, starts, x, zl, y, c):
    block, columns = queries.shape
    half = block // 2
    own = jnp.concatenate(
        [
            lax.dynamic_slice(rows, (c * half, y * HEAD_DIM), (half, HEAD_DIM))
            for rows in (key_rows, value_rows)
        ],
        axis=1,
    )
    striped = jnp.transpose(queries.reshape(2, 8, TILE, columns), (1, 0, 2, 3))
    sent = jnp.concatenate(
        [
            striped.reshape(8, 2 * TILE, columns),
            jnp.broadcast_to(own, (8, half, columns)),
        ],
        axis=1,
    )
    mine = lax.all_to_all(sent, CTX, split_axis=0, concat_axis=0, tiled=True)
    other = lax.ppermute(mine, "c", CORE_SWAP)
    scalars = jnp.concatenate([starts, jnp.stack([x * 2 + zl, c]).astype(jnp.int32)])
    any_spec = pl.BlockSpec(memory_space=pl.ANY)
    return pl.pallas_call(
        lambda *refs: attend_kernel(block, *refs),
        out_shape=jax.ShapeDtypeStruct((8, 2 * TILE, columns), jnp.bfloat16),
        grid_spec=pltpu.PrefetchScalarGridSpec(
            num_scalar_prefetch=1,
            grid=(16,),
            in_specs=[
                pl.BlockSpec((None, TILE, columns), lambda i, s: (i // 2, i % 2, 0)),
                any_spec,
                any_spec,
            ],
            out_specs=pl.BlockSpec((None, TILE, columns), lambda i, s: (i // 2, i % 2, 0)),
            scratch_shapes=[
                pltpu.VMEM((8 * block, 2 * HEAD_DIM), jnp.bfloat16),
                pltpu.VMEM((2 * TILE, 1), jnp.float32),
                pltpu.VMEM((2 * TILE, 1), jnp.float32),
                pltpu.VMEM((2 * TILE, HEAD_DIM), jnp.float32),
                pltpu.SemaphoreType.DMA((16,)),
            ],
        ),
        compiler_params=pltpu.CompilerParams(vmem_limit_bytes=32 << 20),
        name="attend",
    )(scalars, mine, mine, other)


def expert_rows(arrived, gate_weight, up_weight, down_weight):
    in_shape = arrived.shape
    flat_rows = arrived.reshape(-1, in_shape[-1])
    gate_proj = jnp.dot(flat_rows, gate_weight[0], preferred_element_type=jnp.float32)
    up_proj = jnp.dot(flat_rows, up_weight[0], preferred_element_type=jnp.float32)
    hidden = (jax.nn.silu(gate_proj) * up_proj).astype(jnp.bfloat16)
    produced = jnp.dot(hidden, down_weight[0], preferred_element_type=jnp.float32).astype(
        jnp.bfloat16
    )
    return produced.reshape(in_shape)


def shards(
    residual,
    queries,
    key_rows,
    value_rows,
    segment_ids,
    out_weight,
    norm_gain,
    expert_ids,
    route_weight,
    gate_weight,
    up_weight,
    down_weight,
):
    ctx_rows, local_cols = queries.shape
    x, zl, y, c = (lax.axis_index(name) for name in ("x", "zl", "y", "c"))
    counts = jnp.sum(
        segment_ids[None, :] < jnp.arange(SEGS, dtype=jnp.int32)[:, None], axis=1, dtype=jnp.int32
    )
    starts = lax.psum(counts, CTX)
    attended = attend(queries, key_rows, value_rows, starts, x, zl, y, c)
    attended = lax.all_to_all(
        attended.reshape(8, 2, TILE, local_cols), CTX, split_axis=0, concat_axis=1
    ).reshape(ctx_rows, local_cols)
    own_rows = residual.shape[0]
    attention_sum = lax.psum_scatter(
        jnp.dot(attended, out_weight, preferred_element_type=jnp.float32).astype(jnp.bfloat16),
        EXP,
        scatter_dimension=0,
        tiled=True,
    ).astype(jnp.float32)
    mixed_rows = residual.astype(jnp.float32) + attention_sum
    mean_square = jnp.mean(mixed_rows * mixed_rows, axis=-1, keepdims=True)
    normed = (mixed_rows * lax.rsqrt(mean_square + 1e-06) * norm_gain).astype(jnp.bfloat16)
    model_width = normed.shape[1]
    expert_count = 128
    capacity = 2 * own_rows * TOP // expert_count
    flat_ids = expert_ids.reshape(-1)
    onehot = (flat_ids[:, None] == jnp.arange(expert_count, dtype=jnp.int32)[None, :]).astype(
        jnp.int32
    )
    slot_index = jnp.sum(jnp.cumsum(onehot, axis=0) * onehot, axis=1) - 1
    repeated = jnp.repeat(normed, TOP, axis=0)
    outgoing = (
        jnp.zeros((expert_count, capacity, model_width), jnp.bfloat16)
        .at[flat_ids, slot_index]
        .set(repeated)
    )
    returned = lax.all_to_all(
        expert_rows(
            lax.all_to_all(outgoing, ALL, split_axis=0, concat_axis=0, tiled=True),
            gate_weight,
            up_weight,
            down_weight,
        ),
        ALL,
        split_axis=0,
        concat_axis=0,
        tiled=True,
    )
    fetched = returned[flat_ids, slot_index].astype(jnp.float32) * route_weight.reshape(-1)[:, None]
    routed = jnp.sum(fetched.reshape(own_rows, TOP, model_width), axis=1)
    return (mixed_rows + routed).astype(jnp.bfloat16)


def solution(mesh):
    fine = Mesh(mesh.devices.reshape(PARTS), ALL)
    return jax.shard_map(
        shards,
        mesh=fine,
        in_specs=(
            P(ALL, None),
            P(CTX, EXP),
            P(CTX, None),
            P(CTX, None),
            P(CTX),
            P(EXP, None),
            P(),
            P(ALL, None),
            P(ALL, None),
            P(ALL, None, None),
            P(ALL, None, None),
            P(ALL, None, None),
        ),
        out_specs=P(ALL, None),
        check_vma=False,
    )
```

time: 2110 us -> 609 us (0.29)
  waiting for transfers between devices: 967 us -> 212 us
  loops' own time: 490 us -> 0 us
  local copies, waits for them, and re-layouts: 355 us -> 46.4 us
  Pallas kernels: 0 us -> 72.4 us
  blocking collectives: 145 us -> 206 us
  matrix products: 75.7 us -> 35.4 us
  other arithmetic: 38.7 us -> 14.9 us
    reduce_scatter x1, waiting for transfers between devices: 704 us -> 98.8 us  [shards(): lax.psum_scatter(jnp.dot(attended, out_weight, preferred_element_type=jnp...]
    another operation x129 -> x0, loops' own time: 490 us -> none  [the longest x1 488 us: attend_keys(): return lax.fori_loop(0, query_count * key_count, tile_step, running)]
    slice x384 -> x0, local copies, waits for them, and re-layouts: 221 us -> none  [the longest x128 78 us: tile_step(): part_segs[-1]]
    all_gather x2 -> x0, waiting for transfers between devices: 150 us -> none  [the longest x1 93.1 us: shards(): lax.all_gather(my_values, 'ctx', axis=0, tiled=True)]
    all_to_all x1 -> x3, blocking collectives: 112 us -> 196 us  [the longest x1 112 us: shards(): lax.all_to_all(outgoing, ALL, split_axis=0, concat_axis=0, tiled=True)]
    pallas_call x0 -> x1, Pallas kernels: none -> 72.4 us  [attend(): pl.pallas_call(lambda *refs: attend_kernel(block, *refs), out_shape=jax.S...]
    dot_general x20 -> x0, matrix products: 39.1 us -> none  [the longest x10 24.5 us: update(): jnp.einsum('hqk,kd->qhd', weights, value_part, preferred_element_type=jnp...]
    dynamic_update_slice x30 -> x0, local copies, waits for them, and re-layouts: 38.6 us -> none  [the longest x10 33.9 us: update(): lax.dynamic_update_slice_in_dim(accumulated, new_accum, query_begin, 0)]
  transfers between devices with their start and end apart: 4 -> 3, of which waited for: 4 -> 2; matrix products, arithmetic and copies ran while one was open for 0% -> 0% of each run, Pallas kernels for 0% -> 0%
where the time goes in v1:
time: 609 us; the launch traced here: 606 us
  waiting for transfers between devices  212 us (35%)
  blocking collectives  206 us (34%)
  Pallas kernels  72.4 us (12%)
  local copies, waits for them, and re-layouts  46.4 us (8%)
  matrix products  35.4 us (6%)
  other arithmetic  14.9 us (2%)
  between operations  13.6 us (2%)
    all_to_all x1, waiting for transfers between devices, shards(): lax.all_to_all(expert_rows(lax.all_to_all(outgoing, ALL, split_axis=0, co...  113 us
    all_to_all x1, blocking collectives, shards(): lax.all_to_all(outgoing, ALL, split_axis=0, concat_axis=0, tiled=True)  112 us
    reduce_scatter x1, waiting for transfers between devices, shards(): lax.psum_scatter(jnp.dot(attended, out_weight, preferred_element_type=jnp...  98.8 us
    pallas_call x1, Pallas kernels, attend(): pl.pallas_call(lambda *refs: attend_kernel(block, *refs), out_shape=jax.S...  72.4 us
    all_to_all x1, blocking collectives, attend(): mine = lax.all_to_all(sent, CTX, split_axis=0, concat_axis=0, tiled=True)  66.4 us
    gather x1, local copies, waits for them, and re-layouts, shards(): returned[flat_ids, slot_index].astype(jnp.float32)  25.6 us
    dot_general x1, matrix products, expert_rows(): jnp.dot(hidden, down_weight[0], preferred_element_type=jnp.float32)  21.3 us
    all_to_all x1, blocking collectives, shards(): lax.all_to_all(attended.reshape(8, 2, TILE, local_cols), CTX, split_axis=...  16.8 us
  transfers between devices with their start and end apart: 3, of which 2 were waited for; matrix products, arithmetic and copies ran while one was open for 0% of the time, Pallas kernels for 0%

profile of v1, /device:TPU:8, one launch (start us, length us, event | category | flops | bytes accessed | tf_op | source)
XLA Modules:
  0.0 605.7 jit_solution(134248525691186776)
XLA Ops:
  6.5 1.1 dynamic_slice.6
  7.7 1.0 dynamic_slice.7
  8.6 1.3 copy.32
  10.6 66.4 %all_to_all.30.refs_1_.refs_2_ = bf16[8,1280,256]{2,1,0:T(8,128)(2,1)} all-to-all(bf16[8,1280,256]{2,1,0:T(8,128)(2,1)S(1)} %pad_maximum_fusion), channel_id=1, replica_groups=mesh['x'=4,'zl'=2,'y'=4,'zh'=2,'c'=2] {'x','zl'}, dimensions={0} | all-to-all | bytes 10485760 | tf_op jit(solution)/shard_map/all_to_all | solution.py:136
  77.2 10.3 %psum.7 = s32[32]{0:T(128)S(1)} all-reduce(s32[32]{0:T(128)S(1)} %convert_reduce_fusion), channel_id=1, replica_groups=mesh['x'=4,'zl'=2,'y'=4,'zh'=2,'c'=2] {'x','zl'}, use_global_device_ids=true, to_apply=%region_1.0 | all-reduce | flops 32 | bytes 256 | tf_op jit(solution)/shard_map/psum | solution.py:196
  87.5 72.4 %attend.1 = bf16[8,256,256]{2,1,0:T(8,128)(2,1)S(1)} custom-call(s32[34]{0:T(128)S(1)} %pad_add_fusion.1.refs_0_, bf16[8,1280,256]{2,1,0:T(8,128)(2,1)} %all_to_all.30.refs_1_.refs_2_, bf16[8,1280,256]{2,1,0:T(8,128)(2,1)} %all_to_all.30.refs_1_.refs_2_, bf16[8,1280,256]{2,1,0:T(8,128)(2,1)} %collective-permute-done.refs_3_), custom_call_target="tpu_custom_call" | custom-call | tf_op jit(solution)/shard_map/attend/pallas_call | solution.py:140
  159.9 16.8 %all_to_all.31 = bf16[8,2,1,128,256]{4,3,1,2,0:T(8,128)(2,1)S(1)} all-to-all(bf16[8,2,1,128,256]{4,3,1,2,0:T(8,128)(2,1)S(1)} %bitcast.48), channel_id=1, replica_groups=mesh['x'=4,'zl'=2,'y'=4,'zh'=2,'c'=2] {'x','zl'}, dimensions={0} | all-to-all | bytes 2097152 | tf_op jit(solution)/shard_map/all_to_all | solution.py:198
  176.9 5.6 convolution_convert_fusion.1
  182.5 0.7 copy-done.7
  183.8 0.8 copy-done.3
  184.6 1.1 broadcast_add_fusion
  186.4 98.8 %reduce-scatter.2.cloned.1.call-done = bf16[128,2048]{1,0:T(8,128)(2,1)} async-done(((bf16[2048,2048]{1,0:T(8,128)(2,1)}), bf16[128,2048]{1,0:T(8,128)(2,1)}) %reduce-scatter.2.cloned.1.call-update) | async-done | bytes 524304 | tf_op jit(solution)/shard_map/reduce_scatter | solution.py:202
  285.2 1.5 multiply_reduce_fusion
  286.7 2.2 multiply_convert_fusion.1
  288.9 11.7 %scatter_custom_fusion = bf16[2048,2048]{1,0:T(8,128)(2,1)} fusion(s32[1024]{0:T(1024)S(1)} %broadcast_select_fusion, bf16[]{:T(256)} %constant.46.clone.1, bf16[128,2048]{1,0:T(8,128)(2,1)} %multiply_convert_fusion.1), kind=kCustom, calls=%fused_computation.8 | custom fusion | bytes 8912898
  300.6 112.5 %all_to_all.32 = bf16[128,16,2048]{2,1,0:T(8,128)(2,1)S(1)} all-to-all(bf16[128,16,2048]{2,1,0:T(8,128)(2,1)} %bitcast.50), channel_id=1, replica_groups=mesh['x'=4,'zl'=2,'y'=4,'zh'=2,'c'=2] {'x','zl','y','zh','c'}, dimensions={0} | all-to-all | bytes 16777216 | tf_op jit(solution)/shard_map/all_to_all | solution.py:227
  413.1 3.2 copy-done.2
  416.3 8.5 %fusion.7 = f32[2048,768]{1,0:T(8,128)} fusion(bf16[2048,2048]{1,0:T(8,128)(2,1)S(1)} %bitcast.52, bf16[1,2048,768]{2,1,0:T(8,128)(2,1)S(1)} %copy-done.11), kind=kOutput, calls=%fused_computation.13 | convolution fusion | flops 6442450944 | bytes 17825792 | tf_op jit(solution)/shard_map/dot_general | solution.py:168
  424.8 21.3 %convolution_convert_fusion = bf16[2048,2048]{1,0:T(8,128)(2,1)} fusion(f32[2048,768]{1,0:T(8,128)} %fusion.7, bf16[2048,2048]{1,0:T(8,128)(2,1)} %bitcast.53, bf16[1,768,2048]{2,1,0:T(8,128)(2,1)S(1)} %copy-done, bf16[1,2048,768]{2,1,0:T(8,128)(2,1)} %param.22), kind=kOutput, calls=%fused_computation.4 | convolution fusion | flops 12898533376 | bytes 29360128 | tf_op jit(solution)/shard_map/dot_general | solution.py:171
  446.1 5.3 all-to-all-start.3
  451.5 113.0 %all-to-all-done.3 = bf16[128,16,2048]{2,1,0:T(8,128)(2,1)} async-done(((bf16[128,16,2048]{2,1,0:T(8,128)(2,1)}), bf16[128,16,2048]{2,1,0:T(8,128)(2,1)}, u32[]{:S(2)}, u32[]{:S(2)}) %all-to-all-start.3) | async-done | bytes 8388640 | tf_op jit(solution)/shard_map/all_to_all | solution.py:225
  564.5 25.6 %gather_fusion = bf16[1024,2048]{1,0:T(8,128)(2,1)} fusion(bf16[128,16,2048]{2,1,0:T(8,128)(2,1)} %all-to-all-done.3, s32[1024]{0:T(1024)S(1)} %bitcast.49), kind=kCustom, calls=%fused_computation | custom fusion | bytes 8396800 | tf_op jit(solution)/shard_map/gather | solution.py:237
  590.1 6.5 %fusion = f32[128,2048]{1,0:T(8,128)S(1)} fusion(bf16[1024,2048]{1,0:T(8,128)(2,1)} %gather_fusion, f32[128,8]{1,0:T(8,128)S(1)} %copy.40), kind=kLoop, calls=%fused_computation.3 | loop fusion | flops 6029312 | bytes 5246976 | tf_op jit(solution)/shard_map/reduce_sum | solution.py:238
  596.6 2.2 add_convert_fusion
  (49 shorter events, 2.5 us)
Async XLA Ops:
  6.5 418.3 %copy-start = (bf16[1,768,2048]{2,1,0:T(8,128)(2,1)S(1)}, bf16[1,768,2048]{2,1,0:T(8,128)(2,1)}, u32[]{:S(2)}) copy-start(bf16[1,768,2048]{2,1,0:T(8,128)(2,1)} %param.23) | copy-start | bytes 9437188
  6.5 278.7 %reduce-scatter.2.cloned.1.call-start = ((), (), s32[]{:S(2)}) async-start(), calls=%async_computation.5 | async-start | bytes 8912896 | tf_op jit(solution)/shard_map/reduce_scatter | solution.py:202
  10.6 66.4 %copy-start.6 = (s32[2048]{0:T(1024)S(1)}, s32[2048]{0:T(1024)}, u32[]{:S(2)}) copy-start(s32[2048]{0:T(1024)} %param.16) | copy-start | bytes 24580
  77.0 10.5 %collective-permute-start = (bf16[8,1280,256]{2,1,0:T(8,128)(2,1)}, bf16[8,1280,256]{2,1,0:T(8,128)(2,1)}, u32[]{:S(2)}, u32[]{:S(2)}) collective-permute-start(bf16[8,1280,256]{2,1,0:T(8,128)(2,1)} %all_to_all.30.refs_1_.refs_2_), channel_id=1, source_target_pairs={{0,1},{1,0},{2,3},{3,2},{4,5},{5,4},{6,7},{7,6},{8,9},{9,8},{10,11... | collective-permute-start | bytes 15728648 | tf_op jit(solution)/shard_map/ppermute | solution.py:137
  87.5 89.3 %copy-start.4 = (bf16[256,2048]{1,0:T(8,128)(2,1)S(1)}, bf16[256,2048]{1,0:T(8,128)(2,1)}, u32[]{:S(2)}) copy-start(bf16[256,2048]{1,0:T(8,128)(2,1)} %param.17) | copy-start | bytes 3145732
  182.4 0.7 copy-start.7
  182.4 3.8 copy-start.10
  182.4 3.9 copy-start.9
  182.4 104.3 %copy-start.5 = (f32[2048]{0:T(1024)S(1)}, f32[2048]{0:T(1024)}, u32[]{:S(2)}) copy-start(f32[2048]{0:T(1024)} %param.18) | copy-start | bytes 24580
  183.8 0.8 copy-start.3
  300.6 115.7 %copy-start.11 = (bf16[1,2048,768]{2,1,0:T(8,128)(2,1)S(1)}, bf16[1,2048,768]{2,1,0:T(8,128)(2,1)}, u32[]{:S(2)}) copy-start(bf16[1,2048,768]{2,1,0:T(8,128)(2,1)} %param.21) | copy-start | bytes 9437188
  413.1 3.2 copy-start.2
  446.1 5.3 copy-start.8
  446.1 118.4 %all-to-all-start.3 = ((bf16[128,16,2048]{2,1,0:T(8,128)(2,1)}), bf16[128,16,2048]{2,1,0:T(8,128)(2,1)}, u32[]{:S(2)}, u32[]{:S(2)}) async-start(bf16[128,16,2048]{2,1,0:T(8,128)(2,1)} %bitcast.51), calls=%async_computation.4 | async-start | bytes 16777216 | tf_op jit(solution)/shard_map/all_to_all | solution.py:225
  564.5 34.3 %copy-start.1 = (bf16[1,768,2048]{2,1,0:T(8,128)(2,1)S(1)}, bf16[1,768,2048]{2,1,0:T(8,128)(2,1)}, u32[]{:S(2)}) copy-start(bf16[1,768,2048]{2,1,0:T(8,128)(2,1)} %param.23) | copy-start | bytes 9437188
Sparse Core Ops, SparseCore 0:
  182.6 102.5 reduce-scatter.1

commit v2 on v1

--- a/solution.py
+++ b/solution.py
@@ -22,6 +22,9 @@
 PARTS = (4, 2, 4, 2, 2)
 
 CORE_SWAP = [(0, 1), (1, 0)]
+Z_FLIP = [(0, 3), (3, 0), (1, 2), (2, 1)]
+CAPACITY = 16
+SLOT_TILE = 256
 
 
 def attend_kernel(block, scalars, q_ref, mine_ref, other_ref, o_ref, *scratch):
@@ -162,6 +165,123 @@
     )(scalars, mine, mine, other)
 
 
+def mix_kernel(scalars, attended_ref, w0, w1, w2, w3, residual_ref, gain_ref, slots_ref, *refs):
+    mixed_ref, outgoing_ref, total, normed = refs
+    step = pl.program_id(0)
+
+    @pl.when(step == 0)
+    def _():
+        total[...] = residual_ref[...].astype(jnp.float32)
+
+    for p, w_ref in enumerate((w0, w1, w2, w3)):
+
+        @pl.when((step >= 4 * p) & (step < 4 * p + 4))
+        def _(p=p, w_ref=w_ref):
+            block = (step - 4 * p) * 4 + scalars[p]
+            total[...] += jnp.dot(
+                attended_ref[block], w_ref[...], preferred_element_type=jnp.float32
+            )
+
+    @pl.when(step == 15)
+    def _():
+        mixed = total[...]
+        mixed_ref[...] = mixed
+        mean_square = jnp.mean(mixed * mixed, axis=-1, keepdims=True)
+        normed[...] = (mixed * lax.rsqrt(mean_square + 1e-06) * gain_ref[...]).astype(
+            jnp.bfloat16
+        )
+
+    @pl.when(step >= 16)
+    def _():
+        rows = normed.shape[0]
+        slot = (step - 16) * SLOT_TILE + lax.broadcasted_iota(jnp.int32, (SLOT_TILE, rows), 0)
+        chosen = slots_ref[0:1, :] == slot
+        for k in range(1, TOP):
+            chosen = chosen | (slots_ref[k : k + 1, :] == slot)
+        onehot = jnp.where(chosen, 1.0, 0.0).astype(jnp.bfloat16)
+        outgoing_ref[...] = jnp.dot(
+            onehot, normed[...], preferred_element_type=jnp.float32
+        ).astype(jnp.bfloat16)
+
+
+def mix(attended, weights, order, residual, norm_gain, slots):
+    rows, width = residual.shape
+    count = 128 * CAPACITY
+    whole = lambda shape: pl.BlockSpec(shape, lambda i, s: (0,) * len(shape))
+
+    def weight_spec(p):
+        return pl.BlockSpec((256, width), lambda i, s: (jnp.clip(i - 4 * p, 0, 3), 0))
+
+    return pl.pallas_call(
+        mix_kernel,
+        out_shape=(
+            jax.ShapeDtypeStruct((rows, width), jnp.float32),
+            jax.ShapeDtypeStruct((count, width), jnp.bfloat16),
+        ),
+        grid_spec=pltpu.PrefetchScalarGridSpec(
+            num_scalar_prefetch=1,
+            grid=(16 + count // SLOT_TILE,),
+            in_specs=[whole(attended.shape)]
+            + [weight_spec(p) for p in range(4)]
+            + [whole((rows, width)), whole((1, width)), whole((TOP, rows))],
+            out_specs=(
+                whole((rows, width)),
+                pl.BlockSpec((SLOT_TILE, width), lambda i, s: (jnp.maximum(i - 16, 0), 0)),
+            ),
+            scratch_shapes=[
+                pltpu.VMEM((rows, width), jnp.float32),
+                pltpu.VMEM((rows, width), jnp.bfloat16),
+            ],
+        ),
+        compiler_params=pltpu.CompilerParams(vmem_limit_bytes=32 << 20),
+        name="mix",
+    )(order, attended, *weights, residual, norm_gain.reshape(1, width), slots)
+
+
+def combine_kernel(returned_ref, slots_ref, route_ref, mixed_ref, out_ref, total):
+    step = pl.program_id(0)
+
+    @pl.when(step == 0)
+    def _():
+        total[...] = mixed_ref[...]
+
+    rows = total.shape[0]
+    slot = step * SLOT_TILE + lax.broadcasted_iota(jnp.int32, (rows, SLOT_TILE), 1)
+    share = jnp.zeros((rows, SLOT_TILE), jnp.float32)
+    for k in range(TOP):
+        share = jnp.where(slots_ref[:, k : k + 1] == slot, route_ref[:, k : k + 1], share)
+    high = share.astype(jnp.bfloat16)
+    low = (share - high.astype(jnp.float32)).astype(jnp.bfloat16)
+    both = jnp.dot(
+        jnp.concatenate([high, low], axis=0), returned_ref[...], preferred_element_type=jnp.float32
+    )
+    total[...] += both[:rows] + both[rows:]
+
+    @pl.when(step == pl.num_programs(0) - 1)
+    def _():
+        out_ref[...] = total[...].astype(out_ref.dtype)
+
+
+def combine(returned, slots, route_weight, mixed):
+    rows, width = mixed.shape
+    whole = lambda shape: pl.BlockSpec(shape, lambda i: (0, 0))
+    return pl.pallas_call(
+        combine_kernel,
+        out_shape=jax.ShapeDtypeStruct((rows, width), jnp.bfloat16),
+        grid=(returned.shape[0] // SLOT_TILE,),
+        in_specs=[
+            pl.BlockSpec((SLOT_TILE, width), lambda i: (i, 0)),
+            whole((rows, TOP)),
+            whole((rows, TOP)),
+            whole((rows, width)),
+        ],
+        out_specs=whole((rows, width)),
+        scratch_shapes=[pltpu.VMEM((rows, width), jnp.float32)],
+        compiler_params=pltpu.CompilerParams(vmem_limit_bytes=32 << 20),
+        name="combine",
+    )(returned, slots, route_weight, mixed)
+
+
 def expert_rows(arrived, gate_weight, up_weight, down_weight):
     in_shape = arrived.shape
     flat_rows = arrived.reshape(-1, in_shape[-1])
@@ -188,43 +308,43 @@
     up_weight,
     down_weight,
 ):
-    ctx_rows, local_cols = queries.shape
-    x, zl, y, c = (lax.axis_index(name) for name in ("x", "zl", "y", "c"))
+    columns = queries.shape[1]
+    x, zl, y, zh, c = (lax.axis_index(name) for name in ALL)
+    near = lax.all_gather(out_weight, "y", axis=0, tiled=True)
+    far = lax.all_gather(
+        lax.ppermute(out_weight, ("zl", "zh"), Z_FLIP), "y", axis=0, tiled=True
+    )
+    near_other = lax.ppermute(near, "c", CORE_SWAP)
+    order = jnp.stack(
+        [zh * 2 + c, zh * 2 + 1 - c, (1 - zh) * 2 + c, (1 - zh) * 2 + 1 - c]
+    ).astype(jnp.int32)
+
+    flat_ids = expert_ids.reshape(-1)
+    onehot = (flat_ids[:, None] == jnp.arange(128, dtype=jnp.int32)[None, :]).astype(jnp.int32)
+    slot_index = jnp.sum(jnp.cumsum(onehot, axis=0) * onehot, axis=1) - 1
+    slots = (flat_ids * CAPACITY + slot_index).reshape(expert_ids.shape)
+
     counts = jnp.sum(
         segment_ids[None, :] < jnp.arange(SEGS, dtype=jnp.int32)[:, None], axis=1, dtype=jnp.int32
     )
     starts = lax.psum(counts, CTX)
     attended = attend(queries, key_rows, value_rows, starts, x, zl, y, c)
+    attended, far = lax.optimization_barrier((attended, far))
+    far_other = lax.ppermute(far, "c", CORE_SWAP)
     attended = lax.all_to_all(
-        attended.reshape(8, 2, TILE, local_cols), CTX, split_axis=0, concat_axis=1
-    ).reshape(ctx_rows, local_cols)
-    own_rows = residual.shape[0]
-    attention_sum = lax.psum_scatter(
-        jnp.dot(attended, out_weight, preferred_element_type=jnp.float32).astype(jnp.bfloat16),
-        EXP,
-        scatter_dimension=0,
-        tiled=True,
-    ).astype(jnp.float32)
-    mixed_rows = residual.astype(jnp.float32) + attention_sum
-    mean_square = jnp.mean(mixed_rows * mixed_rows, axis=-1, keepdims=True)
-    normed = (mixed_rows * lax.rsqrt(mean_square + 1e-06) * norm_gain).astype(jnp.bfloat16)
-    model_width = normed.shape[1]
-    expert_count = 128
-    capacity = 2 * own_rows * TOP // expert_count
-    flat_ids = expert_ids.reshape(-1)
-    onehot = (flat_ids[:, None] == jnp.arange(expert_count, dtype=jnp.int32)[None, :]).astype(
-        jnp.int32
-    )
-    slot_index = jnp.sum(jnp.cumsum(onehot, axis=0) * onehot, axis=1) - 1
-    repeated = jnp.repeat(normed, TOP, axis=0)
-    outgoing = (
-        jnp.zeros((expert_count, capacity, model_width), jnp.bfloat16)
-        .at[flat_ids, slot_index]
-        .set(repeated)
+        attended.reshape(8, 2, TILE, columns), CTX, split_axis=0, concat_axis=1
+    )
+    attended = lax.all_to_all(
+        attended.reshape(16, TILE, columns), EXP, split_axis=0, concat_axis=0, tiled=True
+    )
+    mixed, outgoing = mix(
+        attended, (near, near_other, far, far_other), order, residual, norm_gain, slots.T
     )
     returned = lax.all_to_all(
         expert_rows(
-            lax.all_to_all(outgoing, ALL, split_axis=0, concat_axis=0, tiled=True),
+            lax.all_to_all(
+                outgoing.reshape(128, CAPACITY, -1), ALL, split_axis=0, concat_axis=0, tiled=True
+            ),
             gate_weight,
             up_weight,
             down_weight,
@@ -234,9 +354,7 @@
         concat_axis=0,
         tiled=True,
     )
-    fetched = returned[flat_ids, slot_index].astype(jnp.float32) * route_weight.reshape(-1)[:, None]
-    routed = jnp.sum(fetched.reshape(own_rows, TOP, model_width), axis=1)
-    return (mixed_rows + routed).astype(jnp.bfloat16)
+    return combine(returned.reshape(128 * CAPACITY, -1), slots, route_weight, mixed)
 
 
 def solution(mesh):

time: 609 us -> 533 us (0.88)
  blocking collectives: 206 us -> 123 us
  local copies, waits for them, and re-layouts: 46.4 us -> 18.5 us
  Pallas kernels: 72.4 us -> 96.9 us
  starting transfers between devices: 5.34 us -> 28 us
  other arithmetic: 14.9 us -> 5.49 us
    reduce_scatter x1 -> x0, waiting for transfers between devices: 98.8 us -> none  [shards(): lax.psum_scatter(jnp.dot(attended, out_weight, preferred_element_type=jnp...]
    all_to_all x3 -> x1, blocking collectives: 196 us -> 112 us  [shards(): lax.all_to_all(outgoing.reshape(128, CAPACITY, -1), ALL, split_axis=0, co...]
    all_to_all x1 -> x4, waiting for transfers between devices: 113 us -> 188 us  [the longest x1 112 us: shards(): lax.all_to_all(expert_rows(lax.all_to_all(outgoing.reshape(128, CAPACITY,...]
    pallas_call x0 -> x2, Pallas kernels: none -> 28.9 us  [the longest x1 18.8 us: mix(): pl.pallas_call(mix_kernel, out_shape=(jax.ShapeDtypeStruct((rows, width),...]
    gather x1 -> x0, local copies, waits for them, and re-layouts: 25.6 us -> none  [shards(): returned[flat_ids, slot_index].astype(jnp.float32)]
    ppermute x0 -> x3, waiting for transfers between devices: none -> 22.9 us  [the longest x1 22.9 us: shards(): lax.ppermute(out_weight, ('zl', 'zh'), Z_FLIP)]
    all_to_all x1 -> x4, starting transfers between devices: 5.33 us -> 23.3 us  [the longest x1 7.95 us: shards(): lax.all_to_all(attended.reshape(16, TILE, columns), EXP, split_axis=0, co...]
    reduce_sum x2 -> x0, other arithmetic: 7.98 us -> none  [the longest x1 6.53 us: shards(): routed = jnp.sum(fetched.reshape(own_rows, TOP, model_width), axis=1)]
  transfers between devices with their start and end apart: 3 -> 10, of which waited for: 2 -> 5; matrix products, arithmetic and copies ran while one was open for 0% -> 2% of each run, Pallas kernels for 0% -> 13%
where the time goes in v2:
time: 533 us; the launch traced here: 526 us
  waiting for transfers between devices  211 us (40%)
  blocking collectives  123 us (23%)
  Pallas kernels  96.9 us (18%)
  matrix products  29.8 us (6%)
  starting transfers between devices  28 us (5%)
  local copies, waits for them, and re-layouts  18.5 us (3%)
  between operations  13.6 us (3%)
  other arithmetic  5.49 us (1%)
    all_to_all x1, waiting for transfers between devices, shards(): lax.all_to_all(expert_rows(lax.all_to_all(outgoing.reshape(128, CAPACITY,...  112 us
    all_to_all x1, blocking collectives, shards(): lax.all_to_all(outgoing.reshape(128, CAPACITY, -1), ALL, split_axis=0, co...  112 us
    pallas_call x1, Pallas kernels, attend(): pl.pallas_call(lambda *refs: attend_kernel(block, *refs), out_shape=jax.S...  68 us
    all_to_all x1, waiting for transfers between devices, attend(): mine = lax.all_to_all(sent, CTX, split_axis=0, concat_axis=0, tiled=True)  46.6 us
    ppermute x1, waiting for transfers between devices, shards(): lax.ppermute(out_weight, ('zl', 'zh'), Z_FLIP)  22.9 us
    dot_general x1, matrix products, expert_rows(): jnp.dot(hidden, down_weight[0], preferred_element_type=jnp.float32)  21.3 us
    pallas_call x1, Pallas kernels, mix(): pl.pallas_call(mix_kernel, out_shape=(jax.ShapeDtypeStruct((rows, width),...  18.8 us
    all_to_all x1, waiting for transfers between devices, shards(): lax.all_to_all(attended.reshape(8, 2, TILE, columns), CTX, split_axis=0,...  15.6 us
  transfers between devices with their start and end apart: 10, of which 5 were waited for; matrix products, arithmetic and copies ran while one was open for 2% of the time, Pallas kernels for 13%

profile of v2, /device:TPU:8, one launch (start us, length us, event | category | flops | bytes accessed | tf_op | source)
XLA Modules:
  0.0 526.5 jit_solution(4905411488960210732)
XLA Ops:
  9.4 1.3 copy.51
  11.1 2.7 pad_maximum_fusion
  13.7 5.8 %all-to-all-start = ((bf16[8,1280,256]{2,1,0:T(8,128)(2,1)}), bf16[8,1280,256]{2,1,0:T(8,128)(2,1)}, u32[]{:S(2)}, u32[]{:S(2)}) async-start(bf16[8,1280,256]{2,1,0:T(8,128)(2,1)} %pad_maximum_fusion), calls=%async_computation | async-start | bytes 10485760 | tf_op jit(solution)/shard_map/all_to_all | solution.py:139
  19.6 4.1 collective-permute-start.1
  23.7 22.9 %collective-permute-done.1 = bf16[256,2048]{1,0:T(8,128)(2,1)} collective-permute-done((bf16[256,2048]{1,0:T(8,128)(2,1)}, bf16[256,2048]{1,0:T(8,128)(2,1)}, u32[]{:S(2)}, u32[]{:S(2)}) %collective-permute-start.1) | collective-permute-done | bytes 1048608 | tf_op jit(solution)/shard_map/ppermute | solution.py:315
  46.6 46.6 %all-to-all-done.refs_1_.refs_2_ = bf16[8,1280,256]{2,1,0:T(8,128)(2,1)} async-done(((bf16[8,1280,256]{2,1,0:T(8,128)(2,1)}), bf16[8,1280,256]{2,1,0:T(8,128)(2,1)}, u32[]{:S(2)}, u32[]{:S(2)}) %all-to-all-start) | async-done | bytes 5242912 | tf_op jit(solution)/shard_map/all_to_all | solution.py:139
  93.3 10.7 %psum.7 = s32[32]{0:T(128)S(1)} all-reduce(s32[32]{0:T(128)S(1)} %convert_reduce_fusion), channel_id=1, replica_groups=mesh['x'=4,'zl'=2,'y'=4,'zh'=2,'c'=2] {'x','zl'}, use_global_device_ids=true, to_apply=%region_1.2 | all-reduce | flops 32 | bytes 256 | tf_op jit(solution)/shard_map/psum | solution.py:330
  104.1 68.0 %attend.1 = bf16[8,256,256]{2,1,0:T(8,128)(2,1)S(1)} custom-call(s32[34]{0:T(128)S(1)} %pad_add_fusion.1.refs_0_, bf16[8,1280,256]{2,1,0:T(8,128)(2,1)} %all-to-all-done.refs_1_.refs_2_, bf16[8,1280,256]{2,1,0:T(8,128)(2,1)} %all-to-all-done.refs_1_.refs_2_, bf16[8,1280,256]{2,1,0:T(8,128)(2,1)} %collective-permute-done.refs_3_), custom_call_target="tpu_custom_call" | custom-call | tf_op jit(solution)/shard_map/attend/pallas_call | solution.py:143
  173.6 4.2 all-to-all-start.1
  179.2 15.6 %all-to-all-done.1 = bf16[8,2,1,128,256]{4,3,1,2,0:T(8,128)(2,1)} async-done(((bf16[8,2,1,128,256]{4,3,1,2,0:T(8,128)(2,1)}), bf16[8,2,1,128,256]{4,3,1,2,0:T(8,128)(2,1)}, u32[]{:S(2)}, u32[]{:S(2)}) %all-to-all-start.1) | async-done | bytes 1048608 | tf_op jit(solution)/shard_map/all_to_all | solution.py:334
  194.8 2.3 copy.53
  197.1 8.0 %all-to-all-start.2 = ((bf16[16,128,256]{2,1,0:T(8,128)(2,1)}), bf16[16,128,256]{2,1,0:T(8,128)(2,1)}, u32[]{:S(2)}, u32[]{:S(2)}) async-start(bf16[16,128,256]{2,1,0:T(8,128)(2,1)} %bitcast.51), calls=%async_computation.2 | async-start | bytes 2097152 | tf_op jit(solution)/shard_map/all_to_all | solution.py:337
  207.7 13.2 %all-to-all-done.2.attended_ref = bf16[16,128,256]{2,1,0:T(8,128)(2,1)} async-done(((bf16[16,128,256]{2,1,0:T(8,128)(2,1)}), bf16[16,128,256]{2,1,0:T(8,128)(2,1)}, u32[]{:S(2)}, u32[]{:S(2)}) %all-to-all-start.2) | async-done | bytes 1048608 | tf_op jit(solution)/shard_map/all_to_all | solution.py:337
  221.0 2.2 copy-done.3
  223.2 2.2 copy-done.4
  226.4 18.8 %mix.1 = (f32[128,2048]{1,0:T(8,128)S(1)}, bf16[2048,2048]{1,0:T(8,128)(2,1)}) custom-call(s32[4]{0:T(128)S(1)} %pad_add_fusion.scalars, bf16[16,128,256]{2,1,0:T(8,128)(2,1)} %all-to-all-done.2.attended_ref, bf16[1024,2048]{1,0:T(8,128)(2,1)S(1)} %copy-done.3, bf16[1024,2048]{1,0:T(8,128)(2,1)} %collective-permute-done.2.w1, ...), custom_call_target="tpu_custom_call" | custom-call | tf_op jit(solution)/shard_map/mix/pallas_call | solution.py:215
  245.2 112.2 %all_to_all.35 = bf16[128,16,2048]{2,1,0:T(8,128)(2,1)S(1)} all-to-all(bf16[128,16,2048]{2,1,0:T(8,128)(2,1)} %bitcast.46), channel_id=1, replica_groups=mesh['x'=4,'zl'=2,'y'=4,'zh'=2,'c'=2] {'x','zl','y','zh','c'}, dimensions={0} | all-to-all | bytes 16777216 | tf_op jit(solution)/shard_map/all_to_all | solution.py:345
  357.4 3.3 copy-done.9
  360.7 8.5 %fusion.3 = f32[2048,768]{1,0:T(8,128)} fusion(bf16[2048,2048]{1,0:T(8,128)(2,1)S(1)} %bitcast.48, bf16[1,2048,768]{2,1,0:T(8,128)(2,1)S(1)} %copy-done.13), kind=kOutput, calls=%fused_computation.5 | convolution fusion | flops 6442450944 | bytes 17825792 | tf_op jit(solution)/shard_map/dot_general | solution.py:288
  369.3 21.3 %convolution_convert_fusion = bf16[2048,2048]{1,0:T(8,128)(2,1)} fusion(f32[2048,768]{1,0:T(8,128)} %fusion.3, bf16[2048,2048]{1,0:T(8,128)(2,1)} %bitcast.49, bf16[1,768,2048]{2,1,0:T(8,128)(2,1)S(1)} %copy-done, bf16[1,2048,768]{2,1,0:T(8,128)(2,1)} %param.22), kind=kOutput, calls=%fused_computation | convolution fusion | flops 12898533376 | bytes 29360128 | tf_op jit(solution)/shard_map/dot_general | solution.py:291
  390.6 5.3 %all-to-all-start.4 = ((bf16[128,16,2048]{2,1,0:T(8,128)(2,1)}), bf16[128,16,2048]{2,1,0:T(8,128)(2,1)}, u32[]{:S(2)}, u32[]{:S(2)}) async-start(bf16[128,16,2048]{2,1,0:T(8,128)(2,1)} %bitcast.47), calls=%async_computation.4 | async-start | bytes 16777216 | tf_op jit(solution)/shard_map/all_to_all | solution.py:343
  396.0 112.3 %all-to-all-done.4 = bf16[128,16,2048]{2,1,0:T(8,128)(2,1)} async-done(((bf16[128,16,2048]{2,1,0:T(8,128)(2,1)}), bf16[128,16,2048]{2,1,0:T(8,128)(2,1)}, u32[]{:S(2)}, u32[]{:S(2)}) %all-to-all-start.4) | async-done | bytes 8388640 | tf_op jit(solution)/shard_map/all_to_all | solution.py:343
  508.3 1.2 copy-done.6
  509.5 10.1 %combine.1 = bf16[128,2048]{1,0:T(8,128)(2,1)} custom-call(bf16[2048,2048]{1,0:T(8,128)(2,1)} %bitcast.25.returned_ref, s32[128,8]{1,0:T(8,128)S(1)} %add.43.slots_ref, f32[128,8]{1,0:T(8,128)S(1)} %copy.60.route_ref, f32[128,2048]{1,0:T(8,128)S(1)} %copy-done.6), custom_call_target="tpu_custom_call" | custom-call | tf_op jit(solution)/shard_map/combine/pallas_call | solution.py:268
  (61 shorter events, 10.2 us)
Async XLA Ops:
  6.5 362.7 %copy-start = (bf16[1,768,2048]{2,1,0:T(8,128)(2,1)S(1)}, bf16[1,768,2048]{2,1,0:T(8,128)(2,1)}, u32[]{:S(2)}) copy-start(bf16[1,768,2048]{2,1,0:T(8,128)(2,1)} %param.23) | copy-start | bytes 9437188
  6.5 97.5 %all-gather.5.cloned.1.call-start = ((), (), s32[]{:S(2)}) async-start(), calls=%async_computation.6 | async-start | bytes 5242880 | tf_op jit(solution)/shard_map/all_gather | solution.py:313
  13.7 79.4 %copy-start.11 = (s32[2048]{0:T(1024)S(1)}, s32[2048]{0:T(1024)}, u32[]{:S(2)}) copy-start(s32[2048]{0:T(1024)} %param.16) | copy-start | bytes 24580
  13.7 79.4 %all-to-all-start = ((bf16[8,1280,256]{2,1,0:T(8,128)(2,1)}), bf16[8,1280,256]{2,1,0:T(8,128)(2,1)}, u32[]{:S(2)}, u32[]{:S(2)}) async-start(bf16[8,1280,256]{2,1,0:T(8,128)(2,1)} %pad_maximum_fusion), calls=%async_computation | async-start | bytes 10485760 | tf_op jit(solution)/shard_map/all_to_all | solution.py:139
  19.5 153.6 %all-gather.3.cloned.1.call-start = ((), (), s32[]{:S(2)}) async-start(), calls=%async_computation.5 | async-start | bytes 5242880 | tf_op jit(solution)/shard_map/all_gather | solution.py:314
  19.6 27.0 %collective-permute-start.1 = (bf16[256,2048]{1,0:T(8,128)(2,1)}, bf16[256,2048]{1,0:T(8,128)(2,1)}, u32[]{:S(2)}, u32[]{:S(2)}) collective-permute-start(bf16[256,2048]{1,0:T(8,128)(2,1)} %param.17), channel_id=1, source_target_pairs={{0,18},{18,0},{2,16},{16,2},{1,19},{19,1},{3,17},{17,3},{4,22},{22... | collective-permute-start | bytes 3145736 | tf_op jit(solution)/shard_map/ppermute | solution.py:315
  93.2 11.0 %collective-permute-start = (bf16[8,1280,256]{2,1,0:T(8,128)(2,1)}, bf16[8,1280,256]{2,1,0:T(8,128)(2,1)}, u32[]{:S(2)}, u32[]{:S(2)}) collective-permute-start(bf16[8,1280,256]{2,1,0:T(8,128)(2,1)} %all-to-all-done.refs_1_.refs_2_), channel_id=1, source_target_pairs={{0,1},{1,0},{2,3},{3,2},{4,5},{5,4},{6,7},{7,6},{8,9},{9,8},{10,11... | collective-permute-start | bytes 15728648 | tf_op jit(solution)/shard_map/ppermute | solution.py:140
  104.1 73.8 %copy-start.10 = (s32[128,8]{0,1:T(8,128)S(1)}, s32[128,8]{0,1:T(8,128)}, u32[]{:S(2)}) copy-start(s32[128,8]{0,1:T(8,128)} %param.19) | copy-start | bytes 12292
  104.1 103.7 %collective-permute-start.2 = (bf16[1024,2048]{1,0:T(8,128)(2,1)}, bf16[1024,2048]{1,0:T(8,128)(2,1)}, u32[]{:S(2)}, u32[]{:S(2)}) collective-permute-start(bf16[1024,2048]{1,0:T(8,128)(2,1)} %all-gather.5.cloned.1.call-done.w0), channel_id=1, source_target_pairs={{0,1},{1,0},{2,3},{3,2},{4,5},{5,4},{6,7},{7,6},{8,9},{9,8},{10,11... | collective-permute-start | bytes 12582920 | tf_op jit(solution)/shard_map/ppermute | solution.py:317
  172.2 1.0 copy-start.2
  173.1 47.9 %copy-start.8 = (f32[2048]{0:T(1024)S(1)}, f32[2048]{0:T(1024)}, u32[]{:S(2)}) copy-start(f32[2048]{0:T(1024)} %param.18) | copy-start | bytes 24580
  173.1 47.9 %collective-permute-start.3 = (bf16[1024,2048]{1,0:T(8,128)(2,1)}, bf16[1024,2048]{1,0:T(8,128)(2,1)}, u32[]{:S(2)}, u32[]{:S(2)}) collective-permute-start(bf16[1024,2048]{1,0:T(8,128)(2,1)} %all-gather.3.cloned.1.call-done.w2), channel_id=1, source_target_pairs={{0,1},{1,0},{2,3},{3,2},{4,5},{5,4},{6,7},{7,6},{8,9},{9,8},{10,11... | collective-permute-start | bytes 12582920 | tf_op jit(solution)/shard_map/ppermute | solution.py:333
  173.6 21.1 %all-to-all-start.1 = ((bf16[8,2,1,128,256]{4,3,1,2,0:T(8,128)(2,1)}), bf16[8,2,1,128,256]{4,3,1,2,0:T(8,128)(2,1)}, u32[]{:S(2)}, u32[]{:S(2)}) async-start(bf16[8,2,1,128,256]{4,3,1,2,0:T(8,128)(2,1)} %bitcast.43), calls=%async_computation.1 | async-start | bytes 2097152 | tf_op jit(solution)/shard_map/all_to_all | solution.py:334
  197.1 23.9 %all-to-all-start.2 = ((bf16[16,128,256]{2,1,0:T(8,128)(2,1)}), bf16[16,128,256]{2,1,0:T(8,128)(2,1)}, u32[]{:S(2)}, u32[]{:S(2)}) async-start(bf16[16,128,256]{2,1,0:T(8,128)(2,1)} %bitcast.51), calls=%async_computation.2 | async-start | bytes 2097152 | tf_op jit(solution)/shard_map/all_to_all | solution.py:337
  221.0 2.2 copy-start.3
  223.2 2.2 copy-start.4
  225.4 1.0 copy-start.7
  245.2 112.3 %copy-start.5 = (f32[128,2048]{1,0:T(8,128)}, f32[128,2048]{1,0:T(8,128)S(1)}, u32[]{:S(2)}) copy-start(f32[128,2048]{1,0:T(8,128)S(1)} %get-tuple-element.12.mixed_ref) | copy-start | bytes 3145732
  245.2 115.5 %copy-start.13 = (bf16[1,2048,768]{2,1,0:T(8,128)(2,1)S(1)}, bf16[1,2048,768]{2,1,0:T(8,128)(2,1)}, u32[]{:S(2)}) copy-start(bf16[1,2048,768]{2,1,0:T(8,128)(2,1)} %param.21) | copy-start | bytes 9437188
  357.4 3.3 copy-start.9
  390.6 5.3 %copy-start.12 = (f32[128,8]{0,1:T(8,128)S(1)}, f32[128,8]{0,1:T(8,128)}, u32[]{:S(2)}) copy-start(f32[128,8]{0,1:T(8,128)} %param.20) | copy-start | bytes 12292
  390.6 117.7 %all-to-all-start.4 = ((bf16[128,16,2048]{2,1,0:T(8,128)(2,1)}), bf16[128,16,2048]{2,1,0:T(8,128)(2,1)}, u32[]{:S(2)}, u32[]{:S(2)}) async-start(bf16[128,16,2048]{2,1,0:T(8,128)(2,1)} %bitcast.47), calls=%async_computation.4 | async-start | bytes 16777216 | tf_op jit(solution)/shard_map/all_to_all | solution.py:343
  395.9 123.7 %copy-start.1 = (bf16[1,768,2048]{2,1,0:T(8,128)(2,1)S(1)}, bf16[1,768,2048]{2,1,0:T(8,128)(2,1)}, u32[]{:S(2)}) copy-start(bf16[1,768,2048]{2,1,0:T(8,128)(2,1)} %param.23) | copy-start | bytes 9437188
  508.3 1.2 copy-start.6
Sparse Core Ops, SparseCore 0:
  9.0 49.9 all-gather.4
  60.6 48.6 all-gather.2

commit v3 on v1

v3 whole, which is shorter than its diff:
```python
import math

import jax
import jax.numpy as jnp
from jax import lax
from jax.experimental import pallas as pl
from jax.experimental.pallas import tpu as pltpu
from jax.sharding import Mesh
from jax.sharding import PartitionSpec as P

HEAD_DIM = 128
TOP = 8
SEGS = 32
TILE = 128
KEY_TILE = 512
HIDDEN_SCORE = -1e30
SCORE_SCALE = math.log2(math.e) / math.sqrt(HEAD_DIM)

CTX = ("x", "zl")
EXP = ("y", "zh", "c")
ALL = CTX + EXP
PARTS = (4, 2, 4, 2, 2)

CORE_SWAP = [(0, 1), (1, 0)]
Z_FLIP = [(0, 3), (3, 0), (1, 2), (2, 1)]
CAPACITY = 16
SLOT_TILE = 256
WIDTH_TILE = 512
VMEM_LIMIT = 60 << 20


def attend_kernel(block, scalars, q_ref, mine_ref, other_ref, o_ref, *scratch):
    kv, max_ref, total_ref, sum_ref, score_ref, sems = scratch
    step = pl.program_id(0)
    ctx = scalars[SEGS]
    core = scalars[SEGS + 1]
    half = block // 2

    def fetch(b):
        return [
            pltpu.make_async_copy(
                piece.at[b, pl.ds(2 * TILE, half), :],
                kv.at[pl.ds(pl.multiple_of(KEY_TILE + b * block + side * half, half), half), :],
                sems.at[i, b],
            )
            for i, (piece, side) in enumerate(((mine_ref, core), (other_ref, 1 - core)))
        ]

    @pl.when(step == 0)
    def _():
        for b in range(8):
            for copy in fetch(b):
                copy.start()
        kv[:KEY_TILE, :] = jnp.zeros((KEY_TILE, 2 * HEAD_DIM), kv.dtype)

    for b in range(8):

        @pl.when(step == 2 * b)
        def _(b=b):
            for copy in fetch(b):
                copy.wait()

    begin = (step // 2) * block + (step % 2) * half + ctx * TILE
    end = begin + TILE
    lowest_first = jnp.int32(0)
    for s in range(SEGS):
        lowest_first = jnp.where(scalars[s] <= begin, scalars[s], lowest_first)
    chunks = (end - lowest_first + KEY_TILE - 1) // KEY_TILE

    query = jnp.concatenate([q_ref[:, :HEAD_DIM], q_ref[:, HEAD_DIM:]], axis=0)
    position = begin + lax.broadcasted_iota(jnp.int32, (TILE, HEAD_DIM), 0)
    lowest = jnp.zeros((TILE, HEAD_DIM), jnp.int32)
    for s in range(SEGS):
        lowest = jnp.where(position >= scalars[s], scalars[s], lowest)
    wide = KEY_TILE // HEAD_DIM
    lane = lax.broadcasted_iota(jnp.int32, (TILE, KEY_TILE), 1)
    lowest = jnp.concatenate([lowest] * wide, axis=1) - lane
    position = jnp.concatenate([position] * wide, axis=1) - lane

    max_ref[...] = jnp.full_like(max_ref, HIDDEN_SCORE)
    total_ref[...] = jnp.zeros_like(total_ref)
    sum_ref[...] = jnp.zeros_like(sum_ref)

    def rows_of(chunk):
        return pl.ds(pl.multiple_of(end - chunk * KEY_TILE, TILE), KEY_TILE)

    def score(slot, chunk):
        score_ref[slot] = lax.dot_general(
            query,
            kv[rows_of(chunk), :HEAD_DIM],
            (((1,), (1,)), ((), ())),
            preferred_element_type=jnp.float32,
        )

    def accumulate(slot, chunk):
        first = end - (chunk + 1) * KEY_TILE
        visible = (lowest <= first) & (position >= first)
        scores = jnp.where(
            jnp.concatenate([visible, visible], axis=0), score_ref[slot] * SCORE_SCALE, HIDDEN_SCORE
        )
        old_max = max_ref[...]
        new_max = jnp.maximum(old_max, jnp.max(scores, axis=1, keepdims=True))
        rescale = jnp.exp2(old_max - new_max)
        unnormed = jnp.exp2(scores - jnp.concatenate([new_max] * wide, axis=1))
        total_ref[...] = rescale * total_ref[...] + jnp.sum(unnormed, axis=1, keepdims=True)
        max_ref[...] = new_max
        sum_ref[...] = rescale * sum_ref[...] + jnp.dot(
            unnormed.astype(jnp.bfloat16),
            kv[rows_of(chunk), HEAD_DIM:],
            preferred_element_type=jnp.float32,
        )

    score(0, 0)

    @pl.loop(0, chunks // 2)
    def _(i):
        chunk = 2 * i
        score(1, chunk + 1)
        accumulate(0, chunk)
        score(0, jnp.minimum(chunk + 2, chunks - 1))
        accumulate(1, chunk + 1)

    @pl.when(chunks % 2 == 1)
    def _():
        accumulate(0, chunks - 1)

    attended = (sum_ref[...] / total_ref[...]).astype(o_ref.dtype)
    o_ref[:, :HEAD_DIM] = attended[:TILE]
    o_ref[:, HEAD_DIM:] = attended[TILE:]


def gather_keys(queries, key_rows, value_rows, y, c):
    block, columns = queries.shape
    half = block // 2
    own = jnp.concatenate(
        [
            lax.dynamic_slice(rows, (c * half, y * HEAD_DIM), (half, HEAD_DIM))
            for rows in (key_rows, value_rows)
        ],
        axis=1,
    )
    striped = jnp.transpose(queries.reshape(2, 8, TILE, columns), (1, 0, 2, 3))
    sent = jnp.concatenate(
        [
            striped.reshape(8, 2 * TILE, columns),
            jnp.broadcast_to(own, (8, half, columns)),
        ],
        axis=1,
    )
    mine = lax.all_to_all(sent, CTX, split_axis=0, concat_axis=0, tiled=True)
    other = lax.ppermute(mine, "c", CORE_SWAP)
    return mine, other


def attend(scalars, mine, other, block):
    columns = mine.shape[2]
    any_spec = pl.BlockSpec(memory_space=pl.ANY)
    tile_spec = pl.BlockSpec((None, TILE, columns), lambda i, s: (i // 2, i % 2, 0))
    return pl.pallas_call(
        lambda *refs: attend_kernel(block, *refs),
        out_shape=jax.ShapeDtypeStruct((8, 2 * TILE, columns), jnp.bfloat16),
        grid_spec=pltpu.PrefetchScalarGridSpec(
            num_scalar_prefetch=1,
            grid=(16,),
            in_specs=[tile_spec, any_spec, any_spec],
            out_specs=tile_spec,
            scratch_shapes=[
                pltpu.VMEM((KEY_TILE + 8 * block, 2 * HEAD_DIM), jnp.bfloat16),
                pltpu.VMEM((2 * TILE, HEAD_DIM), jnp.float32),
                pltpu.VMEM((2 * TILE, HEAD_DIM), jnp.float32),
                pltpu.VMEM((2 * TILE, HEAD_DIM), jnp.float32),
                pltpu.VMEM((2, 2 * TILE, KEY_TILE), jnp.float32),
                pltpu.SemaphoreType.DMA((2, 8)),
            ],
        ),
        compiler_params=pltpu.CompilerParams(vmem_limit_bytes=VMEM_LIMIT),
        cost_estimate=pl.CostEstimate(
            flops=8 << 30, bytes_accessed=12 << 20, transcendentals=16 << 20
        ),
        name="attend",
    )(scalars, mine, mine, other)


def place_rows(slots_ref, normed, first, out_ref):
    count, rows = out_ref.shape[0], normed.shape[0]
    slot = first + lax.broadcasted_iota(jnp.int32, (count, rows), 0)
    chosen = slots_ref[0:1, :] == slot
    for k in range(1, TOP):
        chosen = chosen | (slots_ref[k : k + 1, :] == slot)
    onehot = jnp.where(chosen, 1.0, 0.0).astype(jnp.bfloat16)
    out_ref[...] = jnp.dot(onehot, normed, preferred_element_type=jnp.float32).astype(
        out_ref.dtype
    )


def mix_kernel(scalars, attended_ref, w0, w1, w2, w3, residual_ref, gain_ref, slots_ref, *refs):
    mixed_ref, normed_ref, outgoing_ref = refs
    step = pl.program_id(0)
    tiles = mixed_ref.shape[1] // WIDTH_TILE

    for n in range(tiles):

        @pl.when(step == n)
        def _(n=n):
            columns = slice(n * WIDTH_TILE, (n + 1) * WIDTH_TILE)
            total = residual_ref[:, columns].astype(jnp.float32)
            for p, w_ref in enumerate((w0, w1, w2, w3)):
                rows = jnp.concatenate(
                    [attended_ref[4 * k + scalars[p]] for k in range(4)], axis=1
                )
                total += jnp.dot(rows, w_ref[...], preferred_element_type=jnp.float32)
            mixed_ref[:, columns] = total

    @pl.when(step == tiles - 1)
    def _():
        mixed = mixed_ref[...]
        mean_square = jnp.mean(mixed * mixed, axis=-1, keepdims=True)
        normed_ref[...] = (mixed * lax.rsqrt(mean_square + 1e-06) * gain_ref[...]).astype(
            jnp.bfloat16
        )

    @pl.when(step >= tiles)
    def _():
        place_rows(slots_ref, normed_ref[...], (step - tiles) * SLOT_TILE, outgoing_ref)


def whole(shape):
    return pl.BlockSpec(shape, lambda i, *s: (0,) * len(shape))


def mix(attended, weights, order, residual, norm_gain, slots):
    rows, width = residual.shape
    tiles = width // WIDTH_TILE
    count = 128 * CAPACITY // 2

    return pl.pallas_call(
        mix_kernel,
        out_shape=(
            jax.ShapeDtypeStruct((rows, width), jnp.float32),
            jax.ShapeDtypeStruct((rows, width), jnp.bfloat16),
            jax.ShapeDtypeStruct((count, width), jnp.bfloat16),
        ),
        grid_spec=pltpu.PrefetchScalarGridSpec(
            num_scalar_prefetch=1,
            grid=(tiles + count // SLOT_TILE,),
            in_specs=[whole(attended.shape)]
            + [
                pl.BlockSpec((1024, WIDTH_TILE), lambda i, s: (0, jnp.minimum(i, tiles - 1)))
                for _ in weights
            ]
            + [whole((rows, width)), whole((1, width)), whole((TOP, rows))],
            out_specs=(
                whole((rows, width)),
                whole((rows, width)),
                pl.BlockSpec((SLOT_TILE, width), lambda i, s: (jnp.maximum(i - tiles, 0), 0)),
            ),
        ),
        compiler_params=pltpu.CompilerParams(vmem_limit_bytes=VMEM_LIMIT),
        cost_estimate=pl.CostEstimate(
            flops=3 << 30, bytes_accessed=24 << 20, transcendentals=0
        ),
        name="mix",
    )(order, attended, *weights, residual, norm_gain.reshape(1, width), slots)


def place(normed, slots, first):
    rows, width = normed.shape
    count = 128 * CAPACITY // 2

    def kernel(normed_ref, slots_ref, out_ref):
        place_rows(
            slots_ref, normed_ref[...], first + pl.program_id(0) * SLOT_TILE, out_ref
        )

    return pl.pallas_call(
        kernel,
        out_shape=jax.ShapeDtypeStruct((count, width), jnp.bfloat16),
        grid=(count // SLOT_TILE,),
        in_specs=[whole((rows, width)), whole((TOP, rows))],
        out_specs=pl.BlockSpec((SLOT_TILE, width), lambda i: (i, 0)),
        compiler_params=pltpu.CompilerParams(vmem_limit_bytes=VMEM_LIMIT),
        cost_estimate=pl.CostEstimate(
            flops=1 << 29, bytes_accessed=5 << 20, transcendentals=0
        ),
        name="place",
    )(normed, slots)


def combine(returned, slots, route_weight, base, first, dtype):
    rows, width = base.shape
    count = returned.shape[0]

    def kernel(returned_ref, slots_ref, route_ref, base_ref, out_ref, shares):
        @pl.when(pl.program_id(0) == 0)
        def _():
            slot = first + lax.broadcasted_iota(jnp.int32, (rows, count), 1)
            share = jnp.zeros((rows, count), jnp.float32)
            for k in range(TOP):
                share = jnp.where(
                    slots_ref[:, k : k + 1] == slot, route_ref[:, k : k + 1], share
                )
            high = share.astype(jnp.bfloat16)
            shares[:rows, :] = high
            shares[rows:, :] = (share - high.astype(jnp.float32)).astype(jnp.bfloat16)

        both = jnp.dot(shares[...], returned_ref[...], preferred_element_type=jnp.float32)
        out_ref[...] = (base_ref[...] + (both[:rows] + both[rows:])).astype(out_ref.dtype)

    tile = lambda height: pl.BlockSpec((height, WIDTH_TILE), lambda i: (0, i))
    return pl.pallas_call(
        kernel,
        out_shape=jax.ShapeDtypeStruct((rows, width), dtype),
        grid=(width // WIDTH_TILE,),
        in_specs=[tile(count), whole((rows, TOP)), whole((rows, TOP)), tile(rows)],
        out_specs=tile(rows),
        scratch_shapes=[pltpu.VMEM((2 * rows, count), jnp.bfloat16)],
        compiler_params=pltpu.CompilerParams(vmem_limit_bytes=VMEM_LIMIT),
        cost_estimate=pl.CostEstimate(
            flops=1 << 30, bytes_accessed=6 << 20, transcendentals=0
        ),
        name="combine",
    )(returned, slots, route_weight, base)


def expert_rows(arrived, gate_weight, up_weight, down_weight):
    in_shape = arrived.shape
    flat_rows = arrived.reshape(-1, in_shape[-1])
    gate_proj = jnp.dot(flat_rows, gate_weight[0], preferred_element_type=jnp.float32)
    up_proj = jnp.dot(flat_rows, up_weight[0], preferred_element_type=jnp.float32)
    hidden = (jax.nn.silu(gate_proj) * up_proj).astype(jnp.bfloat16)
    produced = jnp.dot(hidden, down_weight[0], preferred_element_type=jnp.float32).astype(
        jnp.bfloat16
    )
    return produced.reshape(in_shape)


def shards(
    residual,
    queries,
    key_rows,
    value_rows,
    segment_ids,
    out_weight,
    norm_gain,
    expert_ids,
    route_weight,
    gate_weight,
    up_weight,
    down_weight,
):
    columns = queries.shape[1]
    x, zl, y, zh, c = (lax.axis_index(name) for name in ALL)
    near = lax.all_gather(out_weight, "y", axis=0, tiled=True)
    near_other = lax.ppermute(near, "c", CORE_SWAP)
    order = jnp.stack(
        [zh * 2 + c, zh * 2 + 1 - c, (1 - zh) * 2 + c, (1 - zh) * 2 + 1 - c]
    ).astype(jnp.int32)

    flat_ids = expert_ids.reshape(-1)
    onehot = (flat_ids[:, None] == jnp.arange(128, dtype=jnp.int32)[None, :]).astype(jnp.int32)
    slot_index = jnp.sum(jnp.cumsum(onehot, axis=0) * onehot, axis=1) - 1
    half = CAPACITY // 2
    slots = (
        slot_index // half * (128 * half) + flat_ids * half + slot_index % half
    ).reshape(expert_ids.shape)

    counts = jnp.sum(
        segment_ids[None, :] < jnp.arange(SEGS, dtype=jnp.int32)[:, None], axis=1, dtype=jnp.int32
    )
    starts = lax.psum(counts, CTX)
    mine, other = gather_keys(queries, key_rows, value_rows, y, c)
    late_weight, mine = lax.optimization_barrier((out_weight, mine))
    far = lax.all_gather(
        lax.ppermute(late_weight, ("zl", "zh"), Z_FLIP), "y", axis=0, tiled=True
    )
    scalars = jnp.concatenate([starts, jnp.stack([x * 2 + zl, c]).astype(jnp.int32)])
    attended = attend(scalars, mine, other, queries.shape[0])
    attended, far = lax.optimization_barrier((attended, far))
    far_other = lax.ppermute(far, "c", CORE_SWAP)
    attended = lax.all_to_all(
        attended.reshape(8, 2, TILE, columns), CTX, split_axis=0, concat_axis=1
    )
    attended = lax.all_to_all(
        attended.reshape(16, TILE, columns), EXP, split_axis=0, concat_axis=0, tiled=True
    )
    mixed, normed, outgoing = mix(
        attended, (near, near_other, far, far_other), order, residual, norm_gain, slots.T
    )
    count, width = outgoing.shape

    def exchange(rows):
        return lax.all_to_all(
            rows.reshape(128, half, width), ALL, split_axis=0, concat_axis=0, tiled=True
        )

    def experts(rows):
        return expert_rows(rows, gate_weight, up_weight, down_weight)

    arrived_0 = exchange(outgoing)
    arrived_1 = exchange(place(normed, slots.T, count))
    returned_0 = exchange(experts(arrived_0)).reshape(count, width)
    returned_1 = exchange(experts(arrived_1)).reshape(count, width)
    partial = combine(returned_0, slots, route_weight, mixed, 0, jnp.float32)
    return combine(returned_1, slots, route_weight, partial, count, jnp.bfloat16)


def solution(mesh):
    fine = Mesh(mesh.devices.reshape(PARTS), ALL)
    return jax.shard_map(
        shards,
        mesh=fine,
        in_specs=(
            P(ALL, None),
            P(CTX, EXP),
            P(CTX, None),
            P(CTX, None),
            P(CTX),
            P(EXP, None),
            P(),
            P(ALL, None),
            P(ALL, None),
            P(ALL, None, None),
            P(ALL, None, None),
            P(ALL, None, None),
        ),
        out_specs=P(ALL, None),
        check_vma=False,
    )
```

time: 609 us -> 467 us (0.77)
  blocking collectives: 206 us -> 76.6 us
  local copies, waits for them, and re-layouts: 46.4 us -> 7.18 us
  starting transfers between devices: 5.34 us -> 37.4 us
  other arithmetic: 14.9 us -> 3.59 us
  waiting for transfers between devices: 212 us -> 220 us
  Pallas kernels: 72.4 us -> 66.3 us
    all_to_all x3 -> x1, blocking collectives: 196 us -> 66.5 us  [gather_keys(): mine = lax.all_to_all(sent, CTX, split_axis=0, concat_axis=0, tiled=True)]
    reduce_scatter x1 -> x0, waiting for transfers between devices: 98.8 us -> none  [shards(): lax.psum_scatter(jnp.dot(attended, out_weight, preferred_element_type=jnp...]
    all_to_all x1 -> x6, waiting for transfers between devices: 113 us -> 197 us  [the longest x4 169 us: exchange(): lax.all_to_all(rows.reshape(128, half, width), ALL, split_axis=0, concat_...]
    pallas_call x1, Pallas kernels: 72.4 us -> 37.6 us  [attend(): pl.pallas_call(lambda *refs: attend_kernel(block, *refs), out_shape=jax.S...]
    pallas_call x0 -> x4, Pallas kernels: none -> 28.8 us  [the longest x1 13.1 us: mix(): pl.pallas_call(mix_kernel, out_shape=(jax.ShapeDtypeStruct((rows, width),...]
    all_to_all x1 -> x6, starting transfers between devices: 5.33 us -> 33.2 us  [the longest x4 22.1 us: exchange(): lax.all_to_all(rows.reshape(128, half, width), ALL, split_axis=0, concat_...]
    gather x1 -> x0, local copies, waits for them, and re-layouts: 25.6 us -> none  [shards(): returned[flat_ids, slot_index].astype(jnp.float32)]
    ppermute x1 -> x4, waiting for transfers between devices: 0.01 us -> 22.1 us  [the longest x1 22.1 us: shards(): lax.ppermute(late_weight, ('zl', 'zh'), Z_FLIP)]
  transfers between devices with their start and end apart: 3 -> 12, of which waited for: 2 -> 7; matrix products, arithmetic and copies ran while one was open for 0% -> 11% of each run, Pallas kernels for 0% -> 10%
where the time goes in v3:
time: 467 us; the launch traced here: 466 us
  waiting for transfers between devices  220 us (47%)
  blocking collectives  76.6 us (16%)
  Pallas kernels  66.3 us (14%)
  matrix products  40.9 us (9%)
  starting transfers between devices  37.4 us (8%)
  between operations  13.7 us (3%)
  local copies, waits for them, and re-layouts  7.18 us (2%)
    all_to_all x4, waiting for transfers between devices, exchange(): lax.all_to_all(rows.reshape(128, half, width), ALL, split_axis=0, concat_...  169 us
    all_to_all x1, blocking collectives, gather_keys(): mine = lax.all_to_all(sent, CTX, split_axis=0, concat_axis=0, tiled=True)  66.5 us
    pallas_call x1, Pallas kernels, attend(): pl.pallas_call(lambda *refs: attend_kernel(block, *refs), out_shape=jax.S...  37.6 us
    dot_general x2, matrix products, expert_rows(): jnp.dot(hidden, down_weight[0], preferred_element_type=jnp.float32)  24.5 us
    all_to_all x4, starting transfers between devices, exchange(): lax.all_to_all(rows.reshape(128, half, width), ALL, split_axis=0, concat_...  22.1 us
    ppermute x1, waiting for transfers between devices, shards(): lax.ppermute(late_weight, ('zl', 'zh'), Z_FLIP)  22.1 us
    dot_general x2, matrix products, expert_rows(): jnp.dot(flat_rows, gate_weight[0], preferred_element_type=jnp.float32)  16.4 us
    all_to_all x1, waiting for transfers between devices, shards(): lax.all_to_all(attended.reshape(16, TILE, columns), EXP, split_axis=0, co...  14.3 us
  transfers between devices with their start and end apart: 12, of which 7 were waited for; matrix products, arithmetic and copies ran while one was open for 11% of the time, Pallas kernels for 10%

profile of v3, /device:TPU:8, one launch (start us, length us, event | category | flops | bytes accessed | tf_op | source)
XLA Modules:
  0.0 465.9 jit_solution(4450922077167006434)
XLA Ops:
  9.7 66.5 %all_to_all.45.refs_1_.refs_2_ = bf16[8,1280,256]{2,1,0:T(8,128)(2,1)} all-to-all(bf16[8,1280,256]{2,1,0:T(8,128)(2,1)S(1)} %pad_maximum_fusion), channel_id=1, replica_groups=mesh['x'=4,'zl'=2,'y'=4,'zh'=2,'c'=2] {'x','zl'}, dimensions={0} | all-to-all | bytes 10485760 | tf_op jit(solution)/shard_map/all_to_all | solution.py:150
  79.8 22.1 %collective-permute-done.1 = bf16[256,2048]{1,0:T(8,128)(2,1)} collective-permute-done((bf16[256,2048]{1,0:T(8,128)(2,1)S(1)}, bf16[256,2048]{1,0:T(8,128)(2,1)}, u32[]{:S(2)}, u32[]{:S(2)}) %collective-permute-start.1) | collective-permute-done | bytes 1048608 | tf_op jit(solution)/shard_map/ppermute | solution.py:374
  102.2 10.1 %psum.7 = s32[32]{0:T(128)S(1)} all-reduce(s32[32]{0:T(128)S(1)} %convert_reduce_fusion), channel_id=1, replica_groups=mesh['x'=4,'zl'=2,'y'=4,'zh'=2,'c'=2] {'x','zl'}, use_global_device_ids=true, to_apply=%region_1.2 | all-reduce | flops 32 | bytes 256 | tf_op jit(solution)/shard_map/psum | solution.py:370
  112.9 37.6 %attend.1 = bf16[8,256,256]{2,1,0:T(8,128)(2,1)} custom-call(s32[34]{0:T(128)} %pad_add_fusion.1.refs_0_, bf16[8,1280,256]{2,1,0:T(8,128)(2,1)} %all_to_all.45.refs_1_.refs_2_, bf16[8,1280,256]{2,1,0:T(8,128)(2,1)} %all_to_all.45.refs_1_.refs_2_, bf16[8,1280,256]{2,1,0:T(8,128)(2,1)} %collective-permute-done.refs_3_), custom_call_target="tpu_custom_call" | custom-call | flops 8589934592 | bytes 12582912 | tf_op jit(solution)/shard_map/attend/pallas_call | solution.py:159
  151.0 4.2 all-to-all-start.1
  158.2 14.2 %all-to-all-done.1 = bf16[8,2,1,128,256]{4,3,1,2,0:T(8,128)(2,1)} async-done(((bf16[8,2,1,128,256]{4,3,1,2,0:T(8,128)(2,1)}), bf16[8,2,1,128,256]{4,3,1,2,0:T(8,128)(2,1)}, u32[]{:S(2)}, u32[]{:S(2)}) %all-to-all-start.1) | async-done | bytes 1048608 | tf_op jit(solution)/shard_map/all_to_all | solution.py:380
  174.7 6.9 %all-to-all-start.2 = ((bf16[16,128,256]{2,1,0:T(8,128)(2,1)}), bf16[16,128,256]{2,1,0:T(8,128)(2,1)}, u32[]{:S(2)}, u32[]{:S(2)}) async-start(bf16[16,128,256]{2,1,0:T(8,128)(2,1)} %bitcast.79), calls=%async_computation.2 | async-start | bytes 2097152 | tf_op jit(solution)/shard_map/all_to_all | solution.py:383
  183.3 14.3 %all-to-all-done.2.attended_ref = bf16[16,128,256]{2,1,0:T(8,128)(2,1)} async-done(((bf16[16,128,256]{2,1,0:T(8,128)(2,1)}), bf16[16,128,256]{2,1,0:T(8,128)(2,1)}, u32[]{:S(2)}, u32[]{:S(2)}) %all-to-all-start.2) | async-done | bytes 1048608 | tf_op jit(solution)/shard_map/all_to_all | solution.py:383
  197.5 13.1 %mix.1 = (f32[128,2048]{1,0:T(8,128)}, bf16[128,2048]{1,0:T(8,128)(2,1)}, bf16[1024,2048]{1,0:T(8,128)(2,1)}) custom-call(s32[4]{0:T(128)} %pad_add_fusion.scalars, bf16[16,128,256]{2,1,0:T(8,128)(2,1)} %all-to-all-done.2.attended_ref, bf16[1024,2048]{1,0:T(8,128)(2,1)} %all-gather.5.cloned.1.call-done.w0, bf16[1024,2048]{1,0:T(8,128)(2,1)} %collective-permute-done.2.w1, ...), custom_call_target="tpu_custom_call" | custom-call | flops 3221225472 | bytes 25165824 | tf_op jit(solution)/shard_map/mix/pallas_call | solution.py:236
  210.7 6.8 %all-to-all-start.5 = ((bf16[128,8,2048]{2,1,0:T(8,128)(2,1)}), bf16[128,8,2048]{2,1,0:T(8,128)(2,1)}, u32[]{:S(2)}, u32[]{:S(2)}) async-start(bf16[128,8,2048]{2,1,0:T(8,128)(2,1)} %bitcast.78), calls=%async_computation.5 | async-start | bytes 8388608 | tf_op jit(solution)/shard_map/all_to_all | solution.py:392
  217.5 4.5 place.1
  222.0 50.8 %all-to-all-done.5 = bf16[128,8,2048]{2,1,0:T(8,128)(2,1)} async-done(((bf16[128,8,2048]{2,1,0:T(8,128)(2,1)}), bf16[128,8,2048]{2,1,0:T(8,128)(2,1)}, u32[]{:S(2)}, u32[]{:S(2)}) %all-to-all-start.5) | async-done | bytes 4194336 | tf_op jit(solution)/shard_map/all_to_all | solution.py:392
  272.8 5.1 %all-to-all-start.3 = ((bf16[128,8,2048]{2,1,0:T(8,128)(2,1)}), bf16[128,8,2048]{2,1,0:T(8,128)(2,1)}, u32[]{:S(2)}, u32[]{:S(2)}) async-start(bf16[128,8,2048]{2,1,0:T(8,128)(2,1)} %bitcast.76), calls=%async_computation.3 | async-start | bytes 8388608 | tf_op jit(solution)/shard_map/all_to_all | solution.py:392
  277.9 8.2 %fusion.2 = f32[1024,768]{1,0:T(8,128)} fusion(bf16[128,8,2048]{2,1,0:T(8,128)(2,1)} %all-to-all-done.5, bf16[1,2048,768]{2,1,0:T(8,128)(2,1)} %param.21), kind=kOutput, calls=%fused_computation.3 | convolution fusion | flops 3221225472 | bytes 10485760 | tf_op jit(solution)/shard_map/dot_general | solution.py:328
  286.1 12.2 %convert_bitcast_fusion = bf16[128,8,2048]{2,1,0:T(8,128)(2,1)} fusion(bf16[1,768,2048]{2,1,0:T(8,128)(2,1)S(1)} %copy-done, f32[1024,768]{1,0:T(8,128)} %fusion.2, bf16[1,2048,768]{2,1,0:T(8,128)(2,1)} %param.22, bf16[128,8,2048]{2,1,0:T(8,128)(2,1)} %all-to-all-done.5), kind=kOutput, calls=%fused_computation.9 | convolution fusion | flops 6449266688 | bytes 17825792 | tf_op jit(solution)/shard_map/dot_general | solution.py:331
  298.3 34.7 %all-to-all-done.3 = bf16[128,8,2048]{2,1,0:T(8,128)(2,1)} async-done(((bf16[128,8,2048]{2,1,0:T(8,128)(2,1)}), bf16[128,8,2048]{2,1,0:T(8,128)(2,1)}, u32[]{:S(2)}, u32[]{:S(2)}) %all-to-all-start.3) | async-done | bytes 4194336 | tf_op jit(solution)/shard_map/all_to_all | solution.py:392
  333.1 5.1 %all-to-all-start.6 = ((bf16[128,8,2048]{2,1,0:T(8,128)(2,1)}), bf16[128,8,2048]{2,1,0:T(8,128)(2,1)}, u32[]{:S(2)}, u32[]{:S(2)}) async-start(bf16[128,8,2048]{2,1,0:T(8,128)(2,1)} %convert_bitcast_fusion), calls=%async_computation.6 | async-start | bytes 8388608 | tf_op jit(solution)/shard_map/all_to_all | solution.py:392
  338.2 8.2 %fusion.6 = f32[1024,768]{1,0:T(8,128)} fusion(bf16[128,8,2048]{2,1,0:T(8,128)(2,1)} %all-to-all-done.3, bf16[1,2048,768]{2,1,0:T(8,128)(2,1)} %param.21), kind=kOutput, calls=%fused_computation.7 | convolution fusion | flops 3221225472 | bytes 10485760 | tf_op jit(solution)/shard_map/dot_general | solution.py:328
  346.4 12.3 %convert_bitcast_fusion.1 = bf16[128,8,2048]{2,1,0:T(8,128)(2,1)} fusion(bf16[1,768,2048]{2,1,0:T(8,128)(2,1)S(1)} %copy-done, f32[1024,768]{1,0:T(8,128)} %fusion.6, bf16[1,2048,768]{2,1,0:T(8,128)(2,1)} %param.22, bf16[128,8,2048]{2,1,0:T(8,128)(2,1)} %all-to-all-done.3), kind=kOutput, calls=%fused_computation.10 | convolution fusion | flops 6449266688 | bytes 17825792 | tf_op jit(solution)/shard_map/dot_general | solution.py:331
  358.7 34.7 %all-to-all-done.6 = bf16[128,8,2048]{2,1,0:T(8,128)(2,1)} async-done(((bf16[128,8,2048]{2,1,0:T(8,128)(2,1)}), bf16[128,8,2048]{2,1,0:T(8,128)(2,1)}, u32[]{:S(2)}, u32[]{:S(2)}) %all-to-all-start.6) | async-done | bytes 4194336 | tf_op jit(solution)/shard_map/all_to_all | solution.py:392
  393.4 5.1 %all-to-all-start.4 = ((bf16[128,8,2048]{2,1,0:T(8,128)(2,1)}), bf16[128,8,2048]{2,1,0:T(8,128)(2,1)}, u32[]{:S(2)}, u32[]{:S(2)}) async-start(bf16[128,8,2048]{2,1,0:T(8,128)(2,1)} %convert_bitcast_fusion.1), calls=%async_computation.4 | async-start | bytes 8388608 | tf_op jit(solution)/shard_map/all_to_all | solution.py:392
  399.2 5.8 %combine.2.base_ref = f32[128,2048]{1,0:T(8,128)} custom-call(bf16[1024,2048]{1,0:T(8,128)(2,1)} %bitcast.29.returned_ref, s32[128,8]{1,0:T(8,128)} %copy-done.2, f32[128,8]{1,0:T(8,128)} %copy.80.route_ref, f32[128,2048]{1,0:T(8,128)} %get-tuple-element.18.base_ref), custom_call_target="tpu_custom_call" | custom-call | flops 1073741824 | bytes 6291456 | tf_op jit(solution)/shard_map/combine/pallas_call | solution.py:310
  405.0 48.7 %all-to-all-done.4 = bf16[128,8,2048]{2,1,0:T(8,128)(2,1)} async-done(((bf16[128,8,2048]{2,1,0:T(8,128)(2,1)}), bf16[128,8,2048]{2,1,0:T(8,128)(2,1)}, u32[]{:S(2)}, u32[]{:S(2)}) %all-to-all-start.4) | async-done | bytes 4194336 | tf_op jit(solution)/shard_map/all_to_all | solution.py:392
  453.6 5.4 %combine.3 = bf16[128,2048]{1,0:T(8,128)(2,1)} custom-call(bf16[1024,2048]{1,0:T(8,128)(2,1)} %bitcast.25.returned_ref, s32[128,8]{1,0:T(8,128)} %copy-done.2, f32[128,8]{1,0:T(8,128)} %copy.80.route_ref, f32[128,2048]{1,0:T(8,128)} %combine.2.base_ref), custom_call_target="tpu_custom_call" | custom-call | flops 1073741824 | bytes 6291456 | tf_op jit(solution)/shard_map/combine/pallas_call | solution.py:310
  (59 shorter events, 15.7 us)
Async XLA Ops:
  6.5 279.6 %copy-start = (bf16[1,768,2048]{2,1,0:T(8,128)(2,1)S(1)}, bf16[1,768,2048]{2,1,0:T(8,128)(2,1)}, u32[]{:S(2)}) copy-start(bf16[1,768,2048]{2,1,0:T(8,128)(2,1)} %param.23) | copy-start | bytes 9437188
  6.5 106.4 %all-gather.5.cloned.1.call-start = ((), (), s32[]{:S(2)}) async-start(), calls=%async_computation.8 | async-start | bytes 5242880 | tf_op jit(solution)/shard_map/all_gather | solution.py:353
  7.3 143.2 %all-gather.3.cloned.1.call-start = ((), (), s32[]{:S(2)}) async-start(), calls=%async_computation.7 | async-start | bytes 5242880 | tf_op jit(solution)/shard_map/all_gather | solution.py:373
  7.3 1.6 dynamic-slice-start
  7.3 1.7 dynamic-slice-start.1
  9.7 66.5 %copy-start.3 = (bf16[256,2048]{1,0:T(8,128)(2,1)S(1)}, bf16[256,2048]{1,0:T(8,128)(2,1)}, u32[]{:S(2)}) copy-start(bf16[256,2048]{1,0:T(8,128)(2,1)} %param.17) | copy-start | bytes 3145732
  9.7 92.3 %copy-start.5 = (s32[2048]{0:T(1024)S(1)}, s32[2048]{0:T(1024)}, u32[]{:S(2)}) copy-start(s32[2048]{0:T(1024)} %param.16) | copy-start | bytes 24580
  76.2 25.7 %collective-permute-start.1 = (bf16[256,2048]{1,0:T(8,128)(2,1)S(1)}, bf16[256,2048]{1,0:T(8,128)(2,1)}, u32[]{:S(2)}, u32[]{:S(2)}) collective-permute-start(bf16[256,2048]{1,0:T(8,128)(2,1)S(1)} %copy-done.3), channel_id=1, source_target_pairs={{0,18},{18,0},{2,16},{16,2},{1,19},{19,1},{3,17},{17,3},{4,22},{22... | collective-permute-start | bytes 3145736 | tf_op jit(solution)/shard_map/ppermute | solution.py:374
  101.9 11.0 %collective-permute-start = (bf16[8,1280,256]{2,1,0:T(8,128)(2,1)}, bf16[8,1280,256]{2,1,0:T(8,128)(2,1)}, u32[]{:S(2)}, u32[]{:S(2)}) collective-permute-start(bf16[8,1280,256]{2,1,0:T(8,128)(2,1)} %all_to_all.45.refs_1_.refs_2_), channel_id=1, source_target_pairs={{0,1},{1,0},{2,3},{3,2},{4,5},{5,4},{6,7},{7,6},{8,9},{9,8},{10,11... | collective-permute-start | bytes 15728648 | tf_op jit(solution)/shard_map/ppermute | solution.py:151
  112.9 42.3 %copy-start.4 = (s32[128,8]{0,1:T(8,128)S(1)}, s32[128,8]{0,1:T(8,128)}, u32[]{:S(2)}) copy-start(s32[128,8]{0,1:T(8,128)} %param.19) | copy-start | bytes 12292
  112.9 70.3 %collective-permute-start.2 = (bf16[1024,2048]{1,0:T(8,128)(2,1)}, bf16[1024,2048]{1,0:T(8,128)(2,1)}, u32[]{:S(2)}, u32[]{:S(2)}) collective-permute-start(bf16[1024,2048]{1,0:T(8,128)(2,1)} %all-gather.5.cloned.1.call-done.w0), channel_id=1, source_target_pairs={{0,1},{1,0},{2,3},{3,2},{4,5},{5,4},{6,7},{7,6},{8,9},{9,8},{10,11... | collective-permute-start | bytes 12582920 | tf_op jit(solution)/shard_map/ppermute | solution.py:354
  150.5 47.0 %collective-permute-start.3 = (bf16[1024,2048]{1,0:T(8,128)(2,1)}, bf16[1024,2048]{1,0:T(8,128)(2,1)}, u32[]{:S(2)}, u32[]{:S(2)}) collective-permute-start(bf16[1024,2048]{1,0:T(8,128)(2,1)} %all-gather.3.cloned.1.call-done.w2), channel_id=1, source_target_pairs={{0,1},{1,0},{2,3},{3,2},{4,5},{5,4},{6,7},{7,6},{8,9},{9,8},{10,11... | collective-permute-start | bytes 12582920 | tf_op jit(solution)/shard_map/ppermute | solution.py:379
  151.0 21.4 %all-to-all-start.1 = ((bf16[8,2,1,128,256]{4,3,1,2,0:T(8,128)(2,1)}), bf16[8,2,1,128,256]{4,3,1,2,0:T(8,128)(2,1)}, u32[]{:S(2)}, u32[]{:S(2)}) async-start(bf16[8,2,1,128,256]{4,3,1,2,0:T(8,128)(2,1)} %bitcast.82), calls=%async_computation.1 | async-start | bytes 2097152 | tf_op jit(solution)/shard_map/all_to_all | solution.py:380
  155.9 0.8 copy-start.1
  174.7 22.9 %all-to-all-start.2 = ((bf16[16,128,256]{2,1,0:T(8,128)(2,1)}), bf16[16,128,256]{2,1,0:T(8,128)(2,1)}, u32[]{:S(2)}, u32[]{:S(2)}) async-start(bf16[16,128,256]{2,1,0:T(8,128)(2,1)} %bitcast.79), calls=%async_computation.2 | async-start | bytes 2097152 | tf_op jit(solution)/shard_map/all_to_all | solution.py:383
  181.9 28.8 %copy-start.2 = (s32[128,8]{1,0:T(8,128)}, s32[128,8]{1,0:T(8,128)S(1)}, u32[]{:S(2)}) copy-start(s32[128,8]{1,0:T(8,128)S(1)} %fusion.34.slots_ref) | copy-start | bytes 12292
  210.7 62.1 %all-to-all-start.5 = ((bf16[128,8,2048]{2,1,0:T(8,128)(2,1)}), bf16[128,8,2048]{2,1,0:T(8,128)(2,1)}, u32[]{:S(2)}, u32[]{:S(2)}) async-start(bf16[128,8,2048]{2,1,0:T(8,128)(2,1)} %bitcast.78), calls=%async_computation.5 | async-start | bytes 8388608 | tf_op jit(solution)/shard_map/all_to_all | solution.py:392
  272.8 60.3 %all-to-all-start.3 = ((bf16[128,8,2048]{2,1,0:T(8,128)(2,1)}), bf16[128,8,2048]{2,1,0:T(8,128)(2,1)}, u32[]{:S(2)}, u32[]{:S(2)}) async-start(bf16[128,8,2048]{2,1,0:T(8,128)(2,1)} %bitcast.76), calls=%async_computation.3 | async-start | bytes 8388608 | tf_op jit(solution)/shard_map/all_to_all | solution.py:392
  333.1 60.3 %all-to-all-start.6 = ((bf16[128,8,2048]{2,1,0:T(8,128)(2,1)}), bf16[128,8,2048]{2,1,0:T(8,128)(2,1)}, u32[]{:S(2)}, u32[]{:S(2)}) async-start(bf16[128,8,2048]{2,1,0:T(8,128)(2,1)} %convert_bitcast_fusion), calls=%async_computation.6 | async-start | bytes 8388608 | tf_op jit(solution)/shard_map/all_to_all | solution.py:392
  358.7 39.8 %copy-start.6 = (f32[128,8]{0,1:T(8,128)S(1)}, f32[128,8]{0,1:T(8,128)}, u32[]{:S(2)}) copy-start(f32[128,8]{0,1:T(8,128)} %param.20) | copy-start | bytes 12292
  393.4 60.3 %all-to-all-start.4 = ((bf16[128,8,2048]{2,1,0:T(8,128)(2,1)}), bf16[128,8,2048]{2,1,0:T(8,128)(2,1)}, u32[]{:S(2)}, u32[]{:S(2)}) async-start(bf16[128,8,2048]{2,1,0:T(8,128)(2,1)} %convert_bitcast_fusion.1), calls=%async_computation.4 | async-start | bytes 8388608 | tf_op jit(solution)/shard_map/all_to_all | solution.py:392
Sparse Core Ops, SparseCore 0:
  9.0 49.9 all-gather.4
  102.0 46.9 all-gather.2

commit v4 on v3

--- a/solution.py
+++ b/solution.py
@@ -13,16 +13,17 @@
 SEGS = 32
 TILE = 128
 KEY_TILE = 512
+UNROLL = 4
 HIDDEN_SCORE = -1e30
 SCORE_SCALE = math.log2(math.e) / math.sqrt(HEAD_DIM)
 
 CTX = ("x", "zl")
-EXP = ("y", "zh", "c")
+EXP = ("yh", "yl", "zh", "c")
 ALL = CTX + EXP
-PARTS = (4, 2, 4, 2, 2)
+PARTS = (4, 2, 2, 2, 2, 2)
+OWNER = ("yl", "zh", "c", "yh")
 
 CORE_SWAP = [(0, 1), (1, 0)]
-Z_FLIP = [(0, 3), (3, 0), (1, 2), (2, 1)]
 CAPACITY = 16
 SLOT_TILE = 256
 WIDTH_TILE = 512
@@ -110,19 +111,27 @@
             preferred_element_type=jnp.float32,
         )
 
+    last = chunks - 1
     score(0, 0)
 
-    @pl.loop(0, chunks // 2)
+    def run(first, count):
+        for i in range(count):
+            score((i + 1) % 2, jnp.minimum(first + i + 1, last))
+            accumulate(i % 2, first + i)
+
+    @pl.loop(0, chunks // UNROLL)
     def _(i):
-        chunk = 2 * i
-        score(1, chunk + 1)
-        accumulate(0, chunk)
-        score(0, jnp.minimum(chunk + 2, chunks - 1))
-        accumulate(1, chunk + 1)
+        run(UNROLL * i, UNROLL)
+
+    if UNROLL == 4:
+
+        @pl.when(chunks % 4 >= 2)
+        def _():
+            run(chunks // 4 * 4, 2)
 
     @pl.when(chunks % 2 == 1)
     def _():
-        accumulate(0, chunks - 1)
+        accumulate(0, last)
 
     attended = (sum_ref[...] / total_ref[...]).astype(o_ref.dtype)
     o_ref[:, :HEAD_DIM] = attended[:TILE]
@@ -193,7 +202,7 @@
     )
 
 
-def mix_kernel(scalars, attended_ref, w0, w1, w2, w3, residual_ref, gain_ref, slots_ref, *refs):
+def mix_kernel(scalars, attended_ref, w0, w1, residual_ref, gain_ref, slots_ref, *refs):
     mixed_ref, normed_ref, outgoing_ref = refs
     step = pl.program_id(0)
     tiles = mixed_ref.shape[1] // WIDTH_TILE
@@ -204,9 +213,13 @@
         def _(n=n):
             columns = slice(n * WIDTH_TILE, (n + 1) * WIDTH_TILE)
             total = residual_ref[:, columns].astype(jnp.float32)
-            for p, w_ref in enumerate((w0, w1, w2, w3)):
+            for p, w_ref in enumerate((w0, w1)):
                 rows = jnp.concatenate(
-                    [attended_ref[4 * k + scalars[p]] for k in range(4)], axis=1
+                    [
+                        attended_ref[k % 4 * 4 + scalars[p] * 2 + k // 4]
+                        for k in range(8)
+                    ],
+                    axis=1,
                 )
                 total += jnp.dot(rows, w_ref[...], preferred_element_type=jnp.float32)
             mixed_ref[:, columns] = total
@@ -245,7 +258,7 @@
             grid=(tiles + count // SLOT_TILE,),
             in_specs=[whole(attended.shape)]
             + [
-                pl.BlockSpec((1024, WIDTH_TILE), lambda i, s: (0, jnp.minimum(i, tiles - 1)))
+                pl.BlockSpec((2048, WIDTH_TILE), lambda i, s: (0, jnp.minimum(i, tiles - 1)))
                 for _ in weights
             ]
             + [whole((rows, width)), whole((1, width)), whole((TOP, rows))],
@@ -286,40 +299,76 @@
     )(normed, slots)
 
 
-def combine(returned, slots, route_weight, base, first, dtype):
+def share_rows(slots_ref, route_ref, first, count):
+    rows = slots_ref.shape[0]
+    slot = first + lax.broadcasted_iota(jnp.int32, (rows, count), 1)
+    share = jnp.zeros((rows, count), jnp.float32)
+    for k in range(TOP):
+        share = jnp.where(slots_ref[:, k : k + 1] == slot, route_ref[:, k : k + 1], share)
+    high = share.astype(jnp.bfloat16)
+    low = (share - high.astype(jnp.float32)).astype(jnp.bfloat16)
+    return jnp.concatenate([high, low], axis=0)
+
+
+def add_routed(shares, returned_ref, base_ref, out_ref):
+    rows = base_ref.shape[0]
+    both = jnp.dot(shares, returned_ref[...], preferred_element_type=jnp.float32)
+    out_ref[...] = (base_ref[...] + (both[:rows] + both[rows:])).astype(out_ref.dtype)
+
+
+def column_tile(height):
+    return pl.BlockSpec((height, WIDTH_TILE), lambda i: (0, i))
+
+
+COMBINE_PARAMS = dict(
+    compiler_params=pltpu.CompilerParams(vmem_limit_bytes=VMEM_LIMIT),
+    cost_estimate=pl.CostEstimate(flops=1 << 30, bytes_accessed=6 << 20, transcendentals=0),
+)
+
+
+def combine_first(returned, slots, route_weight, base):
     rows, width = base.shape
     count = returned.shape[0]
 
-    def kernel(returned_ref, slots_ref, route_ref, base_ref, out_ref, shares):
+    def kernel(returned_ref, slots_ref, route_ref, base_ref, out_ref, late_ref, shares):
         @pl.when(pl.program_id(0) == 0)
         def _():
-            slot = first + lax.broadcasted_iota(jnp.int32, (rows, count), 1)
-            share = jnp.zeros((rows, count), jnp.float32)
-            for k in range(TOP):
-                share = jnp.where(
-                    slots_ref[:, k : k + 1] == slot, route_ref[:, k : k + 1], share
-                )
-            high = share.astype(jnp.bfloat16)
-            shares[:rows, :] = high
-            shares[rows:, :] = (share - high.astype(jnp.float32)).astype(jnp.bfloat16)
-
-        both = jnp.dot(shares[...], returned_ref[...], preferred_element_type=jnp.float32)
-        out_ref[...] = (base_ref[...] + (both[:rows] + both[rows:])).astype(out_ref.dtype)
-
-    tile = lambda height: pl.BlockSpec((height, WIDTH_TILE), lambda i: (0, i))
+            shares[...] = share_rows(slots_ref, route_ref, 0, count)
+            late_ref[...] = share_rows(slots_ref, route_ref, count, count)
+
+        add_routed(shares[...], returned_ref, base_ref, out_ref)
+
     return pl.pallas_call(
         kernel,
-        out_shape=jax.ShapeDtypeStruct((rows, width), dtype),
+        out_shape=(
+            jax.ShapeDtypeStruct((rows, width), jnp.float32),
+            jax.ShapeDtypeStruct((2 * rows, count), jnp.bfloat16),
+        ),
         grid=(width // WIDTH_TILE,),
-        in_specs=[tile(count), whole((rows, TOP)), whole((rows, TOP)), tile(rows)],
-        out_specs=tile(rows),
+        in_specs=[column_tile(count), whole((rows, TOP)), whole((rows, TOP)), column_tile(rows)],
+        out_specs=(column_tile(rows), whole((2 * rows, count))),
         scratch_shapes=[pltpu.VMEM((2 * rows, count), jnp.bfloat16)],
-        compiler_params=pltpu.CompilerParams(vmem_limit_bytes=VMEM_LIMIT),
-        cost_estimate=pl.CostEstimate(
-            flops=1 << 30, bytes_accessed=6 << 20, transcendentals=0
-        ),
-        name="combine",
+        name="combine_first",
+        **COMBINE_PARAMS,
     )(returned, slots, route_weight, base)
+
+
+def combine_last(returned, shares, base):
+    rows, width = base.shape
+    count = returned.shape[0]
+
+    def kernel(returned_ref, shares_ref, base_ref, out_ref):
+        add_routed(shares_ref[...], returned_ref, base_ref, out_ref)
+
+    return pl.pallas_call(
+        kernel,
+        out_shape=jax.ShapeDtypeStruct((rows, width), jnp.bfloat16),
+        grid=(width // WIDTH_TILE,),
+        in_specs=[column_tile(count), whole((2 * rows, count)), column_tile(rows)],
+        out_specs=column_tile(rows),
+        name="combine_last",
+        **COMBINE_PARAMS,
+    )(returned, shares, base)
 
 
 def expert_rows(arrived, gate_weight, up_weight, down_weight):
@@ -349,12 +398,9 @@
     down_weight,
 ):
     columns = queries.shape[1]
-    x, zl, y, zh, c = (lax.axis_index(name) for name in ALL)
-    near = lax.all_gather(out_weight, "y", axis=0, tiled=True)
-    near_other = lax.ppermute(near, "c", CORE_SWAP)
-    order = jnp.stack(
-        [zh * 2 + c, zh * 2 + 1 - c, (1 - zh) * 2 + c, (1 - zh) * 2 + 1 - c]
-    ).astype(jnp.int32)
+    x, zl, yh, yl, zh, c = (lax.axis_index(name) for name in ALL)
+    near = lax.all_gather(out_weight, ("yh", "yl", "zh"), axis=0, tiled=True)
+    order = jnp.stack([c, 1 - c]).astype(jnp.int32)
 
     flat_ids = expert_ids.reshape(-1)
     onehot = (flat_ids[:, None] == jnp.arange(128, dtype=jnp.int32)[None, :]).astype(jnp.int32)
@@ -368,23 +414,17 @@
         segment_ids[None, :] < jnp.arange(SEGS, dtype=jnp.int32)[:, None], axis=1, dtype=jnp.int32
     )
     starts = lax.psum(counts, CTX)
-    mine, other = gather_keys(queries, key_rows, value_rows, y, c)
-    late_weight, mine = lax.optimization_barrier((out_weight, mine))
-    far = lax.all_gather(
-        lax.ppermute(late_weight, ("zl", "zh"), Z_FLIP), "y", axis=0, tiled=True
-    )
+    mine, other = gather_keys(queries, key_rows, value_rows, yh * 2 + yl, c)
     scalars = jnp.concatenate([starts, jnp.stack([x * 2 + zl, c]).astype(jnp.int32)])
     attended = attend(scalars, mine, other, queries.shape[0])
-    attended, far = lax.optimization_barrier((attended, far))
-    far_other = lax.ppermute(far, "c", CORE_SWAP)
+    attended = lax.all_to_all(attended, CTX, split_axis=0, concat_axis=0, tiled=True)
+    attended, near = lax.optimization_barrier((attended, near))
+    near_other = lax.ppermute(near, "c", CORE_SWAP)
     attended = lax.all_to_all(
-        attended.reshape(8, 2, TILE, columns), CTX, split_axis=0, concat_axis=1
-    )
-    attended = lax.all_to_all(
-        attended.reshape(16, TILE, columns), EXP, split_axis=0, concat_axis=0, tiled=True
+        attended.reshape(16, TILE, columns), OWNER, split_axis=0, concat_axis=0, tiled=True
     )
     mixed, normed, outgoing = mix(
-        attended, (near, near_other, far, far_other), order, residual, norm_gain, slots.T
+        attended, (near, near_other), order, residual, norm_gain, slots.T
     )
     count, width = outgoing.shape
 
@@ -400,8 +440,8 @@
     arrived_1 = exchange(place(normed, slots.T, count))
     returned_0 = exchange(experts(arrived_0)).reshape(count, width)
     returned_1 = exchange(experts(arrived_1)).reshape(count, width)
-    partial = combine(returned_0, slots, route_weight, mixed, 0, jnp.float32)
-    return combine(returned_1, slots, route_weight, partial, count, jnp.bfloat16)
+    partial, shares = combine_first(returned_0, slots, route_weight, mixed)
+    return combine_last(returned_1, shares, partial)
 
 
 def solution(mesh):

time: 467 us -> 473 us (1.013)
  blocking collectives: 76.6 us -> 108 us
  waiting for transfers between devices: 220 us -> 209 us
  starting transfers between devices: 37.4 us -> 28.5 us
    all_gather x2 -> x1, waiting for transfers between devices: 0.02 us -> 26.3 us  [shards(): near = lax.all_gather(out_weight, ('yh', 'yl', 'zh'), axis=0, tiled=True)]
    ppermute x2 -> x0, waiting for transfers between devices: 22.1 us -> none  [the longest x1 22.1 us: shards(): lax.ppermute(late_weight, ('zl', 'zh'), Z_FLIP)]
    all_to_all x0 -> x1, blocking collectives: none -> 20.8 us  [shards(): lax.all_to_all(attended, CTX, split_axis=0, concat_axis=0, tiled=True)]
    all_to_all x2 -> x1, waiting for transfers between devices: 28.4 us -> 14.2 us  [shards(): lax.all_to_all(attended.reshape(16, TILE, columns), OWNER, split_axis=0,...]
    all_to_all x1, blocking collectives: 66.5 us -> 75.3 us  [gather_keys(): mine = lax.all_to_all(sent, CTX, split_axis=0, concat_axis=0, tiled=True)]
    all_to_all x2 -> x1, starting transfers between devices: 11.1 us -> 5.88 us  [shards(): lax.all_to_all(attended.reshape(16, TILE, columns), OWNER, split_axis=0,...]
  transfers between devices with their start and end apart: 12 -> 8, of which waited for: 7 -> 6; matrix products, arithmetic and copies ran while one was open for 11% -> 10% of each run, Pallas kernels for 10% -> 10%
where the time goes in v4:
time: 473 us; the launch traced here: 472 us
  waiting for transfers between devices  209 us (44%)
  blocking collectives  108 us (23%)
  Pallas kernels  63.2 us (13%)
  matrix products  40.9 us (9%)
  starting transfers between devices  28.5 us (6%)
  between operations  13.6 us (3%)
  local copies, waits for them, and re-layouts  4.92 us (1%)
    all_to_all x4, waiting for transfers between devices, exchange(): lax.all_to_all(rows.reshape(128, half, width), ALL, split_axis=0, concat_...  168 us
    all_to_all x1, blocking collectives, gather_keys(): mine = lax.all_to_all(sent, CTX, split_axis=0, concat_axis=0, tiled=True)  75.3 us
    pallas_call x1, Pallas kernels, attend(): pl.pallas_call(lambda *refs: attend_kernel(block, *refs), out_shape=jax.S...  34.5 us
    all_gather x1, waiting for transfers between devices, shards(): near = lax.all_gather(out_weight, ('yh', 'yl', 'zh'), axis=0, tiled=True)  26.3 us
    dot_general x2, matrix products, expert_rows(): jnp.dot(hidden, down_weight[0], preferred_element_type=jnp.float32)  24.5 us
    all_to_all x4, starting transfers between devices, exchange(): lax.all_to_all(rows.reshape(128, half, width), ALL, split_axis=0, concat_...  22.6 us
    all_to_all x1, blocking collectives, shards(): lax.all_to_all(attended, CTX, split_axis=0, concat_axis=0, tiled=True)  20.8 us
    dot_general x2, matrix products, expert_rows(): jnp.dot(flat_rows, gate_weight[0], preferred_element_type=jnp.float32)  16.4 us
  transfers between devices with their start and end apart: 8, of which 6 were waited for; matrix products, arithmetic and copies ran while one was open for 10% of the time, Pallas kernels for 10%

profile of v4, /device:TPU:8, one launch (start us, length us, event | category | flops | bytes accessed | tf_op | source)
XLA Modules:
  0.0 471.8 jit_solution(17322011692149803981)
XLA Ops:
  7.3 1.5 copy.45
  9.7 75.3 %all_to_all.35.refs_1_.refs_2_ = bf16[8,1280,256]{2,1,0:T(8,128)(2,1)} all-to-all(bf16[8,1280,256]{2,1,0:T(8,128)(2,1)S(1)} %pad_maximum_fusion), channel_id=1, replica_groups=mesh['x'=4,'zl'=2,'yh'=2,'yl'=2,'zh'=2,'c'=2] {'x','zl'}, dimensions={0} | all-to-all | bytes 10485760 | tf_op jit(solution)/shard_map/all_to_all | solution.py:159
  85.2 11.6 %psum.7 = s32[32]{0:T(128)S(1)} all-reduce(s32[32]{0:T(128)S(1)} %convert_reduce_fusion), channel_id=1, replica_groups=mesh['x'=4,'zl'=2,'yh'=2,'yl'=2,'zh'=2,'c'=2] {'x','zl'}, use_global_device_ids=true, to_apply=%region_1.2 | all-reduce | flops 32 | bytes 256 | tf_op jit(solution)/shard_map/psum | solution.py:416
  97.4 34.5 %attend.1 = bf16[8,256,256]{2,1,0:T(8,128)(2,1)} custom-call(s32[34]{0:T(128)} %pad_add_fusion.1.refs_0_, bf16[8,1280,256]{2,1,0:T(8,128)(2,1)} %all_to_all.35.refs_1_.refs_2_, bf16[8,1280,256]{2,1,0:T(8,128)(2,1)} %all_to_all.35.refs_1_.refs_2_, bf16[8,1280,256]{2,1,0:T(8,128)(2,1)} %collective-permute-done.refs_3_), custom_call_target="tpu_custom_call" | custom-call | flops 8589934592 | bytes 12582912 | tf_op jit(solution)/shard_map/attend/pallas_call | solution.py:168
  132.0 20.8 %all_to_all.36 = bf16[8,256,256]{2,1,0:T(8,128)(2,1)} all-to-all(bf16[8,256,256]{2,1,0:T(8,128)(2,1)} %attend.1), channel_id=1, replica_groups=mesh['x'=4,'zl'=2,'yh'=2,'yl'=2,'zh'=2,'c'=2] {'x','zl'}, dimensions={0} | all-to-all | bytes 2097152 | tf_op jit(solution)/shard_map/all_to_all | solution.py:420
  152.8 26.3 %all-gather.2.cloned.1.call-done.w0 = bf16[2048,2048]{1,0:T(8,128)(2,1)} async-done(((bf16[256,2048]{1,0:T(8,128)(2,1)}), bf16[2048,2048]{1,0:T(8,128)(2,1)}) %all-gather.2.cloned.1.call-update) | async-done | bytes 8388624 | tf_op jit(solution)/shard_map/all_gather | solution.py:402
  182.0 5.9 %all-to-all-start.2 = ((bf16[16,128,256]{2,1,0:T(8,128)(2,1)}), bf16[16,128,256]{2,1,0:T(8,128)(2,1)}, u32[]{:S(2)}, u32[]{:S(2)}) async-start(bf16[16,128,256]{2,1,0:T(8,128)(2,1)} %bitcast.70), calls=%async_computation.2 | async-start | bytes 2097152 | tf_op jit(solution)/shard_map/all_to_all | solution.py:423
  189.5 14.2 %all-to-all-done.2.attended_ref = bf16[16,128,256]{2,1,0:T(8,128)(2,1)} async-done(((bf16[16,128,256]{2,1,0:T(8,128)(2,1)}), bf16[16,128,256]{2,1,0:T(8,128)(2,1)}, u32[]{:S(2)}, u32[]{:S(2)}) %all-to-all-start.2) | async-done | bytes 1048608 | tf_op jit(solution)/shard_map/all_to_all | solution.py:423
  203.8 12.8 %mix.1 = (f32[128,2048]{1,0:T(8,128)}, bf16[128,2048]{1,0:T(8,128)(2,1)}, bf16[1024,2048]{1,0:T(8,128)(2,1)}) custom-call(s32[2]{0:T(128)} %pad_add_fusion.scalars, bf16[16,128,256]{2,1,0:T(8,128)(2,1)} %all-to-all-done.2.attended_ref, bf16[2048,2048]{1,0:T(8,128)(2,1)} %all-gather.2.cloned.1.call-done.w0, bf16[2048,2048]{1,0:T(8,128)(2,1)} %collective-permute-done.1.w1, ...), custom_call_target="tpu_custom_call" | custom-call | flops 3221225472 | bytes 25165824 | tf_op jit(solution)/shard_map/mix/pallas_call | solution.py:249
  216.6 7.4 %all-to-all-start.5 = ((bf16[128,8,2048]{2,1,0:T(8,128)(2,1)}), bf16[128,8,2048]{2,1,0:T(8,128)(2,1)}, u32[]{:S(2)}, u32[]{:S(2)}) async-start(bf16[128,8,2048]{2,1,0:T(8,128)(2,1)} %bitcast.69), calls=%async_computation.5 | async-start | bytes 8388608 | tf_op jit(solution)/shard_map/all_to_all | solution.py:432
  224.0 4.5 place.1
  228.4 50.7 %all-to-all-done.5 = bf16[128,8,2048]{2,1,0:T(8,128)(2,1)} async-done(((bf16[128,8,2048]{2,1,0:T(8,128)(2,1)}), bf16[128,8,2048]{2,1,0:T(8,128)(2,1)}, u32[]{:S(2)}, u32[]{:S(2)}) %all-to-all-start.5) | async-done | bytes 4194336 | tf_op jit(solution)/shard_map/all_to_all | solution.py:432
  279.2 5.1 %all-to-all-start.3 = ((bf16[128,8,2048]{2,1,0:T(8,128)(2,1)}), bf16[128,8,2048]{2,1,0:T(8,128)(2,1)}, u32[]{:S(2)}, u32[]{:S(2)}) async-start(bf16[128,8,2048]{2,1,0:T(8,128)(2,1)} %bitcast.67), calls=%async_computation.3 | async-start | bytes 8388608 | tf_op jit(solution)/shard_map/all_to_all | solution.py:432
  284.3 8.2 %fusion.2 = f32[1024,768]{1,0:T(8,128)} fusion(bf16[128,8,2048]{2,1,0:T(8,128)(2,1)} %all-to-all-done.5, bf16[1,2048,768]{2,1,0:T(8,128)(2,1)} %param.21), kind=kOutput, calls=%fused_computation.3 | convolution fusion | flops 3221225472 | bytes 10485760 | tf_op jit(solution)/shard_map/dot_general | solution.py:377
  292.5 12.2 %convert_bitcast_fusion = bf16[128,8,2048]{2,1,0:T(8,128)(2,1)} fusion(bf16[1,768,2048]{2,1,0:T(8,128)(2,1)S(1)} %copy-done, f32[1024,768]{1,0:T(8,128)} %fusion.2, bf16[1,2048,768]{2,1,0:T(8,128)(2,1)} %param.22, bf16[128,8,2048]{2,1,0:T(8,128)(2,1)} %all-to-all-done.5), kind=kOutput, calls=%fused_computation.9 | convolution fusion | flops 6449266688 | bytes 17825792 | tf_op jit(solution)/shard_map/dot_general | solution.py:380
  304.7 34.8 %all-to-all-done.3 = bf16[128,8,2048]{2,1,0:T(8,128)(2,1)} async-done(((bf16[128,8,2048]{2,1,0:T(8,128)(2,1)}), bf16[128,8,2048]{2,1,0:T(8,128)(2,1)}, u32[]{:S(2)}, u32[]{:S(2)}) %all-to-all-start.3) | async-done | bytes 4194336 | tf_op jit(solution)/shard_map/all_to_all | solution.py:432
  339.4 5.1 %all-to-all-start.6 = ((bf16[128,8,2048]{2,1,0:T(8,128)(2,1)}), bf16[128,8,2048]{2,1,0:T(8,128)(2,1)}, u32[]{:S(2)}, u32[]{:S(2)}) async-start(bf16[128,8,2048]{2,1,0:T(8,128)(2,1)} %convert_bitcast_fusion), calls=%async_computation.6 | async-start | bytes 8388608 | tf_op jit(solution)/shard_map/all_to_all | solution.py:432
  344.5 8.2 %fusion.6 = f32[1024,768]{1,0:T(8,128)} fusion(bf16[128,8,2048]{2,1,0:T(8,128)(2,1)} %all-to-all-done.3, bf16[1,2048,768]{2,1,0:T(8,128)(2,1)} %param.21), kind=kOutput, calls=%fused_computation.7 | convolution fusion | flops 3221225472 | bytes 10485760 | tf_op jit(solution)/shard_map/dot_general | solution.py:377
  352.7 12.3 %convert_bitcast_fusion.1 = bf16[128,8,2048]{2,1,0:T(8,128)(2,1)} fusion(bf16[1,768,2048]{2,1,0:T(8,128)(2,1)S(1)} %copy-done, f32[1024,768]{1,0:T(8,128)} %fusion.6, bf16[1,2048,768]{2,1,0:T(8,128)(2,1)} %param.22, bf16[128,8,2048]{2,1,0:T(8,128)(2,1)} %all-to-all-done.3), kind=kOutput, calls=%fused_computation.10 | convolution fusion | flops 6449266688 | bytes 17825792 | tf_op jit(solution)/shard_map/dot_general | solution.py:380
  365.0 34.7 %all-to-all-done.6 = bf16[128,8,2048]{2,1,0:T(8,128)(2,1)} async-done(((bf16[128,8,2048]{2,1,0:T(8,128)(2,1)}), bf16[128,8,2048]{2,1,0:T(8,128)(2,1)}, u32[]{:S(2)}, u32[]{:S(2)}) %all-to-all-start.6) | async-done | bytes 4194336 | tf_op jit(solution)/shard_map/all_to_all | solution.py:432
  399.7 5.1 %all-to-all-start.4 = ((bf16[128,8,2048]{2,1,0:T(8,128)(2,1)}), bf16[128,8,2048]{2,1,0:T(8,128)(2,1)}, u32[]{:S(2)}, u32[]{:S(2)}) async-start(bf16[128,8,2048]{2,1,0:T(8,128)(2,1)} %convert_bitcast_fusion.1), calls=%async_computation.4 | async-start | bytes 8388608 | tf_op jit(solution)/shard_map/all_to_all | solution.py:432
  405.5 6.4 %combine_first.1 = (f32[128,2048]{1,0:T(8,128)}, bf16[256,1024]{1,0:T(8,128)(2,1)}) custom-call(bf16[1024,2048]{1,0:T(8,128)(2,1)} %bitcast.22.returned_ref, s32[128,8]{1,0:T(8,128)} %copy-done.2, f32[128,8]{1,0:T(8,128)} %copy.55.route_ref, f32[128,2048]{1,0:T(8,128)} %get-tuple-element.16.base_ref), custom_call_target="tpu_custom_call" | custom-call | flops 1073741824 | bytes 6291456 | tf_op jit(solution)/shard_map/combine_first/pallas_call | solution.py:341
  411.9 48.1 %all-to-all-done.4 = bf16[128,8,2048]{2,1,0:T(8,128)(2,1)} async-done(((bf16[128,8,2048]{2,1,0:T(8,128)(2,1)}), bf16[128,8,2048]{2,1,0:T(8,128)(2,1)}, u32[]{:S(2)}, u32[]{:S(2)}) %all-to-all-start.4) | async-done | bytes 4194336 | tf_op jit(solution)/shard_map/all_to_all | solution.py:432
  460.0 5.0 %combine_last.1 = bf16[128,2048]{1,0:T(8,128)(2,1)} custom-call(bf16[1024,2048]{1,0:T(8,128)(2,1)} %bitcast.18.returned_ref, bf16[256,1024]{1,0:T(8,128)(2,1)} %get-tuple-element.17.shares_ref, f32[128,2048]{1,0:T(8,128)} %get-tuple-element.18.base_ref), custom_call_target="tpu_custom_call" | custom-call | flops 1073741824 | bytes 6291456 | tf_op jit(solution)/shard_map/combine_last/pallas_call | solution.py:363
  (48 shorter events, 7.7 us)
Async XLA Ops:
  6.5 285.9 %copy-start = (bf16[1,768,2048]{2,1,0:T(8,128)(2,1)S(1)}, bf16[1,768,2048]{2,1,0:T(8,128)(2,1)}, u32[]{:S(2)}) copy-start(bf16[1,768,2048]{2,1,0:T(8,128)(2,1)} %param.23) | copy-start | bytes 9437188
  6.5 172.5 %all-gather.2.cloned.1.call-start = ((), (), s32[]{:S(2)}) async-start(), calls=%async_computation.7 | async-start | bytes 9437184 | tf_op jit(solution)/shard_map/all_gather | solution.py:402
  7.3 1.6 dynamic-slice-start
  7.3 1.7 dynamic-slice-start.1
  9.7 75.3 %copy-start.4 = (s32[2048]{0:T(1024)S(1)}, s32[2048]{0:T(1024)}, u32[]{:S(2)}) copy-start(s32[2048]{0:T(1024)} %param.16) | copy-start | bytes 24580
  85.0 12.4 %collective-permute-start = (bf16[8,1280,256]{2,1,0:T(8,128)(2,1)}, bf16[8,1280,256]{2,1,0:T(8,128)(2,1)}, u32[]{:S(2)}, u32[]{:S(2)}) collective-permute-start(bf16[8,1280,256]{2,1,0:T(8,128)(2,1)} %all_to_all.35.refs_1_.refs_2_), channel_id=1, source_target_pairs={{0,1},{1,0},{2,3},{3,2},{4,5},{5,4},{6,7},{7,6},{8,9},{9,8},{10,11... | collective-permute-start | bytes 15728648 | tf_op jit(solution)/shard_map/ppermute | solution.py:160
  97.4 81.6 %copy-start.3 = (s32[128,8]{0,1:T(8,128)S(1)}, s32[128,8]{0,1:T(8,128)}, u32[]{:S(2)}) copy-start(s32[128,8]{0,1:T(8,128)} %param.19) | copy-start | bytes 12292
  179.0 24.7 %collective-permute-start.1 = (bf16[2048,2048]{1,0:T(8,128)(2,1)}, bf16[2048,2048]{1,0:T(8,128)(2,1)}, u32[]{:S(2)}, u32[]{:S(2)}) collective-permute-start(bf16[2048,2048]{1,0:T(8,128)(2,1)} %all-gather.2.cloned.1.call-done.w0), channel_id=1, source_target_pairs={{0,1},{1,0},{2,3},{3,2},{4,5},{5,4},{6,7},{7,6},{8,9},{9,8},{10,11... | collective-permute-start | bytes 25165832 | tf_op jit(solution)/shard_map/ppermute | solution.py:422
  179.6 0.8 copy-start.1
  182.0 21.8 %all-to-all-start.2 = ((bf16[16,128,256]{2,1,0:T(8,128)(2,1)}), bf16[16,128,256]{2,1,0:T(8,128)(2,1)}, u32[]{:S(2)}, u32[]{:S(2)}) async-start(bf16[16,128,256]{2,1,0:T(8,128)(2,1)} %bitcast.70), calls=%async_computation.2 | async-start | bytes 2097152 | tf_op jit(solution)/shard_map/all_to_all | solution.py:423
  188.3 28.3 %copy-start.2 = (s32[128,8]{1,0:T(8,128)}, s32[128,8]{1,0:T(8,128)S(1)}, u32[]{:S(2)}) copy-start(s32[128,8]{1,0:T(8,128)S(1)} %fusion.34.slots_ref) | copy-start | bytes 12292
  216.6 62.6 %all-to-all-start.5 = ((bf16[128,8,2048]{2,1,0:T(8,128)(2,1)}), bf16[128,8,2048]{2,1,0:T(8,128)(2,1)}, u32[]{:S(2)}, u32[]{:S(2)}) async-start(bf16[128,8,2048]{2,1,0:T(8,128)(2,1)} %bitcast.69), calls=%async_computation.5 | async-start | bytes 8388608 | tf_op jit(solution)/shard_map/all_to_all | solution.py:432
  279.2 60.3 %all-to-all-start.3 = ((bf16[128,8,2048]{2,1,0:T(8,128)(2,1)}), bf16[128,8,2048]{2,1,0:T(8,128)(2,1)}, u32[]{:S(2)}, u32[]{:S(2)}) async-start(bf16[128,8,2048]{2,1,0:T(8,128)(2,1)} %bitcast.67), calls=%async_computation.3 | async-start | bytes 8388608 | tf_op jit(solution)/shard_map/all_to_all | solution.py:432
  339.4 60.3 %all-to-all-start.6 = ((bf16[128,8,2048]{2,1,0:T(8,128)(2,1)}), bf16[128,8,2048]{2,1,0:T(8,128)(2,1)}, u32[]{:S(2)}, u32[]{:S(2)}) async-start(bf16[128,8,2048]{2,1,0:T(8,128)(2,1)} %convert_bitcast_fusion), calls=%async_computation.6 | async-start | bytes 8388608 | tf_op jit(solution)/shard_map/all_to_all | solution.py:432
  365.0 39.8 %copy-start.5 = (f32[128,8]{0,1:T(8,128)S(1)}, f32[128,8]{0,1:T(8,128)}, u32[]{:S(2)}) copy-start(f32[128,8]{0,1:T(8,128)} %param.20) | copy-start | bytes 12292
  399.7 60.3 %all-to-all-start.4 = ((bf16[128,8,2048]{2,1,0:T(8,128)(2,1)}), bf16[128,8,2048]{2,1,0:T(8,128)(2,1)}, u32[]{:S(2)}, u32[]{:S(2)}) async-start(bf16[128,8,2048]{2,1,0:T(8,128)(2,1)} %convert_bitcast_fusion.1), calls=%async_computation.4 | async-start | bytes 8388608 | tf_op jit(solution)/shard_map/all_to_all | solution.py:432
Sparse Core Ops, SparseCore 0:
  9.7 169.2 all-gather.1

commit v5 on v4

--- a/solution.py
+++ b/solution.py
@@ -24,6 +24,7 @@
 OWNER = ("yl", "zh", "c", "yh")
 
 CORE_SWAP = [(0, 1), (1, 0)]
+Z_FLIP = [(0, 3), (3, 0), (1, 2), (2, 1)]
 CAPACITY = 16
 SLOT_TILE = 256
 WIDTH_TILE = 512
@@ -202,7 +203,7 @@
     )
 
 
-def mix_kernel(scalars, attended_ref, w0, w1, residual_ref, gain_ref, slots_ref, *refs):
+def mix_kernel(scalars, attended_ref, w0, w1, w2, w3, residual_ref, gain_ref, slots_ref, *refs):
     mixed_ref, normed_ref, outgoing_ref = refs
     step = pl.program_id(0)
     tiles = mixed_ref.shape[1] // WIDTH_TILE
@@ -213,12 +214,9 @@
         def _(n=n):
             columns = slice(n * WIDTH_TILE, (n + 1) * WIDTH_TILE)
             total = residual_ref[:, columns].astype(jnp.float32)
-            for p, w_ref in enumerate((w0, w1)):
+            for p, w_ref in enumerate((w0, w1, w2, w3)):
                 rows = jnp.concatenate(
-                    [
-                        attended_ref[k % 4 * 4 + scalars[p] * 2 + k // 4]
-                        for k in range(8)
-                    ],
+                    [attended_ref[k % 2 * 8 + scalars[p] * 2 + k // 2] for k in range(4)],
                     axis=1,
                 )
                 total += jnp.dot(rows, w_ref[...], preferred_element_type=jnp.float32)
@@ -258,7 +256,7 @@
             grid=(tiles + count // SLOT_TILE,),
             in_specs=[whole(attended.shape)]
             + [
-                pl.BlockSpec((2048, WIDTH_TILE), lambda i, s: (0, jnp.minimum(i, tiles - 1)))
+                pl.BlockSpec((1024, WIDTH_TILE), lambda i, s: (0, jnp.minimum(i, tiles - 1)))
                 for _ in weights
             ]
             + [whole((rows, width)), whole((1, width)), whole((TOP, rows))],
@@ -399,8 +397,11 @@
 ):
     columns = queries.shape[1]
     x, zl, yh, yl, zh, c = (lax.axis_index(name) for name in ALL)
-    near = lax.all_gather(out_weight, ("yh", "yl", "zh"), axis=0, tiled=True)
-    order = jnp.stack([c, 1 - c]).astype(jnp.int32)
+    near = lax.all_gather(out_weight, ("yh", "yl"), axis=0, tiled=True)
+    near_other = lax.ppermute(near, "c", CORE_SWAP)
+    order = jnp.stack(
+        [zh * 2 + c, zh * 2 + 1 - c, (1 - zh) * 2 + c, (1 - zh) * 2 + 1 - c]
+    ).astype(jnp.int32)
 
     flat_ids = expert_ids.reshape(-1)
     onehot = (flat_ids[:, None] == jnp.arange(128, dtype=jnp.int32)[None, :]).astype(jnp.int32)
@@ -415,16 +416,20 @@
     )
     starts = lax.psum(counts, CTX)
     mine, other = gather_keys(queries, key_rows, value_rows, yh * 2 + yl, c)
+    late_weight, mine = lax.optimization_barrier((out_weight, mine))
+    far = lax.ppermute(late_weight, ("zl", "zh"), Z_FLIP)
+    far, starts, other = lax.optimization_barrier((far, starts, other))
+    far = lax.all_gather(far, ("yh", "yl"), axis=0, tiled=True)
     scalars = jnp.concatenate([starts, jnp.stack([x * 2 + zl, c]).astype(jnp.int32)])
     attended = attend(scalars, mine, other, queries.shape[0])
     attended = lax.all_to_all(attended, CTX, split_axis=0, concat_axis=0, tiled=True)
-    attended, near = lax.optimization_barrier((attended, near))
-    near_other = lax.ppermute(near, "c", CORE_SWAP)
+    attended, far = lax.optimization_barrier((attended, far))
+    far_other = lax.ppermute(far, "c", CORE_SWAP)
     attended = lax.all_to_all(
         attended.reshape(16, TILE, columns), OWNER, split_axis=0, concat_axis=0, tiled=True
     )
     mixed, normed, outgoing = mix(
-        attended, (near, near_other), order, residual, norm_gain, slots.T
+        attended, (near, near_other, far, far_other), order, residual, norm_gain, slots.T
     )
     count, width = outgoing.shape
 

time: 473 us -> 469 us (level)
  blocking collectives: 108 us -> 11 us
  waiting for transfers between devices: 209 us -> 285 us
  starting transfers between devices: 28.5 us -> 41.7 us
    all_to_all x2 -> x0, blocking collectives: 96.1 us -> none  [the longest x1 75.3 us: gather_keys(): mine = lax.all_to_all(sent, CTX, split_axis=0, concat_axis=0, tiled=True)]
    all_to_all x0 -> x2, waiting for transfers between devices: none -> 89 us  [the longest x1 72.9 us: gather_keys(): mine = lax.all_to_all(sent, CTX, split_axis=0, concat_axis=0, tiled=True)]
    all_gather x1 -> x2, waiting for transfers between devices: 26.3 us -> 0.02 us  [the longest x1 0.02 us: shards(): near = lax.all_gather(out_weight, ('yh', 'yl'), axis=0, tiled=True)]
    ppermute x0 -> x2, waiting for transfers between devices: none -> 13.1 us  [the longest x1 13.1 us: shards(): far = lax.ppermute(late_weight, ('zl', 'zh'), Z_FLIP)]
    all_to_all x0 -> x2, starting transfers between devices: none -> 10 us  [the longest x1 5.79 us: gather_keys(): mine = lax.all_to_all(sent, CTX, split_axis=0, concat_axis=0, tiled=True)]
  transfers between devices with their start and end apart: 8 -> 13, of which waited for: 6 -> 8; matrix products, arithmetic and copies ran while one was open for 10% -> 10% of each run, Pallas kernels for 10% -> 10%
where the time goes in v5:
time: 469 us; the launch traced here: 467 us
  waiting for transfers between devices  285 us (61%)
  Pallas kernels  63.1 us (13%)
  starting transfers between devices  41.7 us (9%)
  matrix products  41 us (9%)
  between operations  13.6 us (3%)
  blocking collectives  11 us (2%)
  other arithmetic  5.77 us (1%)
  local copies, waits for them, and re-layouts  5.49 us (1%)
    all_to_all x4, waiting for transfers between devices, exchange(): lax.all_to_all(rows.reshape(128, half, width), ALL, split_axis=0, concat_...  168 us
    all_to_all x1, waiting for transfers between devices, gather_keys(): mine = lax.all_to_all(sent, CTX, split_axis=0, concat_axis=0, tiled=True)  72.9 us
    pallas_call x1, Pallas kernels, attend(): pl.pallas_call(lambda *refs: attend_kernel(block, *refs), out_shape=jax.S...  34.2 us
    dot_general x2, matrix products, expert_rows(): jnp.dot(hidden, down_weight[0], preferred_element_type=jnp.float32)  24.6 us
    all_to_all x4, starting transfers between devices, exchange(): lax.all_to_all(rows.reshape(128, half, width), ALL, split_axis=0, concat_...  21.9 us
    dot_general x2, matrix products, expert_rows(): jnp.dot(flat_rows, gate_weight[0], preferred_element_type=jnp.float32)  16.4 us
    all_to_all x1, waiting for transfers between devices, shards(): lax.all_to_all(attended, CTX, split_axis=0, concat_axis=0, tiled=True)  16.1 us
    all_to_all x1, waiting for transfers between devices, shards(): lax.all_to_all(attended.reshape(16, TILE, columns), OWNER, split_axis=0,...  14.2 us
  transfers between devices with their start and end apart: 13, of which 8 were waited for; matrix products, arithmetic and copies ran while one was open for 10% of the time, Pallas kernels for 10%

profile of v5, /device:TPU:8, one launch (start us, length us, event | category | flops | bytes accessed | tf_op | source)
XLA Modules:
  0.0 467.1 jit_solution(7772992644975160748)
XLA Ops:
  11.8 5.8 %all-to-all-start = ((bf16[8,1280,256]{2,1,0:T(8,128)(2,1)}), bf16[8,1280,256]{2,1,0:T(8,128)(2,1)}, u32[]{:S(2)}, u32[]{:S(2)}) async-start(bf16[8,1280,256]{2,1,0:T(8,128)(2,1)} %pad_maximum_fusion), calls=%async_computation | async-start | bytes 10485760 | tf_op jit(solution)/shard_map/all_to_all | solution.py:160
  18.4 72.9 %all-to-all-done.refs_1_.refs_2_ = bf16[8,1280,256]{2,1,0:T(8,128)(2,1)} async-done(((bf16[8,1280,256]{2,1,0:T(8,128)(2,1)}), bf16[8,1280,256]{2,1,0:T(8,128)(2,1)}, u32[]{:S(2)}, u32[]{:S(2)}) %all-to-all-start) | async-done | bytes 5242912 | tf_op jit(solution)/shard_map/all_to_all | solution.py:160
  94.2 11.0 %psum.7 = s32[32]{0:T(128)S(1)} all-reduce(s32[32]{0:T(128)S(1)} %convert_reduce_fusion), channel_id=1, replica_groups=mesh['x'=4,'zl'=2,'yh'=2,'yl'=2,'zh'=2,'c'=2] {'x','zl'}, use_global_device_ids=true, to_apply=%region_1.2 | all-reduce | flops 32 | bytes 256 | tf_op jit(solution)/shard_map/psum | solution.py:417
  105.2 13.1 %collective-permute-done = bf16[256,2048]{1,0:T(8,128)(2,1)} collective-permute-done((bf16[256,2048]{1,0:T(8,128)(2,1)}, bf16[256,2048]{1,0:T(8,128)(2,1)}, u32[]{:S(2)}, u32[]{:S(2)}) %collective-permute-start) | collective-permute-done | bytes 1048608 | tf_op jit(solution)/shard_map/ppermute | solution.py:420
  119.0 34.2 %attend.1 = bf16[8,256,256]{2,1,0:T(8,128)(2,1)} custom-call(s32[34]{0:T(128)} %pad_add_fusion.1.refs_0_, bf16[8,1280,256]{2,1,0:T(8,128)(2,1)} %all-to-all-done.refs_1_.refs_2_, bf16[8,1280,256]{2,1,0:T(8,128)(2,1)} %all-to-all-done.refs_1_.refs_2_, bf16[8,1280,256]{2,1,0:T(8,128)(2,1)} %collective-permute-done.1.refs_3_), custom_call_target="tpu_custom_call" | custom-call | flops 8589934592 | bytes 12582912 | tf_op jit(solution)/shard_map/attend/pallas_call | solution.py:169
  157.6 16.1 %all-to-all-done.1 = bf16[8,256,256]{2,1,0:T(8,128)(2,1)} async-done(((bf16[8,256,256]{2,1,0:T(8,128)(2,1)}), bf16[8,256,256]{2,1,0:T(8,128)(2,1)}, u32[]{:S(2)}, u32[]{:S(2)}) %all-to-all-start.1) | async-done | bytes 1048608 | tf_op jit(solution)/shard_map/all_to_all | solution.py:425
  176.7 6.8 %all-to-all-start.2 = ((bf16[16,128,256]{2,1,0:T(8,128)(2,1)}), bf16[16,128,256]{2,1,0:T(8,128)(2,1)}, u32[]{:S(2)}, u32[]{:S(2)}) async-start(bf16[16,128,256]{2,1,0:T(8,128)(2,1)} %bitcast.9), calls=%async_computation.2 | async-start | bytes 2097152 | tf_op jit(solution)/shard_map/all_to_all | solution.py:428
  185.2 14.2 %all-to-all-done.2.attended_ref = bf16[16,128,256]{2,1,0:T(8,128)(2,1)} async-done(((bf16[16,128,256]{2,1,0:T(8,128)(2,1)}), bf16[16,128,256]{2,1,0:T(8,128)(2,1)}, u32[]{:S(2)}, u32[]{:S(2)}) %all-to-all-start.2) | async-done | bytes 1048608 | tf_op jit(solution)/shard_map/all_to_all | solution.py:428
  199.4 13.1 %mix.1 = (f32[128,2048]{1,0:T(8,128)}, bf16[128,2048]{1,0:T(8,128)(2,1)}, bf16[1024,2048]{1,0:T(8,128)(2,1)}) custom-call(s32[4]{0:T(128)} %pad_add_fusion.scalars, bf16[16,128,256]{2,1,0:T(8,128)(2,1)} %all-to-all-done.2.attended_ref, bf16[1024,2048]{1,0:T(8,128)(2,1)} %all-gather.5.cloned.1.call-done.w0, bf16[1024,2048]{1,0:T(8,128)(2,1)} %collective-permute-done.2.w1, ...), custom_call_target="tpu_custom_call" | custom-call | flops 3221225472 | bytes 25165824 | tf_op jit(solution)/shard_map/mix/pallas_call | solution.py:247
  212.5 6.6 %all-to-all-start.5 = ((bf16[128,8,2048]{2,1,0:T(8,128)(2,1)}), bf16[128,8,2048]{2,1,0:T(8,128)(2,1)}, u32[]{:S(2)}, u32[]{:S(2)}) async-start(bf16[128,8,2048]{2,1,0:T(8,128)(2,1)} %bitcast.72), calls=%async_computation.5 | async-start | bytes 8388608 | tf_op jit(solution)/shard_map/all_to_all | solution.py:437
  219.1 4.4 place.1
  223.6 50.8 %all-to-all-done.5 = bf16[128,8,2048]{2,1,0:T(8,128)(2,1)} async-done(((bf16[128,8,2048]{2,1,0:T(8,128)(2,1)}), bf16[128,8,2048]{2,1,0:T(8,128)(2,1)}, u32[]{:S(2)}, u32[]{:S(2)}) %all-to-all-start.5) | async-done | bytes 4194336 | tf_op jit(solution)/shard_map/all_to_all | solution.py:437
  274.4 5.1 %all-to-all-start.3 = ((bf16[128,8,2048]{2,1,0:T(8,128)(2,1)}), bf16[128,8,2048]{2,1,0:T(8,128)(2,1)}, u32[]{:S(2)}, u32[]{:S(2)}) async-start(bf16[128,8,2048]{2,1,0:T(8,128)(2,1)} %bitcast.70), calls=%async_computation.3 | async-start | bytes 8388608 | tf_op jit(solution)/shard_map/all_to_all | solution.py:437
  279.5 8.2 %fusion.2 = f32[1024,768]{1,0:T(8,128)} fusion(bf16[128,8,2048]{2,1,0:T(8,128)(2,1)} %all-to-all-done.5, bf16[1,2048,768]{2,1,0:T(8,128)(2,1)} %param.21), kind=kOutput, calls=%fused_computation.3 | convolution fusion | flops 3221225472 | bytes 10485760 | tf_op jit(solution)/shard_map/dot_general | solution.py:375
  287.7 12.3 %convert_bitcast_fusion = bf16[128,8,2048]{2,1,0:T(8,128)(2,1)} fusion(bf16[1,768,2048]{2,1,0:T(8,128)(2,1)S(1)} %copy-done, f32[1024,768]{1,0:T(8,128)} %fusion.2, bf16[1,2048,768]{2,1,0:T(8,128)(2,1)} %param.22, bf16[128,8,2048]{2,1,0:T(8,128)(2,1)} %all-to-all-done.5), kind=kOutput, calls=%fused_computation.9 | convolution fusion | flops 6449266688 | bytes 17825792 | tf_op jit(solution)/shard_map/dot_general | solution.py:378
  300.0 34.7 %all-to-all-done.3 = bf16[128,8,2048]{2,1,0:T(8,128)(2,1)} async-done(((bf16[128,8,2048]{2,1,0:T(8,128)(2,1)}), bf16[128,8,2048]{2,1,0:T(8,128)(2,1)}, u32[]{:S(2)}, u32[]{:S(2)}) %all-to-all-start.3) | async-done | bytes 4194336 | tf_op jit(solution)/shard_map/all_to_all | solution.py:437
  334.7 5.1 %all-to-all-start.6 = ((bf16[128,8,2048]{2,1,0:T(8,128)(2,1)}), bf16[128,8,2048]{2,1,0:T(8,128)(2,1)}, u32[]{:S(2)}, u32[]{:S(2)}) async-start(bf16[128,8,2048]{2,1,0:T(8,128)(2,1)} %convert_bitcast_fusion), calls=%async_computation.6 | async-start | bytes 8388608 | tf_op jit(solution)/shard_map/all_to_all | solution.py:437
  339.8 8.2 %fusion.6 = f32[1024,768]{1,0:T(8,128)} fusion(bf16[128,8,2048]{2,1,0:T(8,128)(2,1)} %all-to-all-done.3, bf16[1,2048,768]{2,1,0:T(8,128)(2,1)} %param.21), kind=kOutput, calls=%fused_computation.7 | convolution fusion | flops 3221225472 | bytes 10485760 | tf_op jit(solution)/shard_map/dot_general | solution.py:375
  348.0 12.3 %convert_bitcast_fusion.1 = bf16[128,8,2048]{2,1,0:T(8,128)(2,1)} fusion(bf16[1,768,2048]{2,1,0:T(8,128)(2,1)S(1)} %copy-done, f32[1024,768]{1,0:T(8,128)} %fusion.6, bf16[1,2048,768]{2,1,0:T(8,128)(2,1)} %param.22, bf16[128,8,2048]{2,1,0:T(8,128)(2,1)} %all-to-all-done.3), kind=kOutput, calls=%fused_computation.10 | convolution fusion | flops 6449266688 | bytes 17825792 | tf_op jit(solution)/shard_map/dot_general | solution.py:378
  360.3 34.7 %all-to-all-done.6 = bf16[128,8,2048]{2,1,0:T(8,128)(2,1)} async-done(((bf16[128,8,2048]{2,1,0:T(8,128)(2,1)}), bf16[128,8,2048]{2,1,0:T(8,128)(2,1)}, u32[]{:S(2)}, u32[]{:S(2)}) %all-to-all-start.6) | async-done | bytes 4194336 | tf_op jit(solution)/shard_map/all_to_all | solution.py:437
  394.9 5.1 %all-to-all-start.4 = ((bf16[128,8,2048]{2,1,0:T(8,128)(2,1)}), bf16[128,8,2048]{2,1,0:T(8,128)(2,1)}, u32[]{:S(2)}, u32[]{:S(2)}) async-start(bf16[128,8,2048]{2,1,0:T(8,128)(2,1)} %convert_bitcast_fusion.1), calls=%async_computation.4 | async-start | bytes 8388608 | tf_op jit(solution)/shard_map/all_to_all | solution.py:437
  400.8 6.4 %combine_first.1 = (f32[128,2048]{1,0:T(8,128)}, bf16[256,1024]{1,0:T(8,128)(2,1)}) custom-call(bf16[1024,2048]{1,0:T(8,128)(2,1)} %bitcast.25.returned_ref, s32[128,8]{1,0:T(8,128)} %copy-done.2, f32[128,8]{1,0:T(8,128)} %copy.55.route_ref, f32[128,2048]{1,0:T(8,128)} %get-tuple-element.26.base_ref), custom_call_target="tpu_custom_call" | custom-call | flops 1073741824 | bytes 6291456 | tf_op jit(solution)/shard_map/combine_first/pallas_call | solution.py:339
  407.1 48.1 %all-to-all-done.4 = bf16[128,8,2048]{2,1,0:T(8,128)(2,1)} async-done(((bf16[128,8,2048]{2,1,0:T(8,128)(2,1)}), bf16[128,8,2048]{2,1,0:T(8,128)(2,1)}, u32[]{:S(2)}, u32[]{:S(2)}) %all-to-all-start.4) | async-done | bytes 4194336 | tf_op jit(solution)/shard_map/all_to_all | solution.py:437
  455.2 5.0 %combine_last.1 = bf16[128,2048]{1,0:T(8,128)(2,1)} custom-call(bf16[1024,2048]{1,0:T(8,128)(2,1)} %bitcast.21.returned_ref, bf16[256,1024]{1,0:T(8,128)(2,1)} %get-tuple-element.27.shares_ref, f32[128,2048]{1,0:T(8,128)} %get-tuple-element.28.base_ref), custom_call_target="tpu_custom_call" | custom-call | flops 1073741824 | bytes 6291456 | tf_op jit(solution)/shard_map/combine_last/pallas_call | solution.py:361
  (57 shorter events, 19.2 us)
Async XLA Ops:
  6.5 281.2 %copy-start = (bf16[1,768,2048]{2,1,0:T(8,128)(2,1)S(1)}, bf16[1,768,2048]{2,1,0:T(8,128)(2,1)}, u32[]{:S(2)}) copy-start(bf16[1,768,2048]{2,1,0:T(8,128)(2,1)} %param.23) | copy-start | bytes 9437188
  6.5 2.2 dynamic-slice-start
  6.5 2.3 dynamic-slice-start.1
  11.8 82.2 %copy-start.4 = (s32[2048]{0:T(1024)S(1)}, s32[2048]{0:T(1024)}, u32[]{:S(2)}) copy-start(s32[2048]{0:T(1024)} %param.16) | copy-start | bytes 24580
  11.8 79.4 %all-to-all-start = ((bf16[8,1280,256]{2,1,0:T(8,128)(2,1)}), bf16[8,1280,256]{2,1,0:T(8,128)(2,1)}, u32[]{:S(2)}, u32[]{:S(2)}) async-start(bf16[8,1280,256]{2,1,0:T(8,128)(2,1)} %pad_maximum_fusion), calls=%async_computation | async-start | bytes 10485760 | tf_op jit(solution)/shard_map/all_to_all | solution.py:160
  17.6 139.9 %all-gather.5.cloned.1.call-start = ((), (), s32[]{:S(2)}) async-start(), calls=%async_computation.8 | async-start | bytes 5242880 | tf_op jit(solution)/shard_map/all_gather | solution.py:400
  18.3 155.4 %all-gather.3.cloned.1.call-start = ((), (), s32[]{:S(2)}) async-start(), calls=%async_computation.7 | async-start | bytes 5242880 | tf_op jit(solution)/shard_map/all_gather | solution.py:422
  91.2 27.1 %collective-permute-start.1 = (bf16[8,1280,256]{2,1,0:T(8,128)(2,1)}, bf16[8,1280,256]{2,1,0:T(8,128)(2,1)}, u32[]{:S(2)}, u32[]{:S(2)}) collective-permute-start(bf16[8,1280,256]{2,1,0:T(8,128)(2,1)} %all-to-all-done.refs_1_.refs_2_), channel_id=1, source_target_pairs={{0,1},{1,0},{2,3},{3,2},{4,5},{5,4},{6,7},{7,6},{8,9},{9,8},{10,11... | collective-permute-start | bytes 15728648 | tf_op jit(solution)/shard_map/ppermute | solution.py:161
  91.2 27.1 %collective-permute-start = (bf16[256,2048]{1,0:T(8,128)(2,1)}, bf16[256,2048]{1,0:T(8,128)(2,1)}, u32[]{:S(2)}, u32[]{:S(2)}) collective-permute-start(bf16[256,2048]{1,0:T(8,128)(2,1)} %param.17), channel_id=1, source_target_pairs={{0,18},{18,0},{2,16},{16,2},{1,19},{19,1},{3,17},{17,3},{4,22},{22... | collective-permute-start | bytes 3145736 | tf_op jit(solution)/shard_map/ppermute | solution.py:420
  119.0 54.7 %copy-start.3 = (s32[128,8]{0,1:T(8,128)S(1)}, s32[128,8]{0,1:T(8,128)}, u32[]{:S(2)}) copy-start(s32[128,8]{0,1:T(8,128)} %param.19) | copy-start | bytes 12292
  153.2 20.5 %all-to-all-start.1 = ((bf16[8,256,256]{2,1,0:T(8,128)(2,1)}), bf16[8,256,256]{2,1,0:T(8,128)(2,1)}, u32[]{:S(2)}, u32[]{:S(2)}) async-start(bf16[8,256,256]{2,1,0:T(8,128)(2,1)} %attend.1), calls=%async_computation.1 | async-start | bytes 2097152 | tf_op jit(solution)/shard_map/all_to_all | solution.py:425
  157.5 27.7 %collective-permute-start.2 = (bf16[1024,2048]{1,0:T(8,128)(2,1)}, bf16[1024,2048]{1,0:T(8,128)(2,1)}, u32[]{:S(2)}, u32[]{:S(2)}) collective-permute-start(bf16[1024,2048]{1,0:T(8,128)(2,1)} %all-gather.5.cloned.1.call-done.w0), channel_id=1, source_target_pairs={{0,1},{1,0},{2,3},{3,2},{4,5},{5,4},{6,7},{7,6},{8,9},{9,8},{10,11... | collective-permute-start | bytes 12582920 | tf_op jit(solution)/shard_map/ppermute | solution.py:401
  173.7 25.7 %collective-permute-start.3 = (bf16[1024,2048]{1,0:T(8,128)(2,1)}, bf16[1024,2048]{1,0:T(8,128)(2,1)}, u32[]{:S(2)}, u32[]{:S(2)}) collective-permute-start(bf16[1024,2048]{1,0:T(8,128)(2,1)} %all-gather.3.cloned.1.call-done.w2), channel_id=1, source_target_pairs={{0,1},{1,0},{2,3},{3,2},{4,5},{5,4},{6,7},{7,6},{8,9},{9,8},{10,11... | collective-permute-start | bytes 12582920 | tf_op jit(solution)/shard_map/ppermute | solution.py:427
  174.3 0.8 copy-start.1
  176.7 22.7 %all-to-all-start.2 = ((bf16[16,128,256]{2,1,0:T(8,128)(2,1)}), bf16[16,128,256]{2,1,0:T(8,128)(2,1)}, u32[]{:S(2)}, u32[]{:S(2)}) async-start(bf16[16,128,256]{2,1,0:T(8,128)(2,1)} %bitcast.9), calls=%async_computation.2 | async-start | bytes 2097152 | tf_op jit(solution)/shard_map/all_to_all | solution.py:428
  183.9 28.6 %copy-start.2 = (s32[128,8]{1,0:T(8,128)}, s32[128,8]{1,0:T(8,128)S(1)}, u32[]{:S(2)}) copy-start(s32[128,8]{1,0:T(8,128)S(1)} %fusion.34.slots_ref) | copy-start | bytes 12292
  212.5 61.9 %all-to-all-start.5 = ((bf16[128,8,2048]{2,1,0:T(8,128)(2,1)}), bf16[128,8,2048]{2,1,0:T(8,128)(2,1)}, u32[]{:S(2)}, u32[]{:S(2)}) async-start(bf16[128,8,2048]{2,1,0:T(8,128)(2,1)} %bitcast.72), calls=%async_computation.5 | async-start | bytes 8388608 | tf_op jit(solution)/shard_map/all_to_all | solution.py:437
  274.4 60.3 %all-to-all-start.3 = ((bf16[128,8,2048]{2,1,0:T(8,128)(2,1)}), bf16[128,8,2048]{2,1,0:T(8,128)(2,1)}, u32[]{:S(2)}, u32[]{:S(2)}) async-start(bf16[128,8,2048]{2,1,0:T(8,128)(2,1)} %bitcast.70), calls=%async_computation.3 | async-start | bytes 8388608 | tf_op jit(solution)/shard_map/all_to_all | solution.py:437
  334.7 60.3 %all-to-all-start.6 = ((bf16[128,8,2048]{2,1,0:T(8,128)(2,1)}), bf16[128,8,2048]{2,1,0:T(8,128)(2,1)}, u32[]{:S(2)}, u32[]{:S(2)}) async-start(bf16[128,8,2048]{2,1,0:T(8,128)(2,1)} %convert_bitcast_fusion), calls=%async_computation.6 | async-start | bytes 8388608 | tf_op jit(solution)/shard_map/all_to_all | solution.py:437
  360.3 39.8 %copy-start.5 = (f32[128,8]{0,1:T(8,128)S(1)}, f32[128,8]{0,1:T(8,128)}, u32[]{:S(2)}) copy-start(f32[128,8]{0,1:T(8,128)} %param.20) | copy-start | bytes 12292
  394.9 60.3 %all-to-all-start.4 = ((bf16[128,8,2048]{2,1,0:T(8,128)(2,1)}), bf16[128,8,2048]{2,1,0:T(8,128)(2,1)}, u32[]{:S(2)}, u32[]{:S(2)}) async-start(bf16[128,8,2048]{2,1,0:T(8,128)(2,1)} %convert_bitcast_fusion.1), calls=%async_computation.4 | async-start | bytes 8388608 | tf_op jit(solution)/shard_map/all_to_all | solution.py:437
Sparse Core Ops, SparseCore 0:
  20.1 49.9 all-gather.4
  118.5 47.7 all-gather.2

commit v6 on v5

--- a/solution.py
+++ b/solution.py
@@ -398,7 +398,6 @@
     columns = queries.shape[1]
     x, zl, yh, yl, zh, c = (lax.axis_index(name) for name in ALL)
     near = lax.all_gather(out_weight, ("yh", "yl"), axis=0, tiled=True)
-    near_other = lax.ppermute(near, "c", CORE_SWAP)
     order = jnp.stack(
         [zh * 2 + c, zh * 2 + 1 - c, (1 - zh) * 2 + c, (1 - zh) * 2 + 1 - c]
     ).astype(jnp.int32)
@@ -418,7 +417,8 @@
     mine, other = gather_keys(queries, key_rows, value_rows, yh * 2 + yl, c)
     late_weight, mine = lax.optimization_barrier((out_weight, mine))
     far = lax.ppermute(late_weight, ("zl", "zh"), Z_FLIP)
-    far, starts, other = lax.optimization_barrier((far, starts, other))
+    far, starts = lax.optimization_barrier((far, starts))
+    near_other = lax.ppermute(near, "c", CORE_SWAP)
     far = lax.all_gather(far, ("yh", "yl"), axis=0, tiled=True)
     scalars = jnp.concatenate([starts, jnp.stack([x * 2 + zl, c]).astype(jnp.int32)])
     attended = attend(scalars, mine, other, queries.shape[0])

time: 469 us -> 449 us (0.957)
  waiting for transfers between devices: 285 us -> 209 us
  blocking collectives: 11 us -> 76.5 us
    all_to_all x1 -> x0, waiting for transfers between devices: 72.9 us -> none  [gather_keys(): mine = lax.all_to_all(sent, CTX, split_axis=0, concat_axis=0, tiled=True)]
    all_to_all x0 -> x1, blocking collectives: none -> 66.4 us  [gather_keys(): mine = lax.all_to_all(sent, CTX, split_axis=0, concat_axis=0, tiled=True)]
    all_to_all x1 -> x0, starting transfers between devices: 5.79 us -> none  [gather_keys(): mine = lax.all_to_all(sent, CTX, split_axis=0, concat_axis=0, tiled=True)]
  transfers between devices with their start and end apart: 13 -> 12, of which waited for: 8 -> 7; matrix products, arithmetic and copies ran while one was open for 10% -> 11% of each run, Pallas kernels for 10% -> 9%
where the time goes in v6:
time: 449 us; the launch traced here: 447 us
  waiting for transfers between devices  209 us (47%)
  blocking collectives  76.5 us (17%)
  Pallas kernels  60 us (13%)
  matrix products  40.9 us (9%)
  starting transfers between devices  38.1 us (8%)
  between operations  13.6 us (3%)
  local copies, waits for them, and re-layouts  4.89 us (1%)
    all_to_all x4, waiting for transfers between devices, exchange(): lax.all_to_all(rows.reshape(128, half, width), ALL, split_axis=0, concat_...  168 us
    all_to_all x1, blocking collectives, gather_keys(): mine = lax.all_to_all(sent, CTX, split_axis=0, concat_axis=0, tiled=True)  66.4 us
    pallas_call x1, Pallas kernels, attend(): pl.pallas_call(lambda *refs: attend_kernel(block, *refs), out_shape=jax.S...  31.2 us
    dot_general x2, matrix products, expert_rows(): jnp.dot(hidden, down_weight[0], preferred_element_type=jnp.float32)  24.6 us
    all_to_all x4, starting transfers between devices, exchange(): lax.all_to_all(rows.reshape(128, half, width), ALL, split_axis=0, concat_...  21.9 us
    dot_general x2, matrix products, expert_rows(): jnp.dot(flat_rows, gate_weight[0], preferred_element_type=jnp.float32)  16.4 us
    all_to_all x1, waiting for transfers between devices, shards(): lax.all_to_all(attended.reshape(16, TILE, columns), OWNER, split_axis=0,...  14.2 us
    all_to_all x1, waiting for transfers between devices, shards(): lax.all_to_all(attended, CTX, split_axis=0, concat_axis=0, tiled=True)  13.7 us
  transfers between devices with their start and end apart: 12, of which 7 were waited for; matrix products, arithmetic and copies ran while one was open for 11% of the time, Pallas kernels for 9%

profile of v6, /device:TPU:8, one launch (start us, length us, event | category | flops | bytes accessed | tf_op | source)
XLA Modules:
  0.0 446.7 jit_solution(11516214578206435297)
XLA Ops:
  9.7 66.4 %all_to_all.35.refs_1_.refs_2_ = bf16[8,1280,256]{2,1,0:T(8,128)(2,1)} all-to-all(bf16[8,1280,256]{2,1,0:T(8,128)(2,1)S(1)} %pad_maximum_fusion), channel_id=1, replica_groups=mesh['x'=4,'zl'=2,'yh'=2,'yl'=2,'zh'=2,'c'=2] {'x','zl'}, dimensions={0} | all-to-all | bytes 10485760 | tf_op jit(solution)/shard_map/all_to_all | solution.py:160
  79.8 10.1 %psum.7 = s32[32]{0:T(128)S(1)} all-reduce(s32[32]{0:T(128)S(1)} %convert_reduce_fusion), channel_id=1, replica_groups=mesh['x'=4,'zl'=2,'yh'=2,'yl'=2,'zh'=2,'c'=2] {'x','zl'}, use_global_device_ids=true, to_apply=%region_1.2 | all-reduce | flops 32 | bytes 256 | tf_op jit(solution)/shard_map/psum | solution.py:416
  89.9 12.1 %collective-permute-done = bf16[256,2048]{1,0:T(8,128)(2,1)} collective-permute-done((bf16[256,2048]{1,0:T(8,128)(2,1)}, bf16[256,2048]{1,0:T(8,128)(2,1)}, u32[]{:S(2)}, u32[]{:S(2)}) %collective-permute-start) | collective-permute-done | bytes 1048608 | tf_op jit(solution)/shard_map/ppermute | solution.py:419
  102.6 31.2 %attend.1 = bf16[8,256,256]{2,1,0:T(8,128)(2,1)} custom-call(s32[34]{0:T(128)} %pad_add_fusion.1.refs_0_, bf16[8,1280,256]{2,1,0:T(8,128)(2,1)} %all_to_all.35.refs_1_.refs_2_, bf16[8,1280,256]{2,1,0:T(8,128)(2,1)} %all_to_all.35.refs_1_.refs_2_, bf16[8,1280,256]{2,1,0:T(8,128)(2,1)} %collective-permute-done.1.refs_3_), custom_call_target="tpu_custom_call" | custom-call | flops 8589934592 | bytes 12582912 | tf_op jit(solution)/shard_map/attend/pallas_call | solution.py:169
  133.8 6.0 %all-to-all-start.1 = ((bf16[8,256,256]{2,1,0:T(8,128)(2,1)}), bf16[8,256,256]{2,1,0:T(8,128)(2,1)}, u32[]{:S(2)}, u32[]{:S(2)}) async-start(bf16[8,256,256]{2,1,0:T(8,128)(2,1)} %attend.1), calls=%async_computation.1 | async-start | bytes 2097152 | tf_op jit(solution)/shard_map/all_to_all | solution.py:425
  139.9 13.7 %all-to-all-done.1 = bf16[8,256,256]{2,1,0:T(8,128)(2,1)} async-done(((bf16[8,256,256]{2,1,0:T(8,128)(2,1)}), bf16[8,256,256]{2,1,0:T(8,128)(2,1)}, u32[]{:S(2)}, u32[]{:S(2)}) %all-to-all-start.1) | async-done | bytes 1048608 | tf_op jit(solution)/shard_map/all_to_all | solution.py:425
  156.7 6.5 %all-to-all-start.2 = ((bf16[16,128,256]{2,1,0:T(8,128)(2,1)}), bf16[16,128,256]{2,1,0:T(8,128)(2,1)}, u32[]{:S(2)}, u32[]{:S(2)}) async-start(bf16[16,128,256]{2,1,0:T(8,128)(2,1)} %bitcast.9), calls=%async_computation.2 | async-start | bytes 2097152 | tf_op jit(solution)/shard_map/all_to_all | solution.py:428
  164.8 14.2 %all-to-all-done.2.attended_ref = bf16[16,128,256]{2,1,0:T(8,128)(2,1)} async-done(((bf16[16,128,256]{2,1,0:T(8,128)(2,1)}), bf16[16,128,256]{2,1,0:T(8,128)(2,1)}, u32[]{:S(2)}, u32[]{:S(2)}) %all-to-all-start.2) | async-done | bytes 1048608 | tf_op jit(solution)/shard_map/all_to_all | solution.py:428
  179.0 13.1 %mix.1 = (f32[128,2048]{1,0:T(8,128)}, bf16[128,2048]{1,0:T(8,128)(2,1)}, bf16[1024,2048]{1,0:T(8,128)(2,1)}) custom-call(s32[4]{0:T(128)} %pad_add_fusion.scalars, bf16[16,128,256]{2,1,0:T(8,128)(2,1)} %all-to-all-done.2.attended_ref, bf16[1024,2048]{1,0:T(8,128)(2,1)} %all-gather.5.cloned.1.call-done.w0, bf16[1024,2048]{1,0:T(8,128)(2,1)} %collective-permute-done.2.w1, ...), custom_call_target="tpu_custom_call" | custom-call | flops 3221225472 | bytes 25165824 | tf_op jit(solution)/shard_map/mix/pallas_call | solution.py:247
  192.1 6.7 %all-to-all-start.5 = ((bf16[128,8,2048]{2,1,0:T(8,128)(2,1)}), bf16[128,8,2048]{2,1,0:T(8,128)(2,1)}, u32[]{:S(2)}, u32[]{:S(2)}) async-start(bf16[128,8,2048]{2,1,0:T(8,128)(2,1)} %bitcast.72), calls=%async_computation.5 | async-start | bytes 8388608 | tf_op jit(solution)/shard_map/all_to_all | solution.py:437
  198.7 4.5 place.1
  203.2 50.8 %all-to-all-done.5 = bf16[128,8,2048]{2,1,0:T(8,128)(2,1)} async-done(((bf16[128,8,2048]{2,1,0:T(8,128)(2,1)}), bf16[128,8,2048]{2,1,0:T(8,128)(2,1)}, u32[]{:S(2)}, u32[]{:S(2)}) %all-to-all-start.5) | async-done | bytes 4194336 | tf_op jit(solution)/shard_map/all_to_all | solution.py:437
  254.0 5.1 %all-to-all-start.3 = ((bf16[128,8,2048]{2,1,0:T(8,128)(2,1)}), bf16[128,8,2048]{2,1,0:T(8,128)(2,1)}, u32[]{:S(2)}, u32[]{:S(2)}) async-start(bf16[128,8,2048]{2,1,0:T(8,128)(2,1)} %bitcast.70), calls=%async_computation.3 | async-start | bytes 8388608 | tf_op jit(solution)/shard_map/all_to_all | solution.py:437
  259.1 8.2 %fusion.2 = f32[1024,768]{1,0:T(8,128)} fusion(bf16[128,8,2048]{2,1,0:T(8,128)(2,1)} %all-to-all-done.5, bf16[1,2048,768]{2,1,0:T(8,128)(2,1)} %param.21), kind=kOutput, calls=%fused_computation.3 | convolution fusion | flops 3221225472 | bytes 10485760 | tf_op jit(solution)/shard_map/dot_general | solution.py:375
  267.3 12.3 %convert_bitcast_fusion = bf16[128,8,2048]{2,1,0:T(8,128)(2,1)} fusion(bf16[1,768,2048]{2,1,0:T(8,128)(2,1)S(1)} %copy-done, f32[1024,768]{1,0:T(8,128)} %fusion.2, bf16[1,2048,768]{2,1,0:T(8,128)(2,1)} %param.22, bf16[128,8,2048]{2,1,0:T(8,128)(2,1)} %all-to-all-done.5), kind=kOutput, calls=%fused_computation.9 | convolution fusion | flops 6449266688 | bytes 17825792 | tf_op jit(solution)/shard_map/dot_general | solution.py:378
  279.6 34.7 %all-to-all-done.3 = bf16[128,8,2048]{2,1,0:T(8,128)(2,1)} async-done(((bf16[128,8,2048]{2,1,0:T(8,128)(2,1)}), bf16[128,8,2048]{2,1,0:T(8,128)(2,1)}, u32[]{:S(2)}, u32[]{:S(2)}) %all-to-all-start.3) | async-done | bytes 4194336 | tf_op jit(solution)/shard_map/all_to_all | solution.py:437
  314.3 5.1 %all-to-all-start.6 = ((bf16[128,8,2048]{2,1,0:T(8,128)(2,1)}), bf16[128,8,2048]{2,1,0:T(8,128)(2,1)}, u32[]{:S(2)}, u32[]{:S(2)}) async-start(bf16[128,8,2048]{2,1,0:T(8,128)(2,1)} %convert_bitcast_fusion), calls=%async_computation.6 | async-start | bytes 8388608 | tf_op jit(solution)/shard_map/all_to_all | solution.py:437
  319.4 8.2 %fusion.6 = f32[1024,768]{1,0:T(8,128)} fusion(bf16[128,8,2048]{2,1,0:T(8,128)(2,1)} %all-to-all-done.3, bf16[1,2048,768]{2,1,0:T(8,128)(2,1)} %param.21), kind=kOutput, calls=%fused_computation.7 | convolution fusion | flops 3221225472 | bytes 10485760 | tf_op jit(solution)/shard_map/dot_general | solution.py:375
  327.6 12.3 %convert_bitcast_fusion.1 = bf16[128,8,2048]{2,1,0:T(8,128)(2,1)} fusion(bf16[1,768,2048]{2,1,0:T(8,128)(2,1)S(1)} %copy-done, f32[1024,768]{1,0:T(8,128)} %fusion.6, bf16[1,2048,768]{2,1,0:T(8,128)(2,1)} %param.22, bf16[128,8,2048]{2,1,0:T(8,128)(2,1)} %all-to-all-done.3), kind=kOutput, calls=%fused_computation.10 | convolution fusion | flops 6449266688 | bytes 17825792 | tf_op jit(solution)/shard_map/dot_general | solution.py:378
  339.9 34.7 %all-to-all-done.6 = bf16[128,8,2048]{2,1,0:T(8,128)(2,1)} async-done(((bf16[128,8,2048]{2,1,0:T(8,128)(2,1)}), bf16[128,8,2048]{2,1,0:T(8,128)(2,1)}, u32[]{:S(2)}, u32[]{:S(2)}) %all-to-all-start.6) | async-done | bytes 4194336 | tf_op jit(solution)/shard_map/all_to_all | solution.py:437
  374.6 5.1 %all-to-all-start.4 = ((bf16[128,8,2048]{2,1,0:T(8,128)(2,1)}), bf16[128,8,2048]{2,1,0:T(8,128)(2,1)}, u32[]{:S(2)}, u32[]{:S(2)}) async-start(bf16[128,8,2048]{2,1,0:T(8,128)(2,1)} %convert_bitcast_fusion.1), calls=%async_computation.4 | async-start | bytes 8388608 | tf_op jit(solution)/shard_map/all_to_all | solution.py:437
  380.4 6.3 %combine_first.1 = (f32[128,2048]{1,0:T(8,128)}, bf16[256,1024]{1,0:T(8,128)(2,1)}) custom-call(bf16[1024,2048]{1,0:T(8,128)(2,1)} %bitcast.25.returned_ref, s32[128,8]{1,0:T(8,128)} %copy-done.2, f32[128,8]{1,0:T(8,128)} %copy.55.route_ref, f32[128,2048]{1,0:T(8,128)} %get-tuple-element.24.base_ref), custom_call_target="tpu_custom_call" | custom-call | flops 1073741824 | bytes 6291456 | tf_op jit(solution)/shard_map/combine_first/pallas_call | solution.py:339
  386.7 48.1 %all-to-all-done.4 = bf16[128,8,2048]{2,1,0:T(8,128)(2,1)} async-done(((bf16[128,8,2048]{2,1,0:T(8,128)(2,1)}), bf16[128,8,2048]{2,1,0:T(8,128)(2,1)}, u32[]{:S(2)}, u32[]{:S(2)}) %all-to-all-start.4) | async-done | bytes 4194336 | tf_op jit(solution)/shard_map/all_to_all | solution.py:437
  434.8 5.0 %combine_last.1 = bf16[128,2048]{1,0:T(8,128)(2,1)} custom-call(bf16[1024,2048]{1,0:T(8,128)(2,1)} %bitcast.21.returned_ref, bf16[256,1024]{1,0:T(8,128)(2,1)} %get-tuple-element.25.shares_ref, f32[128,2048]{1,0:T(8,128)} %get-tuple-element.26.base_ref), custom_call_target="tpu_custom_call" | custom-call | flops 1073741824 | bytes 6291456 | tf_op jit(solution)/shard_map/combine_last/pallas_call | solution.py:361
  (56 shorter events, 12.9 us)
Async XLA Ops:
  6.5 260.8 %copy-start = (bf16[1,768,2048]{2,1,0:T(8,128)(2,1)S(1)}, bf16[1,768,2048]{2,1,0:T(8,128)(2,1)}, u32[]{:S(2)}) copy-start(bf16[1,768,2048]{2,1,0:T(8,128)(2,1)} %param.23) | copy-start | bytes 9437188
  6.5 133.3 %all-gather.5.cloned.1.call-start = ((), (), s32[]{:S(2)}) async-start(), calls=%async_computation.8 | async-start | bytes 5242880 | tf_op jit(solution)/shard_map/all_gather | solution.py:400
  7.3 146.4 %all-gather.3.cloned.1.call-start = ((), (), s32[]{:S(2)}) async-start(), calls=%async_computation.7 | async-start | bytes 5242880 | tf_op jit(solution)/shard_map/all_gather | solution.py:422
  7.3 1.6 dynamic-slice-start
  7.3 1.7 dynamic-slice-start.1
  9.7 70.0 %copy-start.4 = (s32[2048]{0:T(1024)S(1)}, s32[2048]{0:T(1024)}, u32[]{:S(2)}) copy-start(s32[2048]{0:T(1024)} %param.16) | copy-start | bytes 24580
  76.1 25.9 %collective-permute-start = (bf16[256,2048]{1,0:T(8,128)(2,1)}, bf16[256,2048]{1,0:T(8,128)(2,1)}, u32[]{:S(2)}, u32[]{:S(2)}) collective-permute-start(bf16[256,2048]{1,0:T(8,128)(2,1)} %param.17), channel_id=1, source_target_pairs={{0,18},{18,0},{2,16},{16,2},{1,19},{19,1},{3,17},{17,3},{4,22},{22... | collective-permute-start | bytes 3145736 | tf_op jit(solution)/shard_map/ppermute | solution.py:419
  79.7 22.9 %collective-permute-start.1 = (bf16[8,1280,256]{2,1,0:T(8,128)(2,1)}, bf16[8,1280,256]{2,1,0:T(8,128)(2,1)}, u32[]{:S(2)}, u32[]{:S(2)}) collective-permute-start(bf16[8,1280,256]{2,1,0:T(8,128)(2,1)} %all_to_all.35.refs_1_.refs_2_), channel_id=1, source_target_pairs={{0,1},{1,0},{2,3},{3,2},{4,5},{5,4},{6,7},{7,6},{8,9},{9,8},{10,11... | collective-permute-start | bytes 15728648 | tf_op jit(solution)/shard_map/ppermute | solution.py:161
  102.6 51.1 %copy-start.3 = (s32[128,8]{0,1:T(8,128)S(1)}, s32[128,8]{0,1:T(8,128)}, u32[]{:S(2)}) copy-start(s32[128,8]{0,1:T(8,128)} %param.19) | copy-start | bytes 12292
  133.8 19.9 %all-to-all-start.1 = ((bf16[8,256,256]{2,1,0:T(8,128)(2,1)}), bf16[8,256,256]{2,1,0:T(8,128)(2,1)}, u32[]{:S(2)}, u32[]{:S(2)}) async-start(bf16[8,256,256]{2,1,0:T(8,128)(2,1)} %attend.1), calls=%async_computation.1 | async-start | bytes 2097152 | tf_op jit(solution)/shard_map/all_to_all | solution.py:425
  139.8 25.0 %collective-permute-start.2 = (bf16[1024,2048]{1,0:T(8,128)(2,1)}, bf16[1024,2048]{1,0:T(8,128)(2,1)}, u32[]{:S(2)}, u32[]{:S(2)}) collective-permute-start(bf16[1024,2048]{1,0:T(8,128)(2,1)} %all-gather.5.cloned.1.call-done.w0), channel_id=1, source_target_pairs={{0,1},{1,0},{2,3},{3,2},{4,5},{5,4},{6,7},{7,6},{8,9},{9,8},{10,11... | collective-permute-start | bytes 12582920 | tf_op jit(solution)/shard_map/ppermute | solution.py:421
  153.7 25.3 %collective-permute-start.3 = (bf16[1024,2048]{1,0:T(8,128)(2,1)}, bf16[1024,2048]{1,0:T(8,128)(2,1)}, u32[]{:S(2)}, u32[]{:S(2)}) collective-permute-start(bf16[1024,2048]{1,0:T(8,128)(2,1)} %all-gather.3.cloned.1.call-done.w2), channel_id=1, source_target_pairs={{0,1},{1,0},{2,3},{3,2},{4,5},{5,4},{6,7},{7,6},{8,9},{9,8},{10,11... | collective-permute-start | bytes 12582920 | tf_op jit(solution)/shard_map/ppermute | solution.py:427
  154.3 0.8 copy-start.1
  156.7 22.3 %all-to-all-start.2 = ((bf16[16,128,256]{2,1,0:T(8,128)(2,1)}), bf16[16,128,256]{2,1,0:T(8,128)(2,1)}, u32[]{:S(2)}, u32[]{:S(2)}) async-start(bf16[16,128,256]{2,1,0:T(8,128)(2,1)} %bitcast.9), calls=%async_computation.2 | async-start | bytes 2097152 | tf_op jit(solution)/shard_map/all_to_all | solution.py:428
  163.5 28.6 %copy-start.2 = (s32[128,8]{1,0:T(8,128)}, s32[128,8]{1,0:T(8,128)S(1)}, u32[]{:S(2)}) copy-start(s32[128,8]{1,0:T(8,128)S(1)} %fusion.34.slots_ref) | copy-start | bytes 12292
  192.1 61.9 %all-to-all-start.5 = ((bf16[128,8,2048]{2,1,0:T(8,128)(2,1)}), bf16[128,8,2048]{2,1,0:T(8,128)(2,1)}, u32[]{:S(2)}, u32[]{:S(2)}) async-start(bf16[128,8,2048]{2,1,0:T(8,128)(2,1)} %bitcast.72), calls=%async_computation.5 | async-start | bytes 8388608 | tf_op jit(solution)/shard_map/all_to_all | solution.py:437
  254.0 60.3 %all-to-all-start.3 = ((bf16[128,8,2048]{2,1,0:T(8,128)(2,1)}), bf16[128,8,2048]{2,1,0:T(8,128)(2,1)}, u32[]{:S(2)}, u32[]{:S(2)}) async-start(bf16[128,8,2048]{2,1,0:T(8,128)(2,1)} %bitcast.70), calls=%async_computation.3 | async-start | bytes 8388608 | tf_op jit(solution)/shard_map/all_to_all | solution.py:437
  314.3 60.3 %all-to-all-start.6 = ((bf16[128,8,2048]{2,1,0:T(8,128)(2,1)}), bf16[128,8,2048]{2,1,0:T(8,128)(2,1)}, u32[]{:S(2)}, u32[]{:S(2)}) async-start(bf16[128,8,2048]{2,1,0:T(8,128)(2,1)} %convert_bitcast_fusion), calls=%async_computation.6 | async-start | bytes 8388608 | tf_op jit(solution)/shard_map/all_to_all | solution.py:437
  339.9 39.8 %copy-start.5 = (f32[128,8]{0,1:T(8,128)S(1)}, f32[128,8]{0,1:T(8,128)}, u32[]{:S(2)}) copy-start(f32[128,8]{0,1:T(8,128)} %param.20) | copy-start | bytes 12292
  374.6 60.3 %all-to-all-start.4 = ((bf16[128,8,2048]{2,1,0:T(8,128)(2,1)}), bf16[128,8,2048]{2,1,0:T(8,128)(2,1)}, u32[]{:S(2)}, u32[]{:S(2)}) async-start(bf16[128,8,2048]{2,1,0:T(8,128)(2,1)} %convert_bitcast_fusion.1), calls=%async_computation.4 | async-start | bytes 8388608 | tf_op jit(solution)/shard_map/all_to_all | solution.py:437
Sparse Core Ops, SparseCore 0:
  9.0 49.9 all-gather.4
  102.1 46.9 all-gather.2

commit v7 on v6

--- a/solution.py
+++ b/solution.py
@@ -26,8 +26,8 @@
 CORE_SWAP = [(0, 1), (1, 0)]
 Z_FLIP = [(0, 3), (3, 0), (1, 2), (2, 1)]
 CAPACITY = 16
-SLOT_TILE = 256
-WIDTH_TILE = 512
+SLOT_TILE = 512
+WIDTH_TILE = 1024
 VMEM_LIMIT = 60 << 20
 
 
@@ -185,7 +185,7 @@
         ),
         compiler_params=pltpu.CompilerParams(vmem_limit_bytes=VMEM_LIMIT),
         cost_estimate=pl.CostEstimate(
-            flops=8 << 30, bytes_accessed=12 << 20, transcendentals=16 << 20
+            flops=20 << 30, bytes_accessed=12 << 20, transcendentals=16 << 20
         ),
         name="attend",
     )(scalars, mine, mine, other)
@@ -215,8 +215,13 @@
             columns = slice(n * WIDTH_TILE, (n + 1) * WIDTH_TILE)
             total = residual_ref[:, columns].astype(jnp.float32)
             for p, w_ref in enumerate((w0, w1, w2, w3)):
+                halves = [slice(None)] if p < 2 else [slice(0, 128), slice(128, 256)]
                 rows = jnp.concatenate(
-                    [attended_ref[k % 2 * 8 + scalars[p] * 2 + k // 2] for k in range(4)],
+                    [
+                        attended_ref[k % 2 * 8 + scalars[p] * 2 + k // 2, :, part]
+                        for part in halves
+                        for k in range(4)
+                    ],
                     axis=1,
                 )
                 total += jnp.dot(rows, w_ref[...], preferred_element_type=jnp.float32)
@@ -415,11 +420,13 @@
     )
     starts = lax.psum(counts, CTX)
     mine, other = gather_keys(queries, key_rows, value_rows, yh * 2 + yl, c)
-    late_weight, mine = lax.optimization_barrier((out_weight, mine))
-    far = lax.ppermute(late_weight, ("zl", "zh"), Z_FLIP)
+    rows = out_weight.shape[0] // 2
+    sent = lax.dynamic_slice_in_dim(out_weight, (1 - zl) * rows, rows, 0)
+    sent, mine = lax.optimization_barrier((sent, mine))
+    far = lax.ppermute(sent, ("zl", "zh"), Z_FLIP)
     far, starts = lax.optimization_barrier((far, starts))
     near_other = lax.ppermute(near, "c", CORE_SWAP)
-    far = lax.all_gather(far, ("yh", "yl"), axis=0, tiled=True)
+    far = lax.all_gather(far, ("zl", "yh", "yl"), axis=0, tiled=True)
     scalars = jnp.concatenate([starts, jnp.stack([x * 2 + zl, c]).astype(jnp.int32)])
     attended = attend(scalars, mine, other, queries.shape[0])
     attended = lax.all_to_all(attended, CTX, split_axis=0, concat_axis=0, tiled=True)

time: 449 us -> 449 us (level)
  starting transfers between devices: 38.1 us -> 45.8 us
  waiting for transfers between devices: 209 us -> 203 us
    ppermute x1, waiting for transfers between devices: 12.1 us -> 2.68 us  [shards(): far = lax.ppermute(sent, ('zl', 'zh'), Z_FLIP)]
    all_to_all x1, starting transfers between devices: 6.46 us -> 13.2 us  [shards(): lax.all_to_all(attended.reshape(16, TILE, columns), OWNER, split_axis=0,...]
where the time goes in v7:
time: 449 us; the launch traced here: 448 us
  waiting for transfers between devices  203 us (45%)
  blocking collectives  76.5 us (17%)
  Pallas kernels  57.5 us (13%)
  starting transfers between devices  45.8 us (10%)
  matrix products  41 us (9%)
  between operations  13.6 us (3%)
  local copies, waits for them, and re-layouts  6.76 us (2%)
    all_to_all x4, waiting for transfers between devices, exchange(): lax.all_to_all(rows.reshape(128, half, width), ALL, split_axis=0, concat_...  170 us
    all_to_all x1, blocking collectives, gather_keys(): mine = lax.all_to_all(sent, CTX, split_axis=0, concat_axis=0, tiled=True)  66.4 us
    pallas_call x1, Pallas kernels, attend(): pl.pallas_call(lambda *refs: attend_kernel(block, *refs), out_shape=jax.S...  31.5 us
    dot_general x2, matrix products, expert_rows(): jnp.dot(hidden, down_weight[0], preferred_element_type=jnp.float32)  24.5 us
    all_to_all x4, starting transfers between devices, exchange(): lax.all_to_all(rows.reshape(128, half, width), ALL, split_axis=0, concat_...  22.6 us
    dot_general x2, matrix products, expert_rows(): jnp.dot(flat_rows, gate_weight[0], preferred_element_type=jnp.float32)  16.4 us
    all_to_all x1, waiting for transfers between devices, shards(): lax.all_to_all(attended, CTX, split_axis=0, concat_axis=0, tiled=True)  16 us
    all_to_all x1, waiting for transfers between devices, shards(): lax.all_to_all(attended.reshape(16, TILE, columns), OWNER, split_axis=0,...  14.2 us
  transfers between devices with their start and end apart: 12, of which 7 were waited for; matrix products, arithmetic and copies ran while one was open for 11% of the time, Pallas kernels for 9%

profile of v7, /device:TPU:8, one launch (start us, length us, event | category | flops | bytes accessed | tf_op | source)
XLA Modules:
  0.0 448.1 jit_solution(15234871937688315575)
XLA Ops:
  9.7 66.4 %all_to_all.35.refs_1_.refs_2_ = bf16[8,1280,256]{2,1,0:T(8,128)(2,1)} all-to-all(bf16[8,1280,256]{2,1,0:T(8,128)(2,1)S(1)} %pad_maximum_fusion), channel_id=1, replica_groups=mesh['x'=4,'zl'=2,'yh'=2,'yl'=2,'zh'=2,'c'=2] {'x','zl'}, dimensions={0} | all-to-all | bytes 10485760 | tf_op jit(solution)/shard_map/all_to_all | solution.py:160
  78.0 3.6 collective-permute-start
  81.7 10.1 %psum.7 = s32[32]{0:T(128)S(1)} all-reduce(s32[32]{0:T(128)S(1)} %convert_reduce_fusion), channel_id=1, replica_groups=mesh['x'=4,'zl'=2,'yh'=2,'yl'=2,'zh'=2,'c'=2] {'x','zl'}, use_global_device_ids=true, to_apply=%region_1.2 | all-reduce | flops 32 | bytes 256 | tf_op jit(solution)/shard_map/psum | solution.py:421
  95.2 31.5 %attend.1 = bf16[8,256,256]{2,1,0:T(8,128)(2,1)} custom-call(s32[34]{0:T(128)} %pad_add_fusion.1.refs_0_, bf16[8,1280,256]{2,1,0:T(8,128)(2,1)} %all_to_all.35.refs_1_.refs_2_, bf16[8,1280,256]{2,1,0:T(8,128)(2,1)} %all_to_all.35.refs_1_.refs_2_, bf16[8,1280,256]{2,1,0:T(8,128)(2,1)} %collective-permute-done.1.refs_3_), custom_call_target="tpu_custom_call" | custom-call | flops 21474836480 | bytes 12582912 | tf_op jit(solution)/shard_map/attend/pallas_call | solution.py:169
  126.7 6.3 %all-to-all-start.1 = ((bf16[8,256,256]{2,1,0:T(8,128)(2,1)}), bf16[8,256,256]{2,1,0:T(8,128)(2,1)}, u32[]{:S(2)}, u32[]{:S(2)}) async-start(bf16[8,256,256]{2,1,0:T(8,128)(2,1)} %attend.1), calls=%async_computation.1 | async-start | bytes 2097152 | tf_op jit(solution)/shard_map/all_to_all | solution.py:432
  133.1 16.0 %all-to-all-done.1 = bf16[8,256,256]{2,1,0:T(8,128)(2,1)} async-done(((bf16[8,256,256]{2,1,0:T(8,128)(2,1)}), bf16[8,256,256]{2,1,0:T(8,128)(2,1)}, u32[]{:S(2)}, u32[]{:S(2)}) %all-to-all-start.1) | async-done | bytes 1048608 | tf_op jit(solution)/shard_map/all_to_all | solution.py:432
  152.1 13.2 %all-to-all-start.2 = ((bf16[16,128,256]{2,1,0:T(8,128)(2,1)}), bf16[16,128,256]{2,1,0:T(8,128)(2,1)}, u32[]{:S(2)}, u32[]{:S(2)}) async-start(bf16[16,128,256]{2,1,0:T(8,128)(2,1)} %bitcast.9), calls=%async_computation.2 | async-start | bytes 2097152 | tf_op jit(solution)/shard_map/all_to_all | solution.py:435
  166.9 14.2 %all-to-all-done.2.attended_ref = bf16[16,128,256]{2,1,0:T(8,128)(2,1)} async-done(((bf16[16,128,256]{2,1,0:T(8,128)(2,1)}), bf16[16,128,256]{2,1,0:T(8,128)(2,1)}, u32[]{:S(2)}, u32[]{:S(2)}) %all-to-all-start.2) | async-done | bytes 1048608 | tf_op jit(solution)/shard_map/all_to_all | solution.py:435
  181.2 12.0 %mix.1 = (f32[128,2048]{1,0:T(8,128)}, bf16[128,2048]{1,0:T(8,128)(2,1)}, bf16[1024,2048]{1,0:T(8,128)(2,1)}) custom-call(s32[4]{0:T(128)} %pad_add_fusion.scalars, bf16[16,128,256]{2,1,0:T(8,128)(2,1)} %all-to-all-done.2.attended_ref, bf16[1024,2048]{1,0:T(8,128)(2,1)} %all-gather.5.cloned.1.call-done.w0, bf16[1024,2048]{1,0:T(8,128)(2,1)} %collective-permute-done.2.w1, ...), custom_call_target="tpu_custom_call" | custom-call | flops 3221225472 | bytes 25165824 | tf_op jit(solution)/shard_map/mix/pallas_call | solution.py:252
  193.2 7.4 %all-to-all-start.5 = ((bf16[128,8,2048]{2,1,0:T(8,128)(2,1)}), bf16[128,8,2048]{2,1,0:T(8,128)(2,1)}, u32[]{:S(2)}, u32[]{:S(2)}) async-start(bf16[128,8,2048]{2,1,0:T(8,128)(2,1)} %bitcast.72), calls=%async_computation.5 | async-start | bytes 8388608 | tf_op jit(solution)/shard_map/all_to_all | solution.py:444
  200.6 4.0 place.1
  204.5 51.2 %all-to-all-done.5 = bf16[128,8,2048]{2,1,0:T(8,128)(2,1)} async-done(((bf16[128,8,2048]{2,1,0:T(8,128)(2,1)}), bf16[128,8,2048]{2,1,0:T(8,128)(2,1)}, u32[]{:S(2)}, u32[]{:S(2)}) %all-to-all-start.5) | async-done | bytes 4194336 | tf_op jit(solution)/shard_map/all_to_all | solution.py:444
  255.8 5.1 %all-to-all-start.3 = ((bf16[128,8,2048]{2,1,0:T(8,128)(2,1)}), bf16[128,8,2048]{2,1,0:T(8,128)(2,1)}, u32[]{:S(2)}, u32[]{:S(2)}) async-start(bf16[128,8,2048]{2,1,0:T(8,128)(2,1)} %bitcast.70), calls=%async_computation.3 | async-start | bytes 8388608 | tf_op jit(solution)/shard_map/all_to_all | solution.py:444
  260.9 8.2 %fusion.2 = f32[1024,768]{1,0:T(8,128)} fusion(bf16[128,8,2048]{2,1,0:T(8,128)(2,1)} %all-to-all-done.5, bf16[1,2048,768]{2,1,0:T(8,128)(2,1)} %param.21), kind=kOutput, calls=%fused_computation.3 | convolution fusion | flops 3221225472 | bytes 10485760 | tf_op jit(solution)/shard_map/dot_general | solution.py:380
  269.1 12.2 %convert_bitcast_fusion = bf16[128,8,2048]{2,1,0:T(8,128)(2,1)} fusion(bf16[1,768,2048]{2,1,0:T(8,128)(2,1)S(1)} %copy-done, f32[1024,768]{1,0:T(8,128)} %fusion.2, bf16[1,2048,768]{2,1,0:T(8,128)(2,1)} %param.22, bf16[128,8,2048]{2,1,0:T(8,128)(2,1)} %all-to-all-done.5), kind=kOutput, calls=%fused_computation.9 | convolution fusion | flops 6449266688 | bytes 17825792 | tf_op jit(solution)/shard_map/dot_general | solution.py:383
  281.3 34.7 %all-to-all-done.3 = bf16[128,8,2048]{2,1,0:T(8,128)(2,1)} async-done(((bf16[128,8,2048]{2,1,0:T(8,128)(2,1)}), bf16[128,8,2048]{2,1,0:T(8,128)(2,1)}, u32[]{:S(2)}, u32[]{:S(2)}) %all-to-all-start.3) | async-done | bytes 4194336 | tf_op jit(solution)/shard_map/all_to_all | solution.py:444
  316.1 5.1 %all-to-all-start.6 = ((bf16[128,8,2048]{2,1,0:T(8,128)(2,1)}), bf16[128,8,2048]{2,1,0:T(8,128)(2,1)}, u32[]{:S(2)}, u32[]{:S(2)}) async-start(bf16[128,8,2048]{2,1,0:T(8,128)(2,1)} %convert_bitcast_fusion), calls=%async_computation.6 | async-start | bytes 8388608 | tf_op jit(solution)/shard_map/all_to_all | solution.py:444
  321.1 8.2 %fusion.6 = f32[1024,768]{1,0:T(8,128)} fusion(bf16[128,8,2048]{2,1,0:T(8,128)(2,1)} %all-to-all-done.3, bf16[1,2048,768]{2,1,0:T(8,128)(2,1)} %param.21), kind=kOutput, calls=%fused_computation.7 | convolution fusion | flops 3221225472 | bytes 10485760 | tf_op jit(solution)/shard_map/dot_general | solution.py:380
  329.3 12.3 %convert_bitcast_fusion.1 = bf16[128,8,2048]{2,1,0:T(8,128)(2,1)} fusion(bf16[1,768,2048]{2,1,0:T(8,128)(2,1)S(1)} %copy-done, f32[1024,768]{1,0:T(8,128)} %fusion.6, bf16[1,2048,768]{2,1,0:T(8,128)(2,1)} %param.22, bf16[128,8,2048]{2,1,0:T(8,128)(2,1)} %all-to-all-done.3), kind=kOutput, calls=%fused_computation.10 | convolution fusion | flops 6449266688 | bytes 17825792 | tf_op jit(solution)/shard_map/dot_general | solution.py:383
  341.6 34.7 %all-to-all-done.6 = bf16[128,8,2048]{2,1,0:T(8,128)(2,1)} async-done(((bf16[128,8,2048]{2,1,0:T(8,128)(2,1)}), bf16[128,8,2048]{2,1,0:T(8,128)(2,1)}, u32[]{:S(2)}, u32[]{:S(2)}) %all-to-all-start.6) | async-done | bytes 4194336 | tf_op jit(solution)/shard_map/all_to_all | solution.py:444
  376.3 5.1 %all-to-all-start.4 = ((bf16[128,8,2048]{2,1,0:T(8,128)(2,1)}), bf16[128,8,2048]{2,1,0:T(8,128)(2,1)}, u32[]{:S(2)}, u32[]{:S(2)}) async-start(bf16[128,8,2048]{2,1,0:T(8,128)(2,1)} %convert_bitcast_fusion.1), calls=%async_computation.4 | async-start | bytes 8388608 | tf_op jit(solution)/shard_map/all_to_all | solution.py:444
  382.2 5.4 %combine_first.1 = (f32[128,2048]{1,0:T(8,128)}, bf16[256,1024]{1,0:T(8,128)(2,1)}) custom-call(bf16[1024,2048]{1,0:T(8,128)(2,1)} %bitcast.25.returned_ref, s32[128,8]{1,0:T(8,128)} %copy-done.2, f32[128,8]{1,0:T(8,128)} %copy.55.route_ref, f32[128,2048]{1,0:T(8,128)} %get-tuple-element.24.base_ref), custom_call_target="tpu_custom_call" | custom-call | flops 1073741824 | bytes 6291456 | tf_op jit(solution)/shard_map/combine_first/pallas_call | solution.py:344
  387.5 49.1 %all-to-all-done.4 = bf16[128,8,2048]{2,1,0:T(8,128)(2,1)} async-done(((bf16[128,8,2048]{2,1,0:T(8,128)(2,1)}), bf16[128,8,2048]{2,1,0:T(8,128)(2,1)}, u32[]{:S(2)}, u32[]{:S(2)}) %all-to-all-start.4) | async-done | bytes 4194336 | tf_op jit(solution)/shard_map/all_to_all | solution.py:444
  436.6 4.6 %combine_last.1 = bf16[128,2048]{1,0:T(8,128)(2,1)} custom-call(bf16[1024,2048]{1,0:T(8,128)(2,1)} %bitcast.21.returned_ref, bf16[256,1024]{1,0:T(8,128)(2,1)} %get-tuple-element.25.shares_ref, f32[128,2048]{1,0:T(8,128)} %get-tuple-element.26.base_ref), custom_call_target="tpu_custom_call" | custom-call | flops 1073741824 | bytes 6291456 | tf_op jit(solution)/shard_map/combine_last/pallas_call | solution.py:366
  (57 shorter events, 13.9 us)
Async XLA Ops:
  6.5 262.6 %copy-start = (bf16[1,768,2048]{2,1,0:T(8,128)(2,1)S(1)}, bf16[1,768,2048]{2,1,0:T(8,128)(2,1)}, u32[]{:S(2)}) copy-start(bf16[1,768,2048]{2,1,0:T(8,128)(2,1)} %param.23) | copy-start | bytes 9437188
  6.5 126.5 %all-gather.5.cloned.1.call-start = ((), (), s32[]{:S(2)}) async-start(), calls=%async_computation.8 | async-start | bytes 5242880 | tf_op jit(solution)/shard_map/all_gather | solution.py:405
  7.3 141.9 %all-gather.3.cloned.1.call-start = ((), (), s32[]{:S(2)}) async-start(), calls=%async_computation.7 | async-start | bytes 4718592 | tf_op jit(solution)/shard_map/all_gather | solution.py:429
  7.3 1.6 dynamic-slice-start
  7.3 1.7 dynamic-slice-start.1
  9.7 71.9 %copy-start.4 = (s32[2048]{0:T(1024)S(1)}, s32[2048]{0:T(1024)}, u32[]{:S(2)}) copy-start(s32[2048]{0:T(1024)} %param.16) | copy-start | bytes 24580
  76.1 19.1 %collective-permute-start.1 = (bf16[8,1280,256]{2,1,0:T(8,128)(2,1)}, bf16[8,1280,256]{2,1,0:T(8,128)(2,1)}, u32[]{:S(2)}, u32[]{:S(2)}) collective-permute-start(bf16[8,1280,256]{2,1,0:T(8,128)(2,1)} %all_to_all.35.refs_1_.refs_2_), channel_id=1, source_target_pairs={{0,1},{1,0},{2,3},{3,2},{4,5},{5,4},{6,7},{7,6},{8,9},{9,8},{10,11... | collective-permute-start | bytes 15728648 | tf_op jit(solution)/shard_map/ppermute | solution.py:161
  78.0 16.5 %collective-permute-start = (bf16[128,2048]{1,0:T(8,128)(2,1)}, bf16[128,2048]{1,0:T(8,128)(2,1)}, u32[]{:S(2)}, u32[]{:S(2)}) collective-permute-start(bf16[128,2048]{1,0:T(8,128)(2,1)} %constant_dynamic-slice_fusion), channel_id=1, source_target_pairs={{0,18},{18,0},{2,16},{16,2},{1,19},{19,1},{3,17},{17,3},{4,22},{22... | collective-permute-start | bytes 1572872 | tf_op jit(solution)/shard_map/ppermute | solution.py:426
  95.2 54.0 %copy-start.3 = (s32[128,8]{0,1:T(8,128)S(1)}, s32[128,8]{0,1:T(8,128)}, u32[]{:S(2)}) copy-start(s32[128,8]{0,1:T(8,128)} %param.19) | copy-start | bytes 12292
  126.7 22.5 %all-to-all-start.1 = ((bf16[8,256,256]{2,1,0:T(8,128)(2,1)}), bf16[8,256,256]{2,1,0:T(8,128)(2,1)}, u32[]{:S(2)}, u32[]{:S(2)}) async-start(bf16[8,256,256]{2,1,0:T(8,128)(2,1)} %attend.1), calls=%async_computation.1 | async-start | bytes 2097152 | tf_op jit(solution)/shard_map/all_to_all | solution.py:432
  133.0 33.9 %collective-permute-start.2 = (bf16[1024,2048]{1,0:T(8,128)(2,1)}, bf16[1024,2048]{1,0:T(8,128)(2,1)}, u32[]{:S(2)}, u32[]{:S(2)}) collective-permute-start(bf16[1024,2048]{1,0:T(8,128)(2,1)} %all-gather.5.cloned.1.call-done.w0), channel_id=1, source_target_pairs={{0,1},{1,0},{2,3},{3,2},{4,5},{5,4},{6,7},{7,6},{8,9},{9,8},{10,11... | collective-permute-start | bytes 12582920 | tf_op jit(solution)/shard_map/ppermute | solution.py:428
  149.2 32.0 %collective-permute-start.3 = (bf16[1024,2048]{1,0:T(8,128)(2,1)}, bf16[1024,2048]{1,0:T(8,128)(2,1)}, u32[]{:S(2)}, u32[]{:S(2)}) collective-permute-start(bf16[1024,2048]{1,0:T(8,128)(2,1)} %all-gather.3.cloned.1.call-done.w2), channel_id=1, source_target_pairs={{0,1},{1,0},{2,3},{3,2},{4,5},{5,4},{6,7},{7,6},{8,9},{9,8},{10,11... | collective-permute-start | bytes 12582920 | tf_op jit(solution)/shard_map/ppermute | solution.py:434
  149.8 0.8 copy-start.1
  152.1 29.0 %all-to-all-start.2 = ((bf16[16,128,256]{2,1,0:T(8,128)(2,1)}), bf16[16,128,256]{2,1,0:T(8,128)(2,1)}, u32[]{:S(2)}, u32[]{:S(2)}) async-start(bf16[16,128,256]{2,1,0:T(8,128)(2,1)} %bitcast.9), calls=%async_computation.2 | async-start | bytes 2097152 | tf_op jit(solution)/shard_map/all_to_all | solution.py:435
  165.7 27.6 %copy-start.2 = (s32[128,8]{1,0:T(8,128)}, s32[128,8]{1,0:T(8,128)S(1)}, u32[]{:S(2)}) copy-start(s32[128,8]{1,0:T(8,128)S(1)} %fusion.34.slots_ref) | copy-start | bytes 12292
  193.2 62.6 %all-to-all-start.5 = ((bf16[128,8,2048]{2,1,0:T(8,128)(2,1)}), bf16[128,8,2048]{2,1,0:T(8,128)(2,1)}, u32[]{:S(2)}, u32[]{:S(2)}) async-start(bf16[128,8,2048]{2,1,0:T(8,128)(2,1)} %bitcast.72), calls=%async_computation.5 | async-start | bytes 8388608 | tf_op jit(solution)/shard_map/all_to_all | solution.py:444
  255.8 60.3 %all-to-all-start.3 = ((bf16[128,8,2048]{2,1,0:T(8,128)(2,1)}), bf16[128,8,2048]{2,1,0:T(8,128)(2,1)}, u32[]{:S(2)}, u32[]{:S(2)}) async-start(bf16[128,8,2048]{2,1,0:T(8,128)(2,1)} %bitcast.70), calls=%async_computation.3 | async-start | bytes 8388608 | tf_op jit(solution)/shard_map/all_to_all | solution.py:444
  316.1 60.3 %all-to-all-start.6 = ((bf16[128,8,2048]{2,1,0:T(8,128)(2,1)}), bf16[128,8,2048]{2,1,0:T(8,128)(2,1)}, u32[]{:S(2)}, u32[]{:S(2)}) async-start(bf16[128,8,2048]{2,1,0:T(8,128)(2,1)} %convert_bitcast_fusion), calls=%async_computation.6 | async-start | bytes 8388608 | tf_op jit(solution)/shard_map/all_to_all | solution.py:444
  341.6 39.8 %copy-start.5 = (f32[128,8]{0,1:T(8,128)S(1)}, f32[128,8]{0,1:T(8,128)}, u32[]{:S(2)}) copy-start(f32[128,8]{0,1:T(8,128)} %param.20) | copy-start | bytes 12292
  376.3 60.3 %all-to-all-start.4 = ((bf16[128,8,2048]{2,1,0:T(8,128)(2,1)}), bf16[128,8,2048]{2,1,0:T(8,128)(2,1)}, u32[]{:S(2)}, u32[]{:S(2)}) async-start(bf16[128,8,2048]{2,1,0:T(8,128)(2,1)} %convert_bitcast_fusion.1), calls=%async_computation.4 | async-start | bytes 8388608 | tf_op jit(solution)/shard_map/all_to_all | solution.py:444
Sparse Core Ops, SparseCore 0:
  9.0 49.9 all-gather.4
  94.6 52.7 all-gather.2

commit v8 on v7

--- a/solution.py
+++ b/solution.py
@@ -419,9 +419,10 @@
         segment_ids[None, :] < jnp.arange(SEGS, dtype=jnp.int32)[:, None], axis=1, dtype=jnp.int32
     )
     starts = lax.psum(counts, CTX)
-    mine, other = gather_keys(queries, key_rows, value_rows, yh * 2 + yl, c)
     rows = out_weight.shape[0] // 2
     sent = lax.dynamic_slice_in_dim(out_weight, (1 - zl) * rows, rows, 0)
+    queries, sent = lax.optimization_barrier((queries, sent))
+    mine, other = gather_keys(queries, key_rows, value_rows, yh * 2 + yl, c)
     sent, mine = lax.optimization_barrier((sent, mine))
     far = lax.ppermute(sent, ("zl", "zh"), Z_FLIP)
     far, starts = lax.optimization_barrier((far, starts))

time: 449 us -> 449 us (level)
  transfers between devices with their start and end apart: 12 -> 12, of which waited for: 7 -> 7; matrix products, arithmetic and copies ran while one was open for 11% -> 11% of each run, Pallas kernels for 9% -> 10%
where the time goes in v8:
time: 449 us; the launch traced here: 448 us
  waiting for transfers between devices  204 us (45%)
  blocking collectives  76.5 us (17%)
  Pallas kernels  59.6 us (13%)
  starting transfers between devices  43.2 us (10%)
  matrix products  41 us (9%)
  between operations  13.7 us (3%)
  local copies, waits for them, and re-layouts  6.59 us (1%)
    all_to_all x4, waiting for transfers between devices, exchange(): lax.all_to_all(rows.reshape(128, half, width), ALL, split_axis=0, concat_...  170 us
    all_to_all x1, blocking collectives, gather_keys(): mine = lax.all_to_all(sent, CTX, split_axis=0, concat_axis=0, tiled=True)  66.4 us
    pallas_call x1, Pallas kernels, attend(): pl.pallas_call(lambda *refs: attend_kernel(block, *refs), out_shape=jax.S...  33.6 us
    dot_general x2, matrix products, expert_rows(): jnp.dot(hidden, down_weight[0], preferred_element_type=jnp.float32)  24.6 us
    all_to_all x4, starting transfers between devices, exchange(): lax.all_to_all(rows.reshape(128, half, width), ALL, split_axis=0, concat_...  22.6 us
    all_to_all x1, waiting for transfers between devices, shards(): lax.all_to_all(attended, CTX, split_axis=0, concat_axis=0, tiled=True)  16.6 us
    dot_general x2, matrix products, expert_rows(): jnp.dot(flat_rows, gate_weight[0], preferred_element_type=jnp.float32)  16.4 us
    all_to_all x1, waiting for transfers between devices, shards(): lax.all_to_all(attended.reshape(16, TILE, columns), OWNER, split_axis=0,...  14.2 us
  transfers between devices with their start and end apart: 12, of which 7 were waited for; matrix products, arithmetic and copies ran while one was open for 11% of the time, Pallas kernels for 10%

profile of v8, /device:TPU:8, one launch (start us, length us, event | category | flops | bytes accessed | tf_op | source)
XLA Modules:
  0.0 447.9 jit_solution(4463167254399014532)
XLA Ops:
  11.4 66.4 %all_to_all.35.refs_1_.refs_2_ = bf16[8,1280,256]{2,1,0:T(8,128)(2,1)} all-to-all(bf16[8,1280,256]{2,1,0:T(8,128)(2,1)S(1)} %pad_maximum_fusion), channel_id=1, replica_groups=mesh['x'=4,'zl'=2,'yh'=2,'yl'=2,'zh'=2,'c'=2] {'x','zl'}, dimensions={0} | all-to-all | bytes 10485760 | tf_op jit(solution)/shard_map/all_to_all | solution.py:160
  77.8 3.6 collective-permute-start
  81.6 10.1 %psum.7 = s32[32]{0:T(128)S(1)} all-reduce(s32[32]{0:T(128)S(1)} %convert_reduce_fusion), channel_id=1, replica_groups=mesh['x'=4,'zl'=2,'yh'=2,'yl'=2,'zh'=2,'c'=2] {'x','zl'}, use_global_device_ids=true, to_apply=%region_1.2 | all-reduce | flops 32 | bytes 256 | tf_op jit(solution)/shard_map/psum | solution.py:421
  95.0 33.6 %attend.1 = bf16[8,256,256]{2,1,0:T(8,128)(2,1)} custom-call(s32[34]{0:T(128)} %pad_add_fusion.1.refs_0_, bf16[8,1280,256]{2,1,0:T(8,128)(2,1)} %all_to_all.35.refs_1_.refs_2_, bf16[8,1280,256]{2,1,0:T(8,128)(2,1)} %all_to_all.35.refs_1_.refs_2_, bf16[8,1280,256]{2,1,0:T(8,128)(2,1)} %collective-permute-done.1.refs_3_), custom_call_target="tpu_custom_call" | custom-call | flops 21474836480 | bytes 12582912 | tf_op jit(solution)/shard_map/attend/pallas_call | solution.py:169
  128.6 4.3 all-to-all-start.1
  133.0 16.6 %all-to-all-done.1 = bf16[8,256,256]{2,1,0:T(8,128)(2,1)} async-done(((bf16[8,256,256]{2,1,0:T(8,128)(2,1)}), bf16[8,256,256]{2,1,0:T(8,128)(2,1)}, u32[]{:S(2)}, u32[]{:S(2)}) %all-to-all-start.1) | async-done | bytes 1048608 | tf_op jit(solution)/shard_map/all_to_all | solution.py:433
  152.6 12.6 %all-to-all-start.2 = ((bf16[16,128,256]{2,1,0:T(8,128)(2,1)}), bf16[16,128,256]{2,1,0:T(8,128)(2,1)}, u32[]{:S(2)}, u32[]{:S(2)}) async-start(bf16[16,128,256]{2,1,0:T(8,128)(2,1)} %bitcast.9), calls=%async_computation.2 | async-start | bytes 2097152 | tf_op jit(solution)/shard_map/all_to_all | solution.py:436
  166.8 14.2 %all-to-all-done.2.attended_ref = bf16[16,128,256]{2,1,0:T(8,128)(2,1)} async-done(((bf16[16,128,256]{2,1,0:T(8,128)(2,1)}), bf16[16,128,256]{2,1,0:T(8,128)(2,1)}, u32[]{:S(2)}, u32[]{:S(2)}) %all-to-all-start.2) | async-done | bytes 1048608 | tf_op jit(solution)/shard_map/all_to_all | solution.py:436
  181.0 12.0 %mix.1 = (f32[128,2048]{1,0:T(8,128)}, bf16[128,2048]{1,0:T(8,128)(2,1)}, bf16[1024,2048]{1,0:T(8,128)(2,1)}) custom-call(s32[4]{0:T(128)} %pad_add_fusion.scalars, bf16[16,128,256]{2,1,0:T(8,128)(2,1)} %all-to-all-done.2.attended_ref, bf16[1024,2048]{1,0:T(8,128)(2,1)} %all-gather.5.cloned.1.call-done.w0, bf16[1024,2048]{1,0:T(8,128)(2,1)} %collective-permute-done.2.w1, ...), custom_call_target="tpu_custom_call" | custom-call | flops 3221225472 | bytes 25165824 | tf_op jit(solution)/shard_map/mix/pallas_call | solution.py:252
  193.1 7.4 %all-to-all-start.5 = ((bf16[128,8,2048]{2,1,0:T(8,128)(2,1)}), bf16[128,8,2048]{2,1,0:T(8,128)(2,1)}, u32[]{:S(2)}, u32[]{:S(2)}) async-start(bf16[128,8,2048]{2,1,0:T(8,128)(2,1)} %bitcast.72), calls=%async_computation.5 | async-start | bytes 8388608 | tf_op jit(solution)/shard_map/all_to_all | solution.py:445
  200.4 4.0 place.1
  204.4 51.2 %all-to-all-done.5 = bf16[128,8,2048]{2,1,0:T(8,128)(2,1)} async-done(((bf16[128,8,2048]{2,1,0:T(8,128)(2,1)}), bf16[128,8,2048]{2,1,0:T(8,128)(2,1)}, u32[]{:S(2)}, u32[]{:S(2)}) %all-to-all-start.5) | async-done | bytes 4194336 | tf_op jit(solution)/shard_map/all_to_all | solution.py:445
  255.6 5.1 %all-to-all-start.3 = ((bf16[128,8,2048]{2,1,0:T(8,128)(2,1)}), bf16[128,8,2048]{2,1,0:T(8,128)(2,1)}, u32[]{:S(2)}, u32[]{:S(2)}) async-start(bf16[128,8,2048]{2,1,0:T(8,128)(2,1)} %bitcast.70), calls=%async_computation.3 | async-start | bytes 8388608 | tf_op jit(solution)/shard_map/all_to_all | solution.py:445
  260.7 8.2 %fusion.2 = f32[1024,768]{1,0:T(8,128)} fusion(bf16[128,8,2048]{2,1,0:T(8,128)(2,1)} %all-to-all-done.5, bf16[1,2048,768]{2,1,0:T(8,128)(2,1)} %param.21), kind=kOutput, calls=%fused_computation.3 | convolution fusion | flops 3221225472 | bytes 10485760 | tf_op jit(solution)/shard_map/dot_general | solution.py:380
  268.9 12.2 %convert_bitcast_fusion = bf16[128,8,2048]{2,1,0:T(8,128)(2,1)} fusion(bf16[1,768,2048]{2,1,0:T(8,128)(2,1)S(1)} %copy-done, f32[1024,768]{1,0:T(8,128)} %fusion.2, bf16[1,2048,768]{2,1,0:T(8,128)(2,1)} %param.22, bf16[128,8,2048]{2,1,0:T(8,128)(2,1)} %all-to-all-done.5), kind=kOutput, calls=%fused_computation.9 | convolution fusion | flops 6449266688 | bytes 17825792 | tf_op jit(solution)/shard_map/dot_general | solution.py:383
  281.2 34.7 %all-to-all-done.3 = bf16[128,8,2048]{2,1,0:T(8,128)(2,1)} async-done(((bf16[128,8,2048]{2,1,0:T(8,128)(2,1)}), bf16[128,8,2048]{2,1,0:T(8,128)(2,1)}, u32[]{:S(2)}, u32[]{:S(2)}) %all-to-all-start.3) | async-done | bytes 4194336 | tf_op jit(solution)/shard_map/all_to_all | solution.py:445
  315.9 5.1 %all-to-all-start.6 = ((bf16[128,8,2048]{2,1,0:T(8,128)(2,1)}), bf16[128,8,2048]{2,1,0:T(8,128)(2,1)}, u32[]{:S(2)}, u32[]{:S(2)}) async-start(bf16[128,8,2048]{2,1,0:T(8,128)(2,1)} %convert_bitcast_fusion), calls=%async_computation.6 | async-start | bytes 8388608 | tf_op jit(solution)/shard_map/all_to_all | solution.py:445
  321.0 8.2 %fusion.6 = f32[1024,768]{1,0:T(8,128)} fusion(bf16[128,8,2048]{2,1,0:T(8,128)(2,1)} %all-to-all-done.3, bf16[1,2048,768]{2,1,0:T(8,128)(2,1)} %param.21), kind=kOutput, calls=%fused_computation.7 | convolution fusion | flops 3221225472 | bytes 10485760 | tf_op jit(solution)/shard_map/dot_general | solution.py:380
  329.2 12.3 %convert_bitcast_fusion.1 = bf16[128,8,2048]{2,1,0:T(8,128)(2,1)} fusion(bf16[1,768,2048]{2,1,0:T(8,128)(2,1)S(1)} %copy-done, f32[1024,768]{1,0:T(8,128)} %fusion.6, bf16[1,2048,768]{2,1,0:T(8,128)(2,1)} %param.22, bf16[128,8,2048]{2,1,0:T(8,128)(2,1)} %all-to-all-done.3), kind=kOutput, calls=%fused_computation.10 | convolution fusion | flops 6449266688 | bytes 17825792 | tf_op jit(solution)/shard_map/dot_general | solution.py:383
  341.5 34.7 %all-to-all-done.6 = bf16[128,8,2048]{2,1,0:T(8,128)(2,1)} async-done(((bf16[128,8,2048]{2,1,0:T(8,128)(2,1)}), bf16[128,8,2048]{2,1,0:T(8,128)(2,1)}, u32[]{:S(2)}, u32[]{:S(2)}) %all-to-all-start.6) | async-done | bytes 4194336 | tf_op jit(solution)/shard_map/all_to_all | solution.py:445
  376.2 5.1 %all-to-all-start.4 = ((bf16[128,8,2048]{2,1,0:T(8,128)(2,1)}), bf16[128,8,2048]{2,1,0:T(8,128)(2,1)}, u32[]{:S(2)}, u32[]{:S(2)}) async-start(bf16[128,8,2048]{2,1,0:T(8,128)(2,1)} %convert_bitcast_fusion.1), calls=%async_computation.4 | async-start | bytes 8388608 | tf_op jit(solution)/shard_map/all_to_all | solution.py:445
  382.0 5.4 %combine_first.1 = (f32[128,2048]{1,0:T(8,128)}, bf16[256,1024]{1,0:T(8,128)(2,1)}) custom-call(bf16[1024,2048]{1,0:T(8,128)(2,1)} %bitcast.25.returned_ref, s32[128,8]{1,0:T(8,128)} %copy-done.2, f32[128,8]{1,0:T(8,128)} %copy.55.route_ref, f32[128,2048]{1,0:T(8,128)} %get-tuple-element.28.base_ref), custom_call_target="tpu_custom_call" | custom-call | flops 1073741824 | bytes 6291456 | tf_op jit(solution)/shard_map/combine_first/pallas_call | solution.py:344
  387.4 49.1 %all-to-all-done.4 = bf16[128,8,2048]{2,1,0:T(8,128)(2,1)} async-done(((bf16[128,8,2048]{2,1,0:T(8,128)(2,1)}), bf16[128,8,2048]{2,1,0:T(8,128)(2,1)}, u32[]{:S(2)}, u32[]{:S(2)}) %all-to-all-start.4) | async-done | bytes 4194336 | tf_op jit(solution)/shard_map/all_to_all | solution.py:445
  436.5 4.6 %combine_last.1 = bf16[128,2048]{1,0:T(8,128)(2,1)} custom-call(bf16[1024,2048]{1,0:T(8,128)(2,1)} %bitcast.21.returned_ref, bf16[256,1024]{1,0:T(8,128)(2,1)} %get-tuple-element.29.shares_ref, f32[128,2048]{1,0:T(8,128)} %get-tuple-element.30.base_ref), custom_call_target="tpu_custom_call" | custom-call | flops 1073741824 | bytes 6291456 | tf_op jit(solution)/shard_map/combine_last/pallas_call | solution.py:366
  (57 shorter events, 13.7 us)
Async XLA Ops:
  6.5 262.4 %copy-start = (bf16[1,768,2048]{2,1,0:T(8,128)(2,1)S(1)}, bf16[1,768,2048]{2,1,0:T(8,128)(2,1)}, u32[]{:S(2)}) copy-start(bf16[1,768,2048]{2,1,0:T(8,128)(2,1)} %param.23) | copy-start | bytes 9437188
  6.5 126.4 %all-gather.5.cloned.1.call-start = ((), (), s32[]{:S(2)}) async-start(), calls=%async_computation.8 | async-start | bytes 5242880 | tf_op jit(solution)/shard_map/all_gather | solution.py:405
  7.3 142.3 %all-gather.3.cloned.1.call-start = ((), (), s32[]{:S(2)}) async-start(), calls=%async_computation.7 | async-start | bytes 4718592 | tf_op jit(solution)/shard_map/all_gather | solution.py:430
  7.3 3.4 dynamic-slice-start
  7.3 3.4 dynamic-slice-start.1
  11.4 70.0 %copy-start.4 = (s32[2048]{0:T(1024)S(1)}, s32[2048]{0:T(1024)}, u32[]{:S(2)}) copy-start(s32[2048]{0:T(1024)} %param.16) | copy-start | bytes 24580
  77.8 17.1 %collective-permute-start.1 = (bf16[8,1280,256]{2,1,0:T(8,128)(2,1)}, bf16[8,1280,256]{2,1,0:T(8,128)(2,1)}, u32[]{:S(2)}, u32[]{:S(2)}) collective-permute-start(bf16[8,1280,256]{2,1,0:T(8,128)(2,1)} %all_to_all.35.refs_1_.refs_2_), channel_id=1, source_target_pairs={{0,1},{1,0},{2,3},{3,2},{4,5},{5,4},{6,7},{7,6},{8,9},{9,8},{10,11... | collective-permute-start | bytes 15728648 | tf_op jit(solution)/shard_map/ppermute | solution.py:161
  77.8 16.5 %collective-permute-start = (bf16[128,2048]{1,0:T(8,128)(2,1)}, bf16[128,2048]{1,0:T(8,128)(2,1)}, u32[]{:S(2)}, u32[]{:S(2)}) collective-permute-start(bf16[128,2048]{1,0:T(8,128)(2,1)} %constant_dynamic-slice_fusion), channel_id=1, source_target_pairs={{0,18},{18,0},{2,16},{16,2},{1,19},{19,1},{3,17},{17,3},{4,22},{22... | collective-permute-start | bytes 1572872 | tf_op jit(solution)/shard_map/ppermute | solution.py:427
  95.0 54.6 %copy-start.3 = (s32[128,8]{0,1:T(8,128)S(1)}, s32[128,8]{0,1:T(8,128)}, u32[]{:S(2)}) copy-start(s32[128,8]{0,1:T(8,128)} %param.19) | copy-start | bytes 12292
  128.6 21.0 %all-to-all-start.1 = ((bf16[8,256,256]{2,1,0:T(8,128)(2,1)}), bf16[8,256,256]{2,1,0:T(8,128)(2,1)}, u32[]{:S(2)}, u32[]{:S(2)}) async-start(bf16[8,256,256]{2,1,0:T(8,128)(2,1)} %attend.1), calls=%async_computation.1 | async-start | bytes 2097152 | tf_op jit(solution)/shard_map/all_to_all | solution.py:433
  132.9 33.9 %collective-permute-start.2 = (bf16[1024,2048]{1,0:T(8,128)(2,1)}, bf16[1024,2048]{1,0:T(8,128)(2,1)}, u32[]{:S(2)}, u32[]{:S(2)}) collective-permute-start(bf16[1024,2048]{1,0:T(8,128)(2,1)} %all-gather.5.cloned.1.call-done.w0), channel_id=1, source_target_pairs={{0,1},{1,0},{2,3},{3,2},{4,5},{5,4},{6,7},{7,6},{8,9},{9,8},{10,11... | collective-permute-start | bytes 12582920 | tf_op jit(solution)/shard_map/ppermute | solution.py:429
  149.6 31.4 %collective-permute-start.3 = (bf16[1024,2048]{1,0:T(8,128)(2,1)}, bf16[1024,2048]{1,0:T(8,128)(2,1)}, u32[]{:S(2)}, u32[]{:S(2)}) collective-permute-start(bf16[1024,2048]{1,0:T(8,128)(2,1)} %all-gather.3.cloned.1.call-done.w2), channel_id=1, source_target_pairs={{0,1},{1,0},{2,3},{3,2},{4,5},{5,4},{6,7},{7,6},{8,9},{9,8},{10,11... | collective-permute-start | bytes 12582920 | tf_op jit(solution)/shard_map/ppermute | solution.py:435
  150.2 0.8 copy-start.1
  152.6 28.4 %all-to-all-start.2 = ((bf16[16,128,256]{2,1,0:T(8,128)(2,1)}), bf16[16,128,256]{2,1,0:T(8,128)(2,1)}, u32[]{:S(2)}, u32[]{:S(2)}) async-start(bf16[16,128,256]{2,1,0:T(8,128)(2,1)} %bitcast.9), calls=%async_computation.2 | async-start | bytes 2097152 | tf_op jit(solution)/shard_map/all_to_all | solution.py:436
  165.5 27.6 %copy-start.2 = (s32[128,8]{1,0:T(8,128)}, s32[128,8]{1,0:T(8,128)S(1)}, u32[]{:S(2)}) copy-start(s32[128,8]{1,0:T(8,128)S(1)} %fusion.34.slots_ref) | copy-start | bytes 12292
  193.1 62.6 %all-to-all-start.5 = ((bf16[128,8,2048]{2,1,0:T(8,128)(2,1)}), bf16[128,8,2048]{2,1,0:T(8,128)(2,1)}, u32[]{:S(2)}, u32[]{:S(2)}) async-start(bf16[128,8,2048]{2,1,0:T(8,128)(2,1)} %bitcast.72), calls=%async_computation.5 | async-start | bytes 8388608 | tf_op jit(solution)/shard_map/all_to_all | solution.py:445
  255.6 60.3 %all-to-all-start.3 = ((bf16[128,8,2048]{2,1,0:T(8,128)(2,1)}), bf16[128,8,2048]{2,1,0:T(8,128)(2,1)}, u32[]{:S(2)}, u32[]{:S(2)}) async-start(bf16[128,8,2048]{2,1,0:T(8,128)(2,1)} %bitcast.70), calls=%async_computation.3 | async-start | bytes 8388608 | tf_op jit(solution)/shard_map/all_to_all | solution.py:445
  315.9 60.3 %all-to-all-start.6 = ((bf16[128,8,2048]{2,1,0:T(8,128)(2,1)}), bf16[128,8,2048]{2,1,0:T(8,128)(2,1)}, u32[]{:S(2)}, u32[]{:S(2)}) async-start(bf16[128,8,2048]{2,1,0:T(8,128)(2,1)} %convert_bitcast_fusion), calls=%async_computation.6 | async-start | bytes 8388608 | tf_op jit(solution)/shard_map/all_to_all | solution.py:445
  341.5 39.8 %copy-start.5 = (f32[128,8]{0,1:T(8,128)S(1)}, f32[128,8]{0,1:T(8,128)}, u32[]{:S(2)}) copy-start(f32[128,8]{0,1:T(8,128)} %param.20) | copy-start | bytes 12292
  376.2 60.3 %all-to-all-start.4 = ((bf16[128,8,2048]{2,1,0:T(8,128)(2,1)}), bf16[128,8,2048]{2,1,0:T(8,128)(2,1)}, u32[]{:S(2)}, u32[]{:S(2)}) async-start(bf16[128,8,2048]{2,1,0:T(8,128)(2,1)} %convert_bitcast_fusion.1), calls=%async_computation.4 | async-start | bytes 8388608 | tf_op jit(solution)/shard_map/all_to_all | solution.py:445
Sparse Core Ops, SparseCore 0:
  9.0 49.9 all-gather.4
  94.5 52.3 all-gather.2
